TPU v7x, 256 devices: a whole 4x4x8 slice. The times are simulated.
256 devices in a mesh: gx: 8 (over x_lo, y), gy: 16 (over z, core), gz: 2 (over x_hi).
Axes of the slice: x: 4 (x_hi: 2, x_lo: 2; x = x_hi * 2 + x_lo), y: 4, z: 8, core: 2. Of those that a mesh axis runs over, the one named last changes fastest.
Arguments:
- velocity: float32 [3, 256, 256, 256], P(None, 'gx', 'gy', 'gz'), may hold values from -6 to 6
- adjoint_seed: float32 [3, 256, 256, 256], P(None, 'gx', 'gy', 'gz'), may hold values from -6 to 6
- susceptibility: float32 [256, 256, 256], P('gx', 'gy', 'gz'), may hold values from 0.5 to 4
- remanence: float32 [256, 256, 256], P('gx', 'gy', 'gz'), may hold values from 0.2 to 1.5
- region_bounds: int32 [2, 3], replicated, may hold values from 0 to 128, as said below
- step_id: int32 [1], replicated, may hold values from 0 to 999
Outputs:
- next_velocity: float32 [3, 256, 256, 256], P(None, 'gx', 'gy', 'gz')
- velocity_adjoint: float32 [3, 256, 256, 256], P(None, 'gx', 'gy', 'gz')
- design_gradient: float32 [256, 256, 256], P('gx', 'gy', 'gz')
Inputs may be any that keep to these rules, and one draw needn't show every extreme that they name: Along every dimension the design region is nonempty and lies in the lower half of the box: region_bounds[0, d] < region_bounds[1, d] <= half the cells along d.
All inputs are finite; a program needn't handle non-finite values.
Results may differ from a plain program's by a relative error of at most 0.000096.
Values sent between devices are 32-bit elements; how exact they have to be, the bound alone decides.
A program may use at most 128 MiB of HBM per device.

v0:
```python
import jax
import jax.numpy as jnp
from jax import lax
from jax.sharding import PartitionSpec as P

NX = 256
NY = 256
NZ = 256


time_step = 0.5
viscosity = 0.2
field_period = 24
full_turn = 6.283185307179586
highest = lax.Precision.HIGHEST


def cut_along(array, dim, peers):
    before, after = (array.shape[:dim], array.shape[dim + 1 :])
    return jnp.moveaxis(array.reshape(*before, peers, -1, *after), dim, 0)


def summed_on_arrival(array, axis, dim):
    peers = lax.axis_size(axis)
    blocks = lax.all_to_all(cut_along(array, dim, peers), axis, 0, 0, tiled=True)
    return jnp.sum(blocks, axis=0)


def sent_together(arrays, axis, split_dim, concat_dim, along):
    ends, at = ([], 0)
    for a in arrays[:-1]:
        at += a.shape[along]
        ends.append(at)
    both = jnp.concatenate(arrays, axis=along)
    return tuple(
        jnp.split(
            lax.all_to_all(both, axis, split_axis=split_dim, concat_axis=concat_dim, tiled=True),
            ends,
            axis=along,
        )
    )


def passed_along(array, axis, by):
    peers = lax.axis_size(axis)
    pairs = [(i, i + by) for i in range(peers) if 0 <= i + by < peers]
    return lax.ppermute(array, axis, pairs)


def padded_2(array, sides, width):
    edges = {}
    for axis, dim in sides:
        peers, length = (lax.axis_size(axis), array.shape[dim])
        up = [(i, (i + 1) % peers) for i in range(peers - 1)]
        last = lax.slice_in_dim(array, length - width, length, axis=dim)
        first = lax.slice_in_dim(array, 0, width, axis=dim)
        edges[dim] = (
            lax.ppermute(last, axis, up),
            lax.ppermute(first, axis, [(b, a) for a, b in up]),
        )
    done = []
    for _, dim in sides:
        low, high = edges[dim]
        around = [(width, width) if d in done else (0, 0) for d in range(array.ndim)]
        array = jnp.concatenate([jnp.pad(low, around), array, jnp.pad(high, around)], axis=dim)
        done.append(dim)
    return array


def padded_3(block, sides, width):
    for axis, dim in sides:
        count = lax.axis_size(axis)
        forward = [(i, i + 1) for i in range(count - 1)]
        backward = [(target, source) for source, target in forward]
        low = lax.ppermute(
            lax.slice_in_dim(block, block.shape[dim] - width, None, axis=dim), axis, forward
        )
        high = lax.ppermute(lax.slice_in_dim(block, 0, width, axis=dim), axis, backward)
        block = jnp.concatenate([low, block, high], axis=dim)
    return block


def phase_tables(row_index, col_index, length):
    phase_turns = row_index[:, None] * col_index[None, :] % length
    phase_angle = full_turn * phase_turns.astype(jnp.float32) / length
    return (jnp.cos(phase_angle), jnp.sin(phase_angle))


def folded_index(cell_index, length):
    return jnp.where(cell_index < length // 2, cell_index, cell_index - length)


def arrival_order(length):
    position = jnp.arange(length, dtype=jnp.int32)
    return position


def depth_sum(partial_term):
    return summed_on_arrival(partial_term, "gz", 3)


def column_turn(real_part, imag_part):
    return sent_together((real_part, imag_part), "gy", 1, 2, 0)


def row_turn(real_part, imag_part):
    return sent_together((real_part, imag_part), ("gx", "gy"), 2, 1, 0)


def rotate(real_part, imag_part, cosine, sine, form, direction):
    real_cos = jnp.einsum(form, real_part, cosine, precision=highest)
    real_sin = jnp.einsum(form, real_part, sine, precision=highest)
    imag_cos = jnp.einsum(form, imag_part, cosine, precision=highest)
    imag_sin = jnp.einsum(form, imag_part, sine, precision=highest)
    return (real_cos - direction * imag_sin, imag_cos + direction * real_sin)


def depth_section(real_part, imag_part, magnet_only):
    if magnet_only:
        half_depth = NZ // 2
        moved_real, moved_imag = passed_along(
            (real_part[..., half_depth:], imag_part[..., half_depth:]), "gz", 1
        )
        lower_device = lax.axis_index("gz") == 0
        return (
            jnp.where(lower_device, real_part[..., :half_depth], moved_real),
            jnp.where(lower_device, imag_part[..., :half_depth], moved_imag),
        )
    field_count = real_part.shape[0]
    summed = depth_sum(jnp.concatenate([real_part, imag_part], axis=0))
    return (summed[:field_count], summed[field_count:])


def forward_spectrum(fields, magnet_only):
    depth_cells = fields.shape[3]
    depth_index = lax.axis_index("gz") * depth_cells + jnp.arange(depth_cells, dtype=jnp.int32)
    cosine, sine = phase_tables(depth_index, jnp.arange(NZ, dtype=jnp.int32), NZ)
    real_part = jnp.einsum("fabc,ck->fabk", fields, cosine, precision=highest)
    imag_part = -jnp.einsum("fabc,ck->fabk", fields, sine, precision=highest)
    real_part, imag_part = depth_section(real_part, imag_part, magnet_only)
    real_part, imag_part = column_turn(real_part, imag_part)
    second_index = jnp.arange(NY, dtype=jnp.int32)
    cosine, sine = phase_tables(second_index, second_index, NY)
    real_part, imag_part = rotate(real_part, imag_part, cosine, sine, "fabk,bq->faqk", -1.0)
    real_part, imag_part = row_turn(real_part, imag_part)
    cosine, sine = phase_tables(arrival_order(NX), jnp.arange(NX, dtype=jnp.int32), NX)
    return rotate(real_part, imag_part, cosine, sine, "fapk,aq->fqpk", -1.0)


def inverse_field(real_part, imag_part, magnet_only):
    first_index = jnp.arange(NX, dtype=jnp.int32)
    cosine, sine = phase_tables(first_index, first_index, NX)
    real_part, imag_part = rotate(real_part, imag_part, cosine, sine, "fqpk,qa->fpak", 1.0)
    real_part, imag_part = row_turn(real_part, imag_part)
    cosine, sine = phase_tables(arrival_order(NY), jnp.arange(NY, dtype=jnp.int32), NY)
    real_part, imag_part = rotate(real_part, imag_part, cosine, sine, "fpak,pb->fbak", 1.0)
    real_part, imag_part = column_turn(real_part, imag_part)
    depth_cells = real_part.shape[3]
    depth_index = lax.axis_index("gz") * depth_cells + jnp.arange(depth_cells, dtype=jnp.int32)
    norm_scale = 1.0 / (NX * NY * NZ)
    if magnet_only:
        cosine, sine = phase_tables(depth_index, jnp.arange(NZ // 2, dtype=jnp.int32), NZ)
        own_term = jnp.einsum("fbak,kc->fabc", real_part, cosine, precision=highest) - jnp.einsum(
            "fbak,kc->fabc", imag_part, sine, precision=highest
        )
        own_term = own_term * norm_scale
        arrived = passed_along(own_term, "gz", -1)
        return own_term + arrived
    cosine, sine = phase_tables(depth_index, jnp.arange(NZ, dtype=jnp.int32), NZ)
    partial_term = jnp.einsum("fbak,kc->fabc", real_part, cosine, precision=highest) - jnp.einsum(
        "fbak,kc->fabc", imag_part, sine, precision=highest
    )
    return depth_sum(partial_term * norm_scale)


def spectral_kernels(run_second, depth_cells):
    fold_first = folded_index(jnp.arange(NX, dtype=jnp.int32), NX)[:, None, None]
    second_index = (
        lax.axis_index("gx") * lax.axis_size("gy") + lax.axis_index("gy")
    ) * run_second + jnp.arange(run_second, dtype=jnp.int32)
    fold_second = folded_index(second_index, NY)[None, :, None]
    third_index = lax.axis_index("gz") * depth_cells + jnp.arange(depth_cells, dtype=jnp.int32)
    fold_third = folded_index(third_index, NZ)[None, None, :]
    wave_first = full_turn * fold_first.astype(jnp.float32) / NX
    wave_second = full_turn * fold_second.astype(jnp.float32) / NY
    wave_third = full_turn * fold_third.astype(jnp.float32) / NZ
    anchor = (fold_first == 0) & (fold_second == 0) & (fold_third == 0)
    square = wave_first * wave_first + wave_second * wave_second + wave_third * wave_third
    safe_square = jnp.where(anchor, 1.0, square)
    return [
        jnp.where(anchor, 0.0, -(component_wave * wave_third) / safe_square)
        for component_wave in (wave_first, wave_second, wave_third)
    ]


def central_slope(padded, axis_number):
    if axis_number == 0:
        return (padded[..., 2:, 1:-1, 1:-1] - padded[..., :-2, 1:-1, 1:-1]) * 0.5
    if axis_number == 1:
        return (padded[..., 1:-1, 2:, 1:-1] - padded[..., 1:-1, :-2, 1:-1]) * 0.5
    return (padded[..., 1:-1, 1:-1, 2:] - padded[..., 1:-1, 1:-1, :-2]) * 0.5


def laplace(padded):
    beside = padded[..., 2:, 1:-1, 1:-1] + padded[..., :-2, 1:-1, 1:-1]
    beside = beside + padded[..., 1:-1, 2:, 1:-1] + padded[..., 1:-1, :-2, 1:-1]
    beside = beside + padded[..., 1:-1, 1:-1, 2:] + padded[..., 1:-1, 1:-1, :-2]
    return beside - 6.0 * padded[..., 1:-1, 1:-1, 1:-1]


def on_device(velocity, adjoint_seed, susceptibility, remanence, region_bounds, step_id):
    span_first, span_second, span_third = susceptibility.shape
    place_first = lax.axis_index("gx") * span_first + jnp.arange(span_first, dtype=jnp.int32)
    place_second = lax.axis_index("gy") * span_second + jnp.arange(span_second, dtype=jnp.int32)
    place_third = lax.axis_index("gz") * span_third + jnp.arange(span_third, dtype=jnp.int32)
    inside_first = (place_first >= region_bounds[0, 0]) & (place_first < region_bounds[1, 0])
    inside_second = (place_second >= region_bounds[0, 1]) & (place_second < region_bounds[1, 1])
    inside_third = (place_third >= region_bounds[0, 2]) & (place_third < region_bounds[1, 2])
    region_mask = (
        inside_first[:, None, None] & inside_second[None, :, None] & inside_third[None, None, :]
    ).astype(jnp.float32)
    stacked = jnp.concatenate([velocity, adjoint_seed, susceptibility[None]], axis=0)
    padded_all = padded_2(stacked, (("gx", 1), ("gy", 2), ("gz", 3)), 1)
    magnet_real, magnet_imag = forward_spectrum((remanence * region_mask)[None], True)
    kernels = spectral_kernels(magnet_real.shape[2], magnet_real.shape[3])
    demag_field = inverse_field(
        jnp.stack([kernel * magnet_real[0] for kernel in kernels]),
        jnp.stack([kernel * magnet_imag[0] for kernel in kernels]),
        False,
    )
    phase_angle = full_turn * (step_id[0] % field_period).astype(jnp.float32) / field_period
    applied = jnp.stack([jnp.cos(phase_angle), jnp.sin(phase_angle), jnp.zeros((), jnp.float32)])
    total_field = demag_field + applied[:, None, None, None]
    energy = 0.5 * jnp.sum(total_field * total_field, axis=0)
    padded_energy = padded_3(energy, (("gx", 0), ("gy", 1), ("gz", 2)), 1)
    padded_velocity = padded_all[0:3]
    padded_seed = padded_all[3:6]
    padded_suscept = padded_all[6]
    advect = jnp.stack(
        [
            velocity[0] * central_slope(padded_velocity[comp], 0)
            + velocity[1] * central_slope(padded_velocity[comp], 1)
            + velocity[2] * central_slope(padded_velocity[comp], 2)
            for comp in range(3)
        ]
    )
    pushed = jnp.stack(
        [susceptibility * central_slope(padded_energy, axis_number) for axis_number in range(3)]
    )
    next_velocity = velocity + time_step * (viscosity * laplace(padded_velocity) - advect + pushed)
    flux_terms = padded_suscept[None] * padded_seed
    source = (
        central_slope(flux_terms[0], 0)
        + central_slope(flux_terms[1], 1)
        + central_slope(flux_terms[2], 2)
    )
    source = -time_step * source
    field_adjoint = source[None] * total_field
    adjoint_real, adjoint_imag = forward_spectrum(field_adjoint, False)
    combined_real = (
        kernels[0] * adjoint_real[0] + kernels[1] * adjoint_real[1] + kernels[2] * adjoint_real[2]
    )
    combined_imag = (
        kernels[0] * adjoint_imag[0] + kernels[1] * adjoint_imag[1] + kernels[2] * adjoint_imag[2]
    )
    magnet_adjoint = inverse_field(combined_real[None], combined_imag[None], True)[0]
    design_gradient = region_mask * magnet_adjoint
    shear_terms = jnp.stack(
        [
            adjoint_seed[0] * central_slope(padded_velocity[0], comp)
            + adjoint_seed[1] * central_slope(padded_velocity[1], comp)
            + adjoint_seed[2] * central_slope(padded_velocity[2], comp)
            for comp in range(3)
        ]
    )
    carried = jnp.stack(
        [
            central_slope(padded_velocity[0] * padded_seed[comp], 0)
            + central_slope(padded_velocity[1] * padded_seed[comp], 1)
            + central_slope(padded_velocity[2] * padded_seed[comp], 2)
            for comp in range(3)
        ]
    )
    velocity_adjoint = adjoint_seed + time_step * (
        viscosity * laplace(padded_seed) - shear_terms + carried
    )
    return (next_velocity, velocity_adjoint, design_gradient)


def solution(mesh):
    return jax.shard_map(
        on_device,
        mesh=mesh,
        in_specs=(
            P(None, "gx", "gy", "gz"),
            P(None, "gx", "gy", "gz"),
            P("gx", "gy", "gz"),
            P("gx", "gy", "gz"),
            P(),
            P(),
        ),
        out_specs=(P(None, "gx", "gy", "gz"), P(None, "gx", "gy", "gz"), P("gx", "gy", "gz")),
        check_vma=False,
    )
```

profile of v0, /device:TPU:24, one launch (start us, length us, event | category | flops | bytes accessed | tf_op | source)
XLA Modules:
  0.0 508.0 jit_solution(1813712204972219225)
XLA Ops:
  8.4 4.9 collective-permute-start.7
  15.8 4.2 collective-permute-done.7
  20.0 4.5 collective-permute-done.6
  25.4 8.6 %all-to-all-start = ((f32[2,32,16,128]{3,2,0,1:T(8,128)}), f32[2,32,16,128]{3,2,0,1:T(8,128)S(1)}, u32[]{:S(2)}, u32[]{:S(2)}) async-start(f32[2,32,16,128]{3,2,0,1:T(8,128)} %copy.436), calls=%async_computation | async-start | bytes 1048576 | tf_op jit(solution)/shard_map/all_to_all | solution.py:37
  34.1 15.8 %all-to-all-done = f32[2,32,16,128]{3,2,0,1:T(8,128)S(1)} async-done(((f32[2,32,16,128]{3,2,0,1:T(8,128)}), f32[2,32,16,128]{3,2,0,1:T(8,128)S(1)}, u32[]{:S(2)}, u32[]{:S(2)}) %all-to-all-start) | async-done | bytes 524320 | tf_op jit(solution)/shard_map/all_to_all | solution.py:37
  57.7 8.6 %all-to-all-start.1 = ((f32[2,2,256,128]{3,1,0,2:T(2,128)}), f32[2,2,256,128]{3,1,0,2:T(2,128)S(1)}, u32[]{:S(2)}, u32[]{:S(2)}) async-start(f32[2,2,256,128]{3,1,0,2:T(2,128)} %copy.438), calls=%async_computation.1 | async-start | bytes 1048576 | tf_op jit(solution)/shard_map/all_to_all | solution.py:37
  66.7 16.7 %all-to-all-done.1 = f32[2,2,256,128]{3,1,0,2:T(2,128)S(1)} async-done(((f32[2,2,256,128]{3,1,0,2:T(2,128)}), f32[2,2,256,128]{3,1,0,2:T(2,128)S(1)}, u32[]{:S(2)}, u32[]{:S(2)}) %all-to-all-start.1) | async-done | bytes 524320 | tf_op jit(solution)/shard_map/all_to_all | solution.py:37
  98.9 45.5 %all_to_all.130 = f32[6,2,256,128]{3,1,0,2:T(2,128)S(1)} all-to-all(f32[6,2,256,128]{3,1,0,2:T(2,128)S(1)} %copy.440), channel_id=1, replica_groups=mesh['gx'=8,'gy'=16,'gz'=2] {'gx','gy'}, dimensions={2} | all-to-all | bytes 3145728 | tf_op jit(solution)/shard_map/all_to_all | solution.py:37
  155.2 5.3 %all-to-all-start.3 = ((f32[6,256,2,128]{3,2,0,1:T(2,128)}), f32[6,256,2,128]{3,2,0,1:T(2,128)}, u32[]{:S(2)}, u32[]{:S(2)}) async-start(f32[6,256,2,128]{3,2,0,1:T(2,128)} %copy.442), calls=%async_computation.3 | async-start | bytes 3145728 | tf_op jit(solution)/shard_map/all_to_all | solution.py:37
  164.7 4.4 collective-permute-start.1
  178.0 7.3 %collective-permute-start.5 = (f32[7,32,16,1]{1,2,3,0:T(8,128)}, f32[7,32,16,1]{1,2,3,0:T(8,128)}, u32[]{:S(2)}, u32[]{:S(2)}) collective-permute-start(f32[7,32,16,1]{1,2,3,0:T(8,128)} %copy.489), channel_id=1, source_target_pairs={{0,1},{2,3},{4,5},{6,7},{8,9},{10,11},{12,13},{14,15},{16,17},{18,... | collective-permute-start | bytes 43016 | tf_op jit(solution)/shard_map/ppermute | solution.py:58
  220.3 4.6 all-to-all-start.4
  228.2 18.8 %all-to-all-done.4 = f32[2,3,32,16,128]{4,2,3,1,0:T(8,128)} async-done(((f32[2,3,32,16,128]{4,2,3,1,0:T(8,128)}), f32[2,3,32,16,128]{4,2,3,1,0:T(8,128)}, u32[]{:S(2)}, u32[]{:S(2)}) %all-to-all-start.4) | async-done | bytes 1572896 | tf_op jit(solution)/shard_map/all_to_all | solution.py:25
  256.3 41.6 %all_to_all.131 = f32[2,6,32,16,128]{4,3,2,1,0:T(8,128)} all-to-all(f32[2,6,32,16,128]{4,3,2,1,0:T(8,128)S(1)} %bitcast_bitcast_fusion), channel_id=1, replica_groups=mesh['gx'=8,'gy'=16,'gz'=2] {'gz'}, dimensions={0} | all-to-all | bytes 6291456 | tf_op jit(solution)/shard_map/all_to_all | solution.py:25
  303.0 44.4 %all_to_all.132 = f32[6,32,16,128]{3,2,0,1:T(8,128)S(1)} all-to-all(f32[6,32,16,128]{3,2,0,1:T(8,128)S(1)} %copy.466), channel_id=1, replica_groups=mesh['gx'=8,'gy'=16,'gz'=2] {'gy'}, dimensions={1} | all-to-all | bytes 3145728 | tf_op jit(solution)/shard_map/all_to_all | solution.py:37
  357.9 9.1 %all-to-all-start.7 = ((f32[6,2,256,128]{3,1,0,2:T(2,128)}), f32[6,2,256,128]{3,1,0,2:T(2,128)}, u32[]{:S(2)}, u32[]{:S(2)}) async-start(f32[6,2,256,128]{3,1,0,2:T(2,128)} %copy.470), calls=%async_computation.7 | async-start | bytes 3145728 | tf_op jit(solution)/shard_map/all_to_all | solution.py:37
  377.7 26.3 %all-to-all-done.7 = f32[6,2,256,128]{3,1,0,2:T(2,128)} async-done(((f32[6,2,256,128]{3,1,0,2:T(2,128)}), f32[6,2,256,128]{3,1,0,2:T(2,128)}, u32[]{:S(2)}, u32[]{:S(2)}) %all-to-all-start.7) | async-done | bytes 1572896 | tf_op jit(solution)/shard_map/all_to_all | solution.py:37
  422.0 10.7 %all-to-all-start.8 = ((f32[2,2,256,128]{3,1,0,2:T(2,128)}), f32[2,2,256,128]{3,1,0,2:T(2,128)}, u32[]{:S(2)}, u32[]{:S(2)}) async-start(f32[2,2,256,128]{3,1,0,2:T(2,128)} %copy.472), calls=%async_computation.8 | async-start | bytes 1048576 | tf_op jit(solution)/shard_map/all_to_all | solution.py:37
  438.9 5.3 %collective-permute-start.9 = (f32[1,16,128]{2,1,0:T(8,128)S(1)}, f32[1,16,128]{2,1,0:T(8,128)S(1)}, u32[]{:S(2)}, u32[]{:S(2)}) collective-permute-start(f32[1,16,128]{2,1,0:T(8,128)S(1)} %bitcast.458), channel_id=1, source_target_pairs={{0,32},{32,64},{64,96},{96,128},{128,160},{160,192},{192,224},{1,3... | collective-permute-start | bytes 24584 | tf_op jit(solution)/shard_map/ppermute | solution.py:75
  444.2 4.6 fusion.31
  462.8 7.5 %all-to-all-start.9 = ((f32[2,256,2,128]{3,2,0,1:T(2,128)}), f32[2,256,2,128]{3,2,0,1:T(2,128)}, u32[]{:S(2)}, u32[]{:S(2)}) async-start(f32[2,256,2,128]{3,2,0,1:T(2,128)} %copy.474), calls=%async_computation.9 | async-start | bytes 1048576 | tf_op jit(solution)/shard_map/all_to_all | solution.py:37
  477.3 6.1 %collective-permute-start.13 = (f32[34,18,1]{2,0,1:T(8,128)S(1)}, f32[34,18,1]{2,0,1:T(8,128)S(1)}, u32[]{:S(2)}, u32[]{:S(2)}) collective-permute-start(f32[34,18,1]{2,0,1:T(8,128)S(1)} %get-tuple-element.82), channel_id=1, source_target_pairs={{0,1},{2,3},{4,5},{6,7},{8,9},{10,11},{12,13},{14,15},{16,17},{18,... | collective-permute-start | bytes 7352 | tf_op jit(solution)/shard_map/ppermute | solution.py:75
  484.3 6.0 %collective-permute-done.12 = f32[34,18,1]{2,0,1:T(8,128)S(1)} collective-permute-done((f32[34,18,1]{2,0,1:T(8,128)S(1)}, f32[34,18,1]{2,0,1:T(8,128)S(1)}, u32[]{:S(2)}, u32[]{:S(2)}) %collective-permute-start.12) | collective-permute-done | bytes 2480 | tf_op jit(solution)/shard_map/ppermute | solution.py:78
  496.8 5.3 %fusion.40 = f32[3,32,16,128]{3,1,2,0:T(8,128)S(1)} fusion(f32[7,34,18,1]{3,1,2,0:T(8,128)S(1)} %copy-done.2, f32[7,34,1,128]{3,1,2,0:T(8,128)S(1)} %pad.14, f32[7,34,16,128]{3,1,2,0:T(8,128)} %copy-done.8, f32[7,34,1,128]{3,1,2,0:T(8,128)} %copy-done.22, f32[7,34,18,1]{3,1,2,0:T(8,128)S(1)} %pad.16, f32[1,32,16,128]{3,1,2,0:T(8,128)} %get-tuple-element.68, ...), kind=kLoop, calls=%fused_computation.89 | loop fusion | flops 4718592 | bytes 6946272 | tf_op jit(solution)/shard_map/add | solution.py:250
  (251 shorter events, 188.6 us)
Async XLA Ops:
  6.1 82.6 %copy-start.33 = (pred[128]{0:T(512)(128)(4,1)}, pred[128]{0:T(512)(128)(4,1)S(1)}, u32[]{:S(2)}) copy-start(pred[128]{0:T(512)(128)(4,1)S(1)} %get-tuple-element.105) | copy-start | bytes 388
  8.4 11.6 %collective-permute-start.7 = (f32[1,32,16,128]{3,2,1,0:T(8,128)S(1)}, f32[1,32,16,128]{3,2,1,0:T(8,128)S(1)}, u32[]{:S(2)}, u32[]{:S(2)}) collective-permute-start(f32[1,32,16,128]{3,2,1,0:T(8,128)S(1)} %slice.587), channel_id=1, source_target_pairs={{0,1},{2,3},{4,5},{6,7},{8,9},{10,11},{12,13},{14,15},{16,17},{18,... | collective-permute-start | bytes 786440 | tf_op jit(solution)/shard_map/ppermute | solution.py:47
  14.5 10.0 %collective-permute-start.6 = (f32[1,32,16,128]{3,2,1,0:T(8,128)S(1)}, f32[1,32,16,128]{3,2,1,0:T(8,128)S(1)}, u32[]{:S(2)}, u32[]{:S(2)}) collective-permute-start(f32[1,32,16,128]{3,2,1,0:T(8,128)S(1)} %slice.585), channel_id=1, source_target_pairs={{0,1},{2,3},{4,5},{6,7},{8,9},{10,11},{12,13},{14,15},{16,17},{18,... | collective-permute-start | bytes 786440 | tf_op jit(solution)/shard_map/ppermute | solution.py:47
  25.4 24.5 %all-to-all-start = ((f32[2,32,16,128]{3,2,0,1:T(8,128)}), f32[2,32,16,128]{3,2,0,1:T(8,128)S(1)}, u32[]{:S(2)}, u32[]{:S(2)}) async-start(f32[2,32,16,128]{3,2,0,1:T(8,128)} %copy.436), calls=%async_computation | async-start | bytes 1048576 | tf_op jit(solution)/shard_map/all_to_all | solution.py:37
  34.0 54.6 %copy-start.36 = (f32[128]{0:T(128)}, f32[128]{0:T(128)S(1)}, u32[]{:S(2)}) copy-start(f32[128]{0:T(128)S(1)} %get-tuple-element.107) | copy-start | bytes 1540
  57.7 25.6 %all-to-all-start.1 = ((f32[2,2,256,128]{3,1,0,2:T(2,128)}), f32[2,2,256,128]{3,1,0,2:T(2,128)S(1)}, u32[]{:S(2)}, u32[]{:S(2)}) async-start(f32[2,2,256,128]{3,1,0,2:T(2,128)} %copy.438), calls=%async_computation.1 | async-start | bytes 1048576 | tf_op jit(solution)/shard_map/all_to_all | solution.py:37
  155.2 57.2 %all-to-all-start.3 = ((f32[6,256,2,128]{3,2,0,1:T(2,128)}), f32[6,256,2,128]{3,2,0,1:T(2,128)}, u32[]{:S(2)}, u32[]{:S(2)}) async-start(f32[6,256,2,128]{3,2,0,1:T(2,128)} %copy.442), calls=%async_computation.3 | async-start | bytes 3145728 | tf_op jit(solution)/shard_map/all_to_all | solution.py:37
  161.1 39.8 %collective-permute-start = (f32[7,1,16,128]{3,2,1,0:T(8,128)}, f32[7,1,16,128]{3,2,1,0:T(8,128)S(1)}, u32[]{:S(2)}, u32[]{:S(2)}) collective-permute-start(f32[7,1,16,128]{3,2,1,0:T(8,128)} %get-tuple-element.56), channel_id=1, source_target_pairs={{32,0},{64,32},{96,64},{128,96},{160,128},{192,160},{224,192},{33,... | collective-permute-start | bytes 172040 | tf_op jit(solution)/shard_map/ppermute | solution.py:59
  164.7 36.2 %collective-permute-start.1 = (f32[7,1,16,128]{3,2,1,0:T(8,128)S(1)}, f32[7,1,16,128]{3,2,1,0:T(8,128)S(1)}, u32[]{:S(2)}, u32[]{:S(2)}) collective-permute-start(f32[7,1,16,128]{3,2,1,0:T(8,128)S(1)} %get-tuple-element.55), channel_id=1, source_target_pairs={{0,32},{32,64},{64,96},{96,128},{128,160},{160,192},{192,224},{1,3... | collective-permute-start | bytes 172040 | tf_op jit(solution)/shard_map/ppermute | solution.py:58
  173.9 15.0 %collective-permute-start.4 = (f32[7,32,16,1]{1,2,3,0:T(8,128)S(1)}, f32[7,32,16,1]{1,2,3,0:T(8,128)S(1)}, u32[]{:S(2)}, u32[]{:S(2)}) collective-permute-start(f32[7,32,16,1]{1,2,3,0:T(8,128)S(1)} %copy.488), channel_id=1, source_target_pairs={{1,0},{3,2},{5,4},{7,6},{9,8},{11,10},{13,12},{15,14},{17,16},{19,... | collective-permute-start | bytes 43016 | tf_op jit(solution)/shard_map/ppermute | solution.py:59
  178.0 18.2 %collective-permute-start.5 = (f32[7,32,16,1]{1,2,3,0:T(8,128)}, f32[7,32,16,1]{1,2,3,0:T(8,128)}, u32[]{:S(2)}, u32[]{:S(2)}) collective-permute-start(f32[7,32,16,1]{1,2,3,0:T(8,128)} %copy.489), channel_id=1, source_target_pairs={{0,1},{2,3},{4,5},{6,7},{8,9},{10,11},{12,13},{14,15},{16,17},{18,... | collective-permute-start | bytes 43016 | tf_op jit(solution)/shard_map/ppermute | solution.py:58
  186.2 16.1 %collective-permute-start.2 = (f32[7,32,1,128]{3,1,2,0:T(8,128)}, f32[7,32,1,128]{3,1,2,0:T(8,128)}, u32[]{:S(2)}, u32[]{:S(2)}) collective-permute-start(f32[7,32,1,128]{3,1,2,0:T(8,128)} %bitcast.134), channel_id=1, source_target_pairs={{2,0},{4,2},{6,4},{8,6},{10,8},{12,10},{14,12},{16,14},{18,16},{20... | collective-permute-start | bytes 344072 | tf_op jit(solution)/shard_map/ppermute | solution.py:59
  188.8 14.5 %collective-permute-start.3 = (f32[7,32,1,128]{3,1,2,0:T(8,128)}, f32[7,32,1,128]{3,1,2,0:T(8,128)}, u32[]{:S(2)}, u32[]{:S(2)}) collective-permute-start(f32[7,32,1,128]{3,1,2,0:T(8,128)} %bitcast.135), channel_id=1, source_target_pairs={{0,2},{2,4},{4,6},{6,8},{8,10},{10,12},{12,14},{14,16},{16,18},{18... | collective-permute-start | bytes 344072 | tf_op jit(solution)/shard_map/ppermute | solution.py:58
  220.3 26.7 %all-to-all-start.4 = ((f32[2,3,32,16,128]{4,2,3,1,0:T(8,128)}), f32[2,3,32,16,128]{4,2,3,1,0:T(8,128)}, u32[]{:S(2)}, u32[]{:S(2)}) async-start(f32[2,3,32,16,128]{4,2,3,1,0:T(8,128)} %bitcast.422), calls=%async_computation.4 | async-start | bytes 3145728 | tf_op jit(solution)/shard_map/all_to_all | solution.py:25
  357.9 46.1 %all-to-all-start.7 = ((f32[6,2,256,128]{3,1,0,2:T(2,128)}), f32[6,2,256,128]{3,1,0,2:T(2,128)}, u32[]{:S(2)}, u32[]{:S(2)}) async-start(f32[6,2,256,128]{3,1,0,2:T(2,128)} %copy.470), calls=%async_computation.7 | async-start | bytes 3145728 | tf_op jit(solution)/shard_map/all_to_all | solution.py:37
  422.0 31.8 %all-to-all-start.8 = ((f32[2,2,256,128]{3,1,0,2:T(2,128)}), f32[2,2,256,128]{3,1,0,2:T(2,128)}, u32[]{:S(2)}, u32[]{:S(2)}) async-start(f32[2,2,256,128]{3,1,0,2:T(2,128)} %copy.472), calls=%async_computation.8 | async-start | bytes 1048576 | tf_op jit(solution)/shard_map/all_to_all | solution.py:37
  436.3 12.5 %collective-permute-start.8 = (f32[1,16,128]{2,1,0:T(8,128)S(1)}, f32[1,16,128]{2,1,0:T(8,128)S(1)}, u32[]{:S(2)}, u32[]{:S(2)}) collective-permute-start(f32[1,16,128]{2,1,0:T(8,128)S(1)} %bitcast.459), channel_id=1, source_target_pairs={{32,0},{64,32},{96,64},{128,96},{160,128},{192,160},{224,192},{33,... | collective-permute-start | bytes 24584 | tf_op jit(solution)/shard_map/ppermute | solution.py:78
  438.9 9.9 %collective-permute-start.9 = (f32[1,16,128]{2,1,0:T(8,128)S(1)}, f32[1,16,128]{2,1,0:T(8,128)S(1)}, u32[]{:S(2)}, u32[]{:S(2)}) collective-permute-start(f32[1,16,128]{2,1,0:T(8,128)S(1)} %bitcast.458), channel_id=1, source_target_pairs={{0,32},{32,64},{64,96},{96,128},{128,160},{160,192},{192,224},{1,3... | collective-permute-start | bytes 24584 | tf_op jit(solution)/shard_map/ppermute | solution.py:75
  449.4 26.3 %collective-permute-start.10 = (f32[34,1,128]{2,0,1:T(8,128)}, f32[34,1,128]{2,0,1:T(8,128)S(1)}, u32[]{:S(2)}, u32[]{:S(2)}) collective-permute-start(f32[34,1,128]{2,0,1:T(8,128)} %get-tuple-element.84), channel_id=1, source_target_pairs={{2,0},{4,2},{6,4},{8,6},{10,8},{12,10},{14,12},{16,14},{18,16},{20... | collective-permute-start | bytes 52232 | tf_op jit(solution)/shard_map/ppermute | solution.py:78
  450.7 25.1 %collective-permute-start.11 = (f32[34,1,128]{2,0,1:T(8,128)}, f32[34,1,128]{2,0,1:T(8,128)S(1)}, u32[]{:S(2)}, u32[]{:S(2)}) collective-permute-start(f32[34,1,128]{2,0,1:T(8,128)} %get-tuple-element.83), channel_id=1, source_target_pairs={{0,2},{2,4},{4,6},{6,8},{8,10},{10,12},{12,14},{14,16},{16,18},{18... | collective-permute-start | bytes 52232 | tf_op jit(solution)/shard_map/ppermute | solution.py:75
  462.8 29.8 %all-to-all-start.9 = ((f32[2,256,2,128]{3,2,0,1:T(2,128)}), f32[2,256,2,128]{3,2,0,1:T(2,128)}, u32[]{:S(2)}, u32[]{:S(2)}) async-start(f32[2,256,2,128]{3,2,0,1:T(2,128)} %copy.474), calls=%async_computation.9 | async-start | bytes 1048576 | tf_op jit(solution)/shard_map/all_to_all | solution.py:37
  476.0 14.4 %collective-permute-start.12 = (f32[34,18,1]{2,0,1:T(8,128)S(1)}, f32[34,18,1]{2,0,1:T(8,128)S(1)}, u32[]{:S(2)}, u32[]{:S(2)}) collective-permute-start(f32[34,18,1]{2,0,1:T(8,128)S(1)} %get-tuple-element.81), channel_id=1, source_target_pairs={{1,0},{3,2},{5,4},{7,6},{9,8},{11,10},{13,12},{15,14},{17,16},{19,... | collective-permute-start | bytes 7352 | tf_op jit(solution)/shard_map/ppermute | solution.py:78
  477.3 14.3 %collective-permute-start.13 = (f32[34,18,1]{2,0,1:T(8,128)S(1)}, f32[34,18,1]{2,0,1:T(8,128)S(1)}, u32[]{:S(2)}, u32[]{:S(2)}) collective-permute-start(f32[34,18,1]{2,0,1:T(8,128)S(1)} %get-tuple-element.82), channel_id=1, source_target_pairs={{0,1},{2,3},{4,5},{6,7},{8,9},{10,11},{12,13},{14,15},{16,17},{18,... | collective-permute-start | bytes 7352 | tf_op jit(solution)/shard_map/ppermute | solution.py:75
  495.5 11.1 %collective-permute-start.14 = (f32[1,32,16,128]{3,1,2,0:T(8,128)S(1)}, f32[1,32,16,128]{3,1,2,0:T(8,128)S(1)}, u32[]{:S(2)}, u32[]{:S(2)}) collective-permute-start(f32[1,32,16,128]{3,1,2,0:T(8,128)S(1)} %fusion.14), channel_id=1, source_target_pairs={{1,0},{3,2},{5,4},{7,6},{9,8},{11,10},{13,12},{15,14},{17,16},{19,... | collective-permute-start | bytes 786440 | tf_op jit(solution)/shard_map/ppermute | solution.py:47
  (40 other events, 258.3 us)
where the time goes:
time: 518 us; the launch traced here: 508 us
  blocking collectives  132 us (25%)
  starting transfers between devices  103 us (20%)
  waiting for transfers between devices  96.7 us (19%)
  matrix products  67.4 us (13%)
  local copies, waits for them, and re-layouts  54 us (10%)
  other arithmetic  52 us (10%)
    all_to_all x2, blocking collectives, sent_together(): lax.all_to_all(both, axis, split_axis=split_dim, concat_axis=concat_dim,...  89.9 us
    all_to_all x6, waiting for transfers between devices, sent_together(): lax.all_to_all(both, axis, split_axis=split_dim, concat_axis=concat_dim,...  58.8 us
    all_to_all x6, starting transfers between devices, sent_together(): lax.all_to_all(both, axis, split_axis=split_dim, concat_axis=concat_dim,...  49.8 us
    all_to_all x1, blocking collectives, summed_on_arrival(): lax.all_to_all(cut_along(array, dim, peers), axis, 0, 0, tiled=True)  41.6 us
    all_to_all x1, waiting for transfers between devices, summed_on_arrival(): lax.all_to_all(cut_along(array, dim, peers), axis, 0, 0, tiled=True)  18.8 us
    ppermute x3, starting transfers between devices, padded_2(): lax.ppermute(last, axis, up)  15.3 us
    ppermute x3, starting transfers between devices, padded_3(): lax.ppermute(lax.slice_in_dim(block, block.shape[dim] - width, None, axis...  14.4 us
    unnamed x91, local copies, waits for them, and re-layouts  14.2 us
  transfers between devices with their start and end apart: 22, of which 9 were waited for; matrix products, arithmetic and copies ran while one was open for 14% of the time, Pallas kernels for 0%

commit v1 on v0

v1 whole, which is shorter than its diff:
```python
import jax
import jax.numpy as jnp
import numpy as np
from jax import lax
from jax.experimental import pallas as pl
from jax.experimental.pallas import tpu as pltpu
from jax.sharding import PartitionSpec as P

time_step = 0.5
viscosity = 0.2
field_period = 24
full_turn = 6.283185307179586

bf16 = jnp.bfloat16
f32 = jnp.float32
MESH = pl.DeviceIdType.MESH


def pieces(matrix):
    matrix = np.asarray(matrix, np.float32)
    high = matrix.astype(jnp.bfloat16)
    low = (matrix - high.astype(np.float32)).astype(jnp.bfloat16)
    return np.concatenate([high, high, low], axis=-1)


def cut(value, axis):
    high = value.astype(bf16)
    low = (value - high.astype(f32)).astype(bf16)
    return jnp.concatenate([high, low, high], axis=axis)


def mul(matrix, value):
    return jnp.dot(matrix, cut(value, 0), preferred_element_type=f32)


def make_tables():
    turn = 2.0 * np.pi / 256
    eye8, eye16 = np.eye(8), np.eye(16)
    k3 = 1 + 8 * np.arange(16)[:, None] + np.arange(8)[None, :]
    z = np.arange(128)
    phase = turn * k3[:, :, None] * z
    forward_z = np.stack([np.cos(phase), -np.sin(phase)], 1).reshape(256, 128)
    weight = np.where(k3 == 128, 1.0, 2.0)[:, :, None] / 256.0**3
    inverse_z = []
    for part in range(2):
        phase = turn * k3[:, :, None] * (z + 128 * part)
        both = np.stack([np.cos(phase) * weight, -np.sin(phase) * weight], 1)
        inverse_z.append(both.reshape(256, 128).T)
    q, t, ka = np.arange(8), np.arange(2), np.arange(16)
    theta = turn * 16 * (2 * q[:, None, None] + t[None, :, None]) * ka
    c, s = np.cos(theta), np.sin(theta)
    turned = np.stack([np.stack([c, s]), np.stack([-s, c])])
    sign = np.stack([np.ones(8), (-1.0) ** (1 + np.arange(8))])
    forward_x = np.einsum("abqtk,gj,ji->takiqgbj", turned, sign, eye8)
    forward_x = forward_x.reshape(2, 256, 256)
    lower = np.einsum("abqtk,ji->akitqbj", turned[:, :, :4], eye8).reshape(256, 128)
    back = np.stack([np.stack([c, -s]), np.stack([s, c])])
    inverse_x = np.einsum("abqtk,ij->tqaibkj", back, eye8).reshape(256, 256)
    lower_back = np.einsum("abqtk,ij->tqaibkj", back[:, :, :4], eye8).reshape(128, 256)
    b = np.arange(16)
    phi = turn * ka[:, None] * b
    twiddle = np.stack([np.cos(phi), np.sin(phi)])[:, :, None, :, None]
    twiddle = np.broadcast_to(twiddle, (2, 16, 8, 16, 16)).reshape(2, 128, 256)
    angle = turn * 16 * b[:, None] * b
    kron = [np.kron(np.cos(angle), eye16), np.kron(np.sin(angle), eye16)]
    k = np.arange(256)
    angle = turn * (k[:, None] * k % 256)
    second = np.stack([np.cos(angle), np.sin(angle)])
    return dict(
        forward_z=pieces(forward_z),
        inverse_z=pieces(np.stack(inverse_z)),
        forward_x=pieces(forward_x),
        lower_x=pieces(lower),
        inverse_x=pieces(inverse_x),
        lower_back=pieces(lower_back),
        twiddle=twiddle.astype(np.float32),
        kron=pieces(np.stack(kron)),
        second=pieces(second),
        second_lower=pieces(second[:, :, :128]),
    )


def rotated(pair, value, direction):
    value = cut(value, 0)
    first = jnp.dot(pair[0], value, preferred_element_type=f32)
    second = jnp.dot(pair[1], value, preferred_element_type=f32)
    real = first[:, :128] - direction * second[:, 128:]
    imag = first[:, 128:] + direction * second[:, :128]
    return real, imag


def depth_waves(block, forward_z):
    return lax.dot_general(
        forward_z, cut(block, 1), (((1,), (1,)), ((), ())), preferred_element_type=f32
    )


def first_forward(mixed, twiddle, kron):
    real, imag = mixed[:128], mixed[128:]
    c, s = twiddle[0], twiddle[1]
    turned = jnp.concatenate([real * c + imag * s, imag * c - real * s], axis=0)
    return rotated(kron, turned.T, -1.0)


def first_inverse(value, twiddle, kron, inverse_x):
    real, imag = rotated(kron, value, 1.0)
    turned = jnp.concatenate([real, imag], axis=1).T
    real, imag = turned[:128], turned[128:]
    c, s = twiddle[0], twiddle[1]
    turned = jnp.concatenate([real * c - imag * s, imag * c + real * s], axis=0)
    return mul(inverse_x, turned)


def signed_wave(index):
    folded = jnp.where(index < 128, index, index - 256)
    return jnp.where(index == 128, 0, folded).astype(f32) * (full_turn / 256)


def factor_of(index, third):
    half = full_turn / 2
    return jnp.where(third == 128, jnp.where(index == 128, half, 0.0), signed_wave(index))


def spectral_factors(place, gy):
    row = lax.broadcasted_iota(jnp.int32, (256, 128), 0)
    lane = lax.broadcasted_iota(jnp.int32, (256, 128), 1)
    third = 1 + 8 * place + lane % 8
    first = lane // 8 + 16 * gy
    third_wave = third.astype(f32) * (full_turn / 256)
    fold = lambda i: jnp.where(i < 128, i, i - 256).astype(f32) * (full_turn / 256)
    first_wave, second_wave = fold(first), fold(row)
    square = first_wave * first_wave + second_wave * second_wave + third_wave * third_wave
    return -third_wave / square, factor_of(row, third)


def mixing_factors(place):
    row = lax.broadcasted_iota(jnp.int32, (256, 128), 0)
    lane = lax.broadcasted_iota(jnp.int32, (256, 128), 1)
    third = 1 + 8 * place + lane % 8
    return factor_of(lane // 8 + 16 * (row // 16), third), third.astype(f32) * (full_turn / 256)


def twice(value):
    return jnp.concatenate([value, value], axis=1)


class Place:
    def __init__(self):
        self.gx, self.gy, self.gz = (lax.axis_index(a) for a in ("gx", "gy", "gz"))
        self.wave = self.gx * 2 + self.gz

    def by_wave(self, wave):
        return (wave // 2, self.gy, wave % 2)

    def by_second(self, second):
        return (self.gx, second, self.gz)

    def greet(self):
        barrier = pltpu.get_barrier_semaphore()

        def signal(step, carry):
            for target in (
                self.by_wave((self.wave + step) % 16),
                self.by_second((self.gy + step) % 16),
            ):
                pl.semaphore_signal(barrier, inc=1, device_id=target, device_id_type=MESH)
            return carry

        lax.fori_loop(1, 16, signal, 0)
        pl.semaphore_wait(barrier, 30)


class Exchange:
    def __init__(self, me, device, src, dst, send_sem, recv_sem, wanted=None):
        self.me, self.device, self.src, self.dst = me, device, src, dst
        self.send_sem, self.recv_sem, self.wanted = send_sem, recv_sem, wanted

    def each(self, act):
        def body(step, carry):
            peer = (self.me + step) % 16
            copy = pltpu.make_async_remote_copy(
                src_ref=self.src(peer),
                dst_ref=self.dst,
                send_sem=self.send_sem(peer),
                recv_sem=self.recv_sem,
                device_id=self.device(peer),
                device_id_type=MESH,
            )
            if self.wanted is None:
                act(copy)
            else:
                pl.when(self.wanted(peer))(lambda: act(copy))
            return carry

        lax.fori_loop(1, 16, body, 0)

    def start(self):
        self.each(lambda copy: copy.start())
        own = pltpu.make_async_copy(self.src(self.me), self.dst, self.recv_sem)
        if self.wanted is None:
            own.start()
        else:
            pl.when(self.wanted(self.me))(lambda: own.start())

    def finish(self):
        self.each(lambda copy: copy.wait_send())


def arrived(count, block, sem, skip=None):
    def wait(step, carry):
        pltpu.make_async_copy(block(step), block(step), sem(step)).wait()
        return carry

    lax.fori_loop(0, count, wait, 0)


def field_kernel(
    magnet_in, bounds, forward_z, lower_x, twiddle, kron, second_lower, second, inverse_x, inverse_z,
    field_out,
    z_out, z_in, k_out, k_in, y_out, y_in, x_out, x_in,
    z_sent, z_got, k_sent, k_got, y_sent, y_got, x_sent, x_got,
):
    at = Place()
    at.greet()
    has_magnet = (at.gx < 4) & (at.gy < 8) & (at.gz == 0)
    has_rows = at.gy < 8

    depths = Exchange(
        at.wave, at.by_wave, lambda p: z_out.at[p], z_in.at[at.gx % 4],
        lambda p: z_sent.at[p], z_got.at[at.gx % 4],
    )
    firsts = Exchange(
        at.gy, at.by_second, lambda p: k_out.at[p], k_in.at[at.gy % 8],
        lambda p: k_sent.at[p], k_got.at[at.gy % 8],
    )
    seconds = [
        Exchange(
            at.gy, at.by_second, lambda p, f=f: y_out.at[f, p], y_in.at[f, at.gy],
            lambda p, f=f: y_sent.at[f, p], y_got.at[f, at.gy],
        )
        for f in range(2)
    ]
    lasts = [
        Exchange(
            at.wave, at.by_wave, lambda p, f=f: x_out.at[f, p // 2], x_in.at[f, at.wave],
            lambda p, f=f: x_sent.at[f, p], x_got.at[f, at.wave],
        )
        for f in range(3)
    ]

    @pl.when(has_magnet)
    def _():
        magnet = magnet_in[...] * region(at, bounds)
        z_out[...] = depth_waves(magnet, forward_z[...]).reshape(16, 16, 512)
        depths.start()

    @pl.when(has_rows)
    def _():
        arrived(4, lambda i: z_in.at[i], lambda i: z_got.at[i])
        block = z_in[...].reshape(64, 512)
        block = jnp.concatenate([block[:, :256], block[:, 256:]], axis=0)
        real, imag = first_forward(mul(lower_x[...], block), twiddle[...], kron[...])
        k_out[...] = jnp.concatenate([real, imag], axis=1).reshape(16, 16, 256)
        firsts.start()

    potential, second_factor = spectral_factors(at.wave, at.gy)
    arrived(8, lambda i: k_in.at[i], lambda i: k_got.at[i])
    real, imag = rotated(second_lower[...], k_in[...].reshape(128, 256), -1.0)
    value = jnp.concatenate([real * potential, imag * potential], axis=1)
    for f in range(2):
        if f == 1:
            value = value * twice(second_factor)
        real, imag = rotated(second[...], value, 1.0)
        y_out[f] = jnp.concatenate([real, imag], axis=1).reshape(16, 16, 256)
        seconds[f].start()

    first_factor, third_factor = mixing_factors(at.wave)

    def send_first(f, value):
        value = first_inverse(value, twiddle[...], kron[...], inverse_x[...])
        x_out[f, :, :, :256] = value[:128].reshape(8, 16, 256)
        x_out[f, :, :, 256:] = value[128:].reshape(8, 16, 256)
        lasts[f].start()

    arrived(16, lambda i: y_in.at[0, i], lambda i: y_got.at[0, i])
    value = y_in[0].reshape(256, 256)
    send_first(0, value * twice(first_factor))
    send_first(2, value * twice(third_factor))
    arrived(16, lambda i: y_in.at[1, i], lambda i: y_got.at[1, i])
    send_first(1, y_in[1].reshape(256, 256))

    for f in (0, 2, 1):
        arrived(16, lambda i, f=f: x_in.at[f, i], lambda i, f=f: x_got.at[f, i])
        field_out[f] = mul(inverse_z[at.gz], x_in[f].reshape(256, 512)).T

    pl.when(has_magnet)(lambda: depths.finish())
    pl.when(has_rows)(lambda: firsts.finish())
    for each in seconds + lasts:
        each.finish()


def region(at, bounds):
    row = lax.broadcasted_iota(jnp.int32, (512, 128), 0)
    third = lax.broadcasted_iota(jnp.int32, (512, 128), 1) + at.gz * 128
    first, second = row // 16 + at.gx * 32, row % 16 + at.gy * 16
    inside = (first >= bounds[0, 0]) & (first < bounds[1, 0])
    inside = inside & (second >= bounds[0, 1]) & (second < bounds[1, 1])
    inside = inside & (third >= bounds[0, 2]) & (third < bounds[1, 2])
    return jnp.where(inside, 1.0, 0.0)


def gradient_kernel(
    adjoint_in, bounds, forward_z, forward_x, twiddle, kron, second, lower_back, inverse_z,
    gradient_out,
    z_out, z_in, k_out, k_in, y_out, y_in, x_out, x_in,
    z_sent, z_got, k_sent, k_got, y_sent, y_got, x_sent, x_got,
):
    at = Place()
    at.greet()
    keeps = (at.gx < 4) & (at.gy < 8) & (at.gz == 0)
    has_rows = at.gy < 8

    depths = [
        Exchange(
            at.wave, at.by_wave, lambda p, f=f: z_out.at[f, p], z_in.at[f, at.wave],
            lambda p, f=f: z_sent.at[f, p], z_got.at[f, at.wave],
        )
        for f in range(3)
    ]
    firsts = [
        Exchange(
            at.gy, at.by_second, lambda p, f=f: k_out.at[f, p], k_in.at[f, at.gy],
            lambda p, f=f: k_sent.at[f, p], k_got.at[f, at.gy],
        )
        for f in range(2)
    ]
    seconds = Exchange(
        at.gy, at.by_second, lambda p: y_out.at[p % 8], y_in.at[at.gy],
        lambda p: y_sent.at[p], y_got.at[at.gy], lambda p: p < 8,
    )
    lasts = Exchange(
        at.wave, at.by_wave, lambda p: x_out.at[p // 2 % 4], x_in.at[at.wave],
        lambda p: x_sent.at[p], x_got.at[at.wave], lambda p: (p < 8) & (p % 2 == 0),
    )

    for f in (1, 0, 2):
        z_out[f] = depth_waves(adjoint_in[f], forward_z[...]).reshape(16, 16, 512)
        depths[f].start()

    def first_of(f):
        arrived(16, lambda i: z_in.at[f, i], lambda i: z_got.at[f, i])
        block = z_in[f].reshape(256, 512)
        mixed = mul(forward_x[0], block[:, :256]) + mul(forward_x[1], block[:, 256:])
        real, imag = first_forward(mixed, twiddle[...], kron[...])
        return jnp.concatenate([real, imag], axis=1)

    first_factor, third_factor = mixing_factors(at.wave)
    k_out[1] = first_of(1).reshape(16, 16, 256)
    firsts[1].start()
    value = first_of(0) * twice(first_factor)
    value = value + first_of(2) * twice(third_factor)
    k_out[0] = value.reshape(16, 16, 256)
    firsts[0].start()

    potential, second_factor = spectral_factors(at.wave, at.gy)

    def second_of(f):
        arrived(16, lambda i: k_in.at[f, i], lambda i: k_got.at[f, i])
        real, imag = rotated(second[...], k_in[f].reshape(256, 256), -1.0)
        return jnp.concatenate([real, imag], axis=1)

    value = second_of(1) * twice(second_factor)
    value = (value + second_of(0)) * twice(potential)
    real, imag = rotated(second[:, :128], value, 1.0)
    y_out[...] = jnp.concatenate([real, imag], axis=1).reshape(8, 16, 256)
    seconds.start()

    @pl.when(has_rows)
    def _():
        arrived(16, lambda i: y_in.at[i], lambda i: y_got.at[i])
        value = y_in[...].reshape(256, 256)
        value = first_inverse(value, twiddle[...], kron[...], lower_back[...])
        x_out[:, :, :256] = value[:64].reshape(4, 16, 256)
        x_out[:, :, 256:] = value[64:].reshape(4, 16, 256)
        lasts.start()

    gradient_out[...] = jnp.zeros((512, 128), f32)

    @pl.when(keeps)
    def _():
        arrived(16, lambda i: x_in.at[i], lambda i: x_got.at[i])
        value = mul(inverse_z[0], x_in[...].reshape(256, 512)).T
        gradient_out[...] = value * region(at, bounds)

    for each in depths + firsts + [seconds]:
        each.finish()
    pl.when(has_rows)(lambda: lasts.finish())


VMEM = pl.BlockSpec(memory_space=pltpu.VMEM)
SMEM = pl.BlockSpec(memory_space=pltpu.SMEM)


def spectral_call(kernel, out, operands, shapes, sems, number):
    return pl.pallas_call(
        kernel,
        out_shape=jax.ShapeDtypeStruct(out, f32),
        in_specs=[SMEM if i == 1 else VMEM for i in range(len(operands))],
        out_specs=VMEM,
        scratch_shapes=[pltpu.VMEM(s, f32) for s in shapes]
        + [pltpu.SemaphoreType.DMA(s) for s in sems],
        compiler_params=pltpu.CompilerParams(
            collective_id=number, has_side_effects=True, vmem_limit_bytes=56 << 20
        ),
    )(*operands)


def demag_field_of(remanence, bounds, tables):
    names = ["forward_z", "lower_x", "twiddle", "kron", "second_lower", "second", "inverse_x", "inverse_z"]
    operands = [remanence.reshape(512, 128), bounds] + [tables[n] for n in names]
    shapes = [(16, 16, 512), (4, 16, 512), (16, 16, 256), (8, 16, 256)]
    shapes += [(2, 16, 16, 256), (2, 16, 16, 256), (3, 8, 16, 512), (3, 16, 16, 512)]
    sems = [(16,), (4,), (16,), (8,), (2, 16), (2, 16), (3, 16), (3, 16)]
    field = spectral_call(field_kernel, (3, 512, 128), operands, shapes, sems, 0)
    return field.reshape(3, 32, 16, 128)


def design_gradient_of(adjoint, bounds, tables):
    names = ["forward_z", "forward_x", "twiddle", "kron", "second", "lower_back", "inverse_z"]
    operands = [adjoint.reshape(3, 512, 128), bounds] + [tables[n] for n in names]
    shapes = [(3, 16, 16, 512), (3, 16, 16, 512), (2, 16, 16, 256), (2, 16, 16, 256)]
    shapes += [(8, 16, 256), (16, 16, 256), (4, 16, 512), (16, 16, 512)]
    sems = [(3, 16), (3, 16), (2, 16), (2, 16), (16,), (16,), (16,), (16,)]
    gradient = spectral_call(gradient_kernel, (512, 128), operands, shapes, sems, 1)
    return gradient.reshape(32, 16, 128)


def padded_2(array, sides, width):
    edges = {}
    for axis, dim in sides:
        peers, length = (lax.axis_size(axis), array.shape[dim])
        up = [(i, (i + 1) % peers) for i in range(peers - 1)]
        last = lax.slice_in_dim(array, length - width, length, axis=dim)
        first = lax.slice_in_dim(array, 0, width, axis=dim)
        edges[dim] = (
            lax.ppermute(last, axis, up),
            lax.ppermute(first, axis, [(b, a) for a, b in up]),
        )
    done = []
    for _, dim in sides:
        low, high = edges[dim]
        around = [(width, width) if d in done else (0, 0) for d in range(array.ndim)]
        array = jnp.concatenate([jnp.pad(low, around), array, jnp.pad(high, around)], axis=dim)
        done.append(dim)
    return array


def padded_3(block, sides, width):
    for axis, dim in sides:
        count = lax.axis_size(axis)
        forward = [(i, i + 1) for i in range(count - 1)]
        backward = [(target, source) for source, target in forward]
        low = lax.ppermute(
            lax.slice_in_dim(block, block.shape[dim] - width, None, axis=dim), axis, forward
        )
        high = lax.ppermute(lax.slice_in_dim(block, 0, width, axis=dim), axis, backward)
        block = jnp.concatenate([low, block, high], axis=dim)
    return block


def central_slope(padded, axis_number):
    if axis_number == 0:
        return (padded[..., 2:, 1:-1, 1:-1] - padded[..., :-2, 1:-1, 1:-1]) * 0.5
    if axis_number == 1:
        return (padded[..., 1:-1, 2:, 1:-1] - padded[..., 1:-1, :-2, 1:-1]) * 0.5
    return (padded[..., 1:-1, 1:-1, 2:] - padded[..., 1:-1, 1:-1, :-2]) * 0.5


def laplace(padded):
    beside = padded[..., 2:, 1:-1, 1:-1] + padded[..., :-2, 1:-1, 1:-1]
    beside = beside + padded[..., 1:-1, 2:, 1:-1] + padded[..., 1:-1, :-2, 1:-1]
    beside = beside + padded[..., 1:-1, 1:-1, 2:] + padded[..., 1:-1, 1:-1, :-2]
    return beside - 6.0 * padded[..., 1:-1, 1:-1, 1:-1]


def on_device(velocity, adjoint_seed, susceptibility, remanence, region_bounds, step_id):
    tables = make_tables()
    stacked = jnp.concatenate([velocity, adjoint_seed, susceptibility[None]], axis=0)
    padded_all = padded_2(stacked, (("gx", 1), ("gy", 2), ("gz", 3)), 1)
    demag_field = demag_field_of(remanence, region_bounds, tables)
    phase_angle = full_turn * (step_id[0] % field_period).astype(jnp.float32) / field_period
    applied = jnp.stack([jnp.cos(phase_angle), jnp.sin(phase_angle), jnp.zeros((), jnp.float32)])
    total_field = demag_field + applied[:, None, None, None]
    energy = 0.5 * jnp.sum(total_field * total_field, axis=0)
    padded_energy = padded_3(energy, (("gx", 0), ("gy", 1), ("gz", 2)), 1)
    padded_velocity = padded_all[0:3]
    padded_seed = padded_all[3:6]
    padded_suscept = padded_all[6]
    advect = jnp.stack(
        [
            velocity[0] * central_slope(padded_velocity[comp], 0)
            + velocity[1] * central_slope(padded_velocity[comp], 1)
            + velocity[2] * central_slope(padded_velocity[comp], 2)
            for comp in range(3)
        ]
    )
    pushed = jnp.stack(
        [susceptibility * central_slope(padded_energy, axis_number) for axis_number in range(3)]
    )
    next_velocity = velocity + time_step * (viscosity * laplace(padded_velocity) - advect + pushed)
    flux_terms = padded_suscept[None] * padded_seed
    source = (
        central_slope(flux_terms[0], 0)
        + central_slope(flux_terms[1], 1)
        + central_slope(flux_terms[2], 2)
    )
    source = -time_step * source
    field_adjoint = source[None] * total_field
    design_gradient = design_gradient_of(field_adjoint, region_bounds, tables)
    shear_terms = jnp.stack(
        [
            adjoint_seed[0] * central_slope(padded_velocity[0], comp)
            + adjoint_seed[1] * central_slope(padded_velocity[1], comp)
            + adjoint_seed[2] * central_slope(padded_velocity[2], comp)
            for comp in range(3)
        ]
    )
    carried = jnp.stack(
        [
            central_slope(padded_velocity[0] * padded_seed[comp], 0)
            + central_slope(padded_velocity[1] * padded_seed[comp], 1)
            + central_slope(padded_velocity[2] * padded_seed[comp], 2)
            for comp in range(3)
        ]
    )
    velocity_adjoint = adjoint_seed + time_step * (
        viscosity * laplace(padded_seed) - shear_terms + carried
    )
    return (next_velocity, velocity_adjoint, design_gradient)


def solution(mesh):
    return jax.shard_map(
        on_device,
        mesh=mesh,
        in_specs=(
            P(None, "gx", "gy", "gz"),
            P(None, "gx", "gy", "gz"),
            P("gx", "gy", "gz"),
            P("gx", "gy", "gz"),
            P(),
            P(),
        ),
        out_specs=(P(None, "gx", "gy", "gz"), P(None, "gx", "gy", "gz"), P("gx", "gy", "gz")),
        check_vma=False,
    )
```

time: 518 us -> 222 us (0.43)
  the two profiles are of different devices: /device:TPU:24 before, /device:TPU:1 now
where the time goes in v1:
time: 222 us; the launch traced here: 219 us
  Pallas kernels  123 us (55%)
  starting transfers between devices  34.3 us (15%)
  other arithmetic  33.3 us (15%)
  local copies, waits for them, and re-layouts  18.2 us (8%)
  waiting for transfers between devices  8.12 us (4%)
    pallas_call x2, Pallas kernels, spectral_call(): pl.pallas_call(kernel, out_shape=jax.ShapeDtypeStruct(out, f32), in_specs...  123 us
    concatenate x2, other arithmetic, padded_2(): jnp.concatenate([jnp.pad(low, around), array, jnp.pad(high, around)], axi...  15.8 us
    ppermute x3, starting transfers between devices, padded_2(): lax.ppermute(last, axis, up)  13.6 us
    ppermute x3, starting transfers between devices, padded_3(): lax.ppermute(lax.slice_in_dim(block, block.shape[dim] - width, None, axis...  11.3 us
    ppermute x3, waiting for transfers between devices, padded_3(): lax.ppermute(lax.slice_in_dim(block, 0, width, axis=dim), axis, backward)  7.17 us
    ppermute x3, starting transfers between devices, padded_3(): lax.ppermute(lax.slice_in_dim(block, 0, width, axis=dim), axis, backward)  4.73 us
    slice x2, local copies, waits for them, and re-layouts, padded_2(): first = lax.slice_in_dim(array, 0, width, axis=dim)  4.64 us
    ppermute x3, starting transfers between devices, padded_2(): lax.ppermute(first, axis, [(b, a) for a, b in up])  4.62 us
  transfers between devices with their start and end apart: 12, of which 2 were waited for; matrix products, arithmetic and copies ran while one was open for 15% of the time, Pallas kernels for 56%

profile of v1, /device:TPU:1, one launch (start us, length us, event | category | flops | bytes accessed | tf_op | source)
XLA Modules:
  0.0 218.7 jit_solution(13360587778249415470)
XLA Ops:
  0.6 1.7 pad_maximum_fusion.38
  2.3 4.9 %collective-permute-start.3 = (f32[7,32,1,128]{3,2,1,0:T(1,128)S(1)}, f32[7,32,1,128]{3,2,1,0:T(1,128)S(1)}, u32[]{:S(2)}, u32[]{:S(2)}) collective-permute-start(f32[7,32,1,128]{3,2,1,0:T(1,128)S(1)} %get-tuple-element.28), channel_id=1, source_target_pairs={{0,2},{2,4},{4,6},{6,8},{8,10},{10,12},{12,14},{14,16},{16,18},{18... | collective-permute-start | bytes 344072 | tf_op jit(solution)/shard_map/ppermute | solution.py:446
  7.3 2.1 collective-permute-start.2
  9.3 1.6 pad_maximum_fusion.2
  10.9 2.4 %fusion.78 = (f32[7,32,16,1]{3,2,1,0:T(8,128)}, f32[7,32,16,1]{3,2,1,0:T(8,128)}) fusion(f32[7,32,16,128]{3,2,1,0:T(8,128)S(1)} %pad_maximum_fusion.2), kind=kLoop, calls=%fused_computation.187 | loop fusion | bytes 57344 | tf_op jit(solution)/shard_map/slice | solution.py:444
  13.3 2.2 %copy.42 = f32[7,32,16,1]{1,2,3,0:T(8,128)S(1)} copy(f32[7,32,16,1]{3,2,1,0:T(8,128)} %get-tuple-element.26) | data formatting | bytes 28672 | tf_op jit(solution)/shard_map/slice | solution.py:444
  16.9 3.2 %collective-permute-start.1 = (f32[7,1,16,128]{3,2,1,0:T(8,128)S(1)}, f32[7,1,16,128]{3,2,1,0:T(8,128)S(1)}, u32[]{:S(2)}, u32[]{:S(2)}) collective-permute-start(f32[7,1,16,128]{3,2,1,0:T(8,128)S(1)} %get-tuple-element.30), channel_id=1, source_target_pairs={{0,32},{32,64},{64,96},{96,128},{128,160},{160,192},{192,224},{1,3... | collective-permute-start | bytes 172040 | tf_op jit(solution)/shard_map/ppermute | solution.py:446
  22.2 2.2 %copy.44 = f32[7,32,16,1]{1,2,3,0:T(8,128)S(1)} copy(f32[7,32,16,1]{3,2,1,0:T(8,128)} %get-tuple-element.27) | data formatting | bytes 28672 | tf_op jit(solution)/shard_map/slice | solution.py:443
  24.5 5.5 %collective-permute-start.5 = (f32[7,32,16,1]{1,2,3,0:T(8,128)S(1)}, f32[7,32,16,1]{1,2,3,0:T(8,128)S(1)}, u32[]{:S(2)}, u32[]{:S(2)}) collective-permute-start(f32[7,32,16,1]{1,2,3,0:T(8,128)S(1)} %copy.44), channel_id=1, source_target_pairs={{0,1},{2,3},{4,5},{6,7},{8,9},{10,11},{12,13},{14,15},{16,17},{18,... | collective-permute-start | bytes 43016 | tf_op jit(solution)/shard_map/ppermute | solution.py:446
  30.1 64.9 %shard_map.175 = f32[3,512,128]{2,1,0:T(8,128)} custom-call(f32[512,128]{1,0:T(8,128)} %bitcast.189, s32[2,3]{1,0:T(2,128)} %bounds.3, bf16[256,384]{1,0:T(8,128)(2,1)} %constant.53.clone.forward_z, bf16[256,384]{1,0:T(8,128)(2,1)} %constant.54.clone.lower_x, f32[2,128,256]{2,1,0:T(8,128)} %constant.55.clone.twiddle, ...), custom_call_target="tpu_custom_call" | custom-call | tf_op jit(solution)/shard_map/pallas_call | solution.py:405
  95.0 2.0 copy.43
  97.0 3.4 %pad.16 = f32[7,34,18,1]{3,2,1,0:T(8,128)} pad(f32[7,32,16,1]{3,2,1,0:T(8,128)} %copy.43, f32[]{:T(128)} %constant.20.clone.1), padding=0_0x1_1x1_1x0_0 | pad | bytes 31476 | tf_op jit(solution)/shard_map/jit(_pad)/pad | solution.py:453
  100.4 2.0 copy.45
  102.4 2.0 pad.17
  104.8 7.1 %pad_maximum_fusion.1 = f32[7,34,18,130]{3,2,1,0:T(8,128)S(1)} fusion(f32[7,34,18,1]{3,2,1,0:T(8,128)S(1)} %copy-done.2, f32[7,34,1,128]{3,2,1,0:T(1,128)S(1)} %pad.14, f32[7,1,16,128]{3,2,1,0:T(8,128)S(1)} %collective-permute-done, f32[1,32,16,128]{3,2,1,0:T(8,128)S(1)} %bitcast.179, f32[3,32,16,128]{3,2,1,0:T(8,128)S(1)} %copy-done.1, ...), kind=kLoop, calls=%fused_computation.2 | loop fusion | flops 4455360 | bytes 4455360 | tf_op jit(solution)/shard_map/concatenate | solution.py:453
  116.6 2.0 collective-permute-start.7
  121.2 8.8 %pad_maximum_fusion = (f32[7,34,18,129]{3,2,1,0:T(8,128)S(1)}, f32[7,34,18,129]{3,2,1,0:T(8,128)}) fusion(f32[7,34,18,1]{3,2,1,0:T(8,128)S(1)} %copy-done.2, f32[7,34,1,128]{3,2,1,0:T(1,128)S(1)} %pad.14, f32[7,1,16,128]{3,2,1,0:T(8,128)S(1)} %collective-permute-done, f32[1,32,16,128]{3,2,1,0:T(8,128)S(1)} %bitcast.180, f32[3,32,16,128]{3,2,1,0:T(8,128)S(1)} %copy-done.1, ...), kind=kLoop, calls=%fused_computation | loop fusion | flops 7736904 | bytes 6648768 | tf_op jit(solution)/shard_map/concatenate | solution.py:453
  130.0 3.9 %fusion.5 = f32[3,32,16,128]{3,2,1,0:T(8,128)} fusion(f32[3,32,16,128]{3,2,1,0:T(8,128)S(1)} %copy-done.1, f32[7,34,18,129]{3,2,1,0:T(8,128)} %get-tuple-element.25, f32[7,34,18,129]{3,2,1,0:T(8,128)S(1)} %get-tuple-element.24, f32[7,34,1,128]{3,2,1,0:T(1,128)S(1)} %pad.15, f32[7,1,16,128]{3,2,1,0:T(8,128)S(1)} %collective-permute-done, ...), kind=kLoop, calls=%fused_computation.21 | loop fusion | flops 6291456 | bytes 6125568 | tf_op jit(solution)/shard_map/add | solution.py:536
  133.9 3.8 %collective-permute-start.9 = (f32[34,1,128]{2,1,0:T(1,128)S(1)}, f32[34,1,128]{2,1,0:T(1,128)S(1)}, u32[]{:S(2)}, u32[]{:S(2)}) collective-permute-start(f32[34,1,128]{2,1,0:T(1,128)S(1)} %get-tuple-element.42), channel_id=1, source_target_pairs={{0,2},{2,4},{4,6},{6,8},{8,10},{10,12},{12,14},{14,16},{16,18},{18... | collective-permute-start | bytes 52232 | tf_op jit(solution)/shard_map/ppermute | solution.py:463
  137.7 1.9 collective-permute-start.8
  140.4 58.0 %shard_map.176 = f32[512,128]{1,0:T(8,128)} custom-call(f32[3,512,128]{2,1,0:T(8,128)} %get-tuple-element.34.adjoint_in, s32[2,3]{1,0:T(2,128)} %bounds.3, bf16[256,384]{1,0:T(8,128)(2,1)} %constant.53.clone.forward_z, bf16[2,256,768]{2,1,0:T(8,128)(2,1)} %constant.61.clone.forward_x, f32[2,128,256]{2,1,0:T(8,128)} %constant.55.clone.twiddle, ...), custom_call_target="tpu_custom_call" | custom-call | tf_op jit(solution)/shard_map/pallas_call | solution.py:405
  200.0 5.5 %collective-permute-start.11 = (f32[34,18,1]{2,1,0:T(8,128)S(1)}, f32[34,18,1]{2,1,0:T(8,128)S(1)}, u32[]{:S(2)}, u32[]{:S(2)}) collective-permute-start(f32[34,18,1]{2,1,0:T(8,128)S(1)} %get-tuple-element.41), channel_id=1, source_target_pairs={{0,1},{2,3},{4,5},{6,7},{8,9},{10,11},{12,13},{14,15},{16,17},{18,... | collective-permute-start | bytes 7352 | tf_op jit(solution)/shard_map/ppermute | solution.py:463
  205.7 7.2 %collective-permute-done.10 = f32[34,18,1]{2,1,0:T(8,128)S(1)} collective-permute-done((f32[34,18,1]{2,1,0:T(8,128)S(1)}, f32[34,18,1]{2,1,0:T(8,128)S(1)}, u32[]{:S(2)}, u32[]{:S(2)}) %collective-permute-start.10) | collective-permute-done | bytes 2480 | tf_op jit(solution)/shard_map/ppermute | solution.py:466
  214.1 3.9 %fusion.14 = f32[3,32,16,128]{3,2,1,0:T(8,128)} fusion(f32[3,32,16,128]{3,2,1,0:T(8,128)S(1)} %copy-done, f32[7,34,18,129]{3,2,1,0:T(8,128)} %get-tuple-element.25, f32[7,34,18,129]{3,2,1,0:T(8,128)} %copy-done.4, f32[7,34,1,128]{3,2,1,0:T(1,128)S(1)} %pad.15, f32[7,1,16,128]{3,2,1,0:T(8,128)S(1)} %collective-permute-done, ...), kind=kLoop, calls=%fused_computation.48 | loop fusion | flops 6291456 | bytes 6125568 | tf_op jit(solution)/shard_map/add | solution.py:510
  (52 shorter events, 14.8 us)
Async XLA Ops:
  2.3 102.1 %collective-permute-start.3 = (f32[7,32,1,128]{3,2,1,0:T(1,128)S(1)}, f32[7,32,1,128]{3,2,1,0:T(1,128)S(1)}, u32[]{:S(2)}, u32[]{:S(2)}) collective-permute-start(f32[7,32,1,128]{3,2,1,0:T(1,128)S(1)} %get-tuple-element.28), channel_id=1, source_target_pairs={{0,2},{2,4},{4,6},{6,8},{8,10},{10,12},{12,14},{14,16},{16,18},{18... | collective-permute-start | bytes 344072 | tf_op jit(solution)/shard_map/ppermute | solution.py:446
  7.2 9.6 %copy-start = (f32[3,32,16,128]{3,2,1,0:T(8,128)S(1)}, f32[3,32,16,128]{3,2,1,0:T(8,128)}, u32[]{:S(2)}) copy-start(f32[3,32,16,128]{3,2,1,0:T(8,128)} %param.16) | copy-start | bytes 2359300
  7.3 9.6 %copy-start.1 = (f32[3,32,16,128]{3,2,1,0:T(8,128)S(1)}, f32[3,32,16,128]{3,2,1,0:T(8,128)}, u32[]{:S(2)}) copy-start(f32[3,32,16,128]{3,2,1,0:T(8,128)} %param.17) | copy-start | bytes 2359300
  7.3 9.6 %copy-start.3 = (f32[32,16,128]{2,1,0:T(8,128)S(1)}, f32[32,16,128]{2,1,0:T(8,128)}, u32[]{:S(2)}) copy-start(f32[32,16,128]{2,1,0:T(8,128)} %param.18) | copy-start | bytes 786436
  7.3 97.2 %collective-permute-start.2 = (f32[7,32,1,128]{3,2,1,0:T(1,128)S(1)}, f32[7,32,1,128]{3,2,1,0:T(1,128)S(1)}, u32[]{:S(2)}, u32[]{:S(2)}) collective-permute-start(f32[7,32,1,128]{3,2,1,0:T(1,128)S(1)} %get-tuple-element.29), channel_id=1, source_target_pairs={{2,0},{4,2},{6,4},{8,6},{10,8},{12,10},{14,12},{16,14},{18,16},{20... | collective-permute-start | bytes 344072 | tf_op jit(solution)/shard_map/ppermute | solution.py:447
  15.6 8.9 %collective-permute-start.4 = (f32[7,32,16,1]{1,2,3,0:T(8,128)S(1)}, f32[7,32,16,1]{1,2,3,0:T(8,128)S(1)}, u32[]{:S(2)}, u32[]{:S(2)}) collective-permute-start(f32[7,32,16,1]{1,2,3,0:T(8,128)S(1)} %copy.42), channel_id=1, source_target_pairs={{1,0},{3,2},{5,4},{7,6},{9,8},{11,10},{13,12},{15,14},{17,16},{19,... | collective-permute-start | bytes 43016 | tf_op jit(solution)/shard_map/ppermute | solution.py:447
  16.9 87.7 %collective-permute-start.1 = (f32[7,1,16,128]{3,2,1,0:T(8,128)S(1)}, f32[7,1,16,128]{3,2,1,0:T(8,128)S(1)}, u32[]{:S(2)}, u32[]{:S(2)}) collective-permute-start(f32[7,1,16,128]{3,2,1,0:T(8,128)S(1)} %get-tuple-element.30), channel_id=1, source_target_pairs={{0,32},{32,64},{64,96},{96,128},{128,160},{160,192},{192,224},{1,3... | collective-permute-start | bytes 172040 | tf_op jit(solution)/shard_map/ppermute | solution.py:446
  20.1 84.5 %collective-permute-start = (f32[7,1,16,128]{3,2,1,0:T(8,128)S(1)}, f32[7,1,16,128]{3,2,1,0:T(8,128)S(1)}, u32[]{:S(2)}, u32[]{:S(2)}) collective-permute-start(f32[7,1,16,128]{3,2,1,0:T(8,128)S(1)} %get-tuple-element.31), channel_id=1, source_target_pairs={{32,0},{64,32},{96,64},{128,96},{160,128},{192,160},{224,192},{33,... | collective-permute-start | bytes 172040 | tf_op jit(solution)/shard_map/ppermute | solution.py:447
  24.5 75.9 %collective-permute-start.5 = (f32[7,32,16,1]{1,2,3,0:T(8,128)S(1)}, f32[7,32,16,1]{1,2,3,0:T(8,128)S(1)}, u32[]{:S(2)}, u32[]{:S(2)}) collective-permute-start(f32[7,32,16,1]{1,2,3,0:T(8,128)S(1)} %copy.44), channel_id=1, source_target_pairs={{0,1},{2,3},{4,5},{6,7},{8,9},{10,11},{12,13},{14,15},{16,17},{18,... | collective-permute-start | bytes 43016 | tf_op jit(solution)/shard_map/ppermute | solution.py:446
  102.4 2.4 %copy-start.2 = (f32[7,34,18,1]{3,2,1,0:T(8,128)S(1)}, f32[7,34,18,1]{3,2,1,0:T(8,128)}, u32[]{:S(2)}) copy-start(f32[7,34,18,1]{3,2,1,0:T(8,128)} %pad.16) | copy-start | bytes 51412
  114.3 1.1 copy-start.5
  116.6 17.3 %collective-permute-start.7 = (f32[1,16,128]{2,1,0:T(8,128)S(1)}, f32[1,16,128]{2,1,0:T(8,128)S(1)}, u32[]{:S(2)}, u32[]{:S(2)}) collective-permute-start(f32[1,16,128]{2,1,0:T(8,128)S(1)} %get-tuple-element.44), channel_id=1, source_target_pairs={{0,32},{32,64},{64,96},{96,128},{128,160},{160,192},{192,224},{1,3... | collective-permute-start | bytes 24584 | tf_op jit(solution)/shard_map/ppermute | solution.py:463
  118.5 15.3 %collective-permute-start.6 = (f32[1,16,128]{2,1,0:T(8,128)S(1)}, f32[1,16,128]{2,1,0:T(8,128)S(1)}, u32[]{:S(2)}, u32[]{:S(2)}) collective-permute-start(f32[1,16,128]{2,1,0:T(8,128)S(1)} %get-tuple-element.45), channel_id=1, source_target_pairs={{32,0},{64,32},{96,64},{128,96},{160,128},{192,160},{224,192},{33,... | collective-permute-start | bytes 24584 | tf_op jit(solution)/shard_map/ppermute | solution.py:466
  130.0 10.4 %copy-start.4 = (f32[7,34,18,129]{3,2,1,0:T(8,128)}, f32[7,34,18,129]{3,2,1,0:T(8,128)S(1)}, u32[]{:S(2)}) copy-start(f32[7,34,18,129]{3,2,1,0:T(8,128)S(1)} %get-tuple-element.24) | copy-start | bytes 6631636
  133.9 64.6 %collective-permute-start.9 = (f32[34,1,128]{2,1,0:T(1,128)S(1)}, f32[34,1,128]{2,1,0:T(1,128)S(1)}, u32[]{:S(2)}, u32[]{:S(2)}) collective-permute-start(f32[34,1,128]{2,1,0:T(1,128)S(1)} %get-tuple-element.42), channel_id=1, source_target_pairs={{0,2},{2,4},{4,6},{6,8},{8,10},{10,12},{12,14},{14,16},{16,18},{18... | collective-permute-start | bytes 52232 | tf_op jit(solution)/shard_map/ppermute | solution.py:463
  137.7 60.7 %collective-permute-start.8 = (f32[34,1,128]{2,1,0:T(1,128)S(1)}, f32[34,1,128]{2,1,0:T(1,128)S(1)}, u32[]{:S(2)}, u32[]{:S(2)}) collective-permute-start(f32[34,1,128]{2,1,0:T(1,128)S(1)} %get-tuple-element.43), channel_id=1, source_target_pairs={{2,0},{4,2},{6,4},{8,6},{10,8},{12,10},{14,12},{16,14},{18,16},{20... | collective-permute-start | bytes 52232 | tf_op jit(solution)/shard_map/ppermute | solution.py:466
  198.4 19.6 %copy-start.6 = (f32[512,128]{1,0:T(8,128)S(1)}, f32[512,128]{1,0:T(8,128)}, u32[]{:S(2)}) copy-start(f32[512,128]{1,0:T(8,128)} %shard_map.176) | copy-start | bytes 786436
  198.7 14.1 %collective-permute-start.10 = (f32[34,18,1]{2,1,0:T(8,128)S(1)}, f32[34,18,1]{2,1,0:T(8,128)S(1)}, u32[]{:S(2)}, u32[]{:S(2)}) collective-permute-start(f32[34,18,1]{2,1,0:T(8,128)S(1)} %get-tuple-element.40), channel_id=1, source_target_pairs={{1,0},{3,2},{5,4},{7,6},{9,8},{11,10},{13,12},{15,14},{17,16},{19,... | collective-permute-start | bytes 7352 | tf_op jit(solution)/shard_map/ppermute | solution.py:466
  200.0 13.7 %collective-permute-start.11 = (f32[34,18,1]{2,1,0:T(8,128)S(1)}, f32[34,18,1]{2,1,0:T(8,128)S(1)}, u32[]{:S(2)}, u32[]{:S(2)}) collective-permute-start(f32[34,18,1]{2,1,0:T(8,128)S(1)} %get-tuple-element.41), channel_id=1, source_target_pairs={{0,1},{2,3},{4,5},{6,7},{8,9},{10,11},{12,13},{14,15},{16,17},{18,... | collective-permute-start | bytes 7352 | tf_op jit(solution)/shard_map/ppermute | solution.py:463

commit v2 on v1

v2 whole, which is shorter than its diff:
```python
import jax
import jax.numpy as jnp
import numpy as np
from jax import lax
from jax.experimental import pallas as pl
from jax.experimental.pallas import tpu as pltpu
from jax.sharding import PartitionSpec as P

time_step = 0.5
viscosity = 0.2
field_period = 24
full_turn = 6.283185307179586

bf16 = jnp.bfloat16
f32 = jnp.float32
MESH = pl.DeviceIdType.MESH


def pieces(matrix):
    matrix = np.asarray(matrix, np.float32)
    high = matrix.astype(jnp.bfloat16)
    low = (matrix - high.astype(np.float32)).astype(jnp.bfloat16)
    return np.concatenate([high, high, low], axis=-1)


def cut(value, axis):
    high = value.astype(bf16)
    low = (value - high.astype(f32)).astype(bf16)
    return jnp.concatenate([high, low, high], axis=axis)


def mul(matrix, value):
    return jnp.dot(matrix, cut(value, 0), preferred_element_type=f32)


def make_tables():
    turn = 2.0 * np.pi / 256
    eye8, eye16 = np.eye(8), np.eye(16)
    k3 = 1 + 8 * np.arange(16)[:, None] + np.arange(8)[None, :]
    z = np.arange(128)
    phase = turn * k3[:, :, None] * z
    forward_z = np.stack([np.cos(phase), -np.sin(phase)], 1).reshape(256, 128)
    weight = np.where(k3 == 128, 1.0, 2.0)[:, :, None] / 256.0**3
    inverse_z = []
    for part in range(2):
        phase = turn * k3[:, :, None] * (z + 128 * part)
        both = np.stack([np.cos(phase) * weight, -np.sin(phase) * weight], 1)
        inverse_z.append(both.reshape(256, 128).T)
    q, t, ka = np.arange(8), np.arange(2), np.arange(16)
    theta = turn * 16 * (2 * q[:, None, None] + t[None, :, None]) * ka
    c, s = np.cos(theta), np.sin(theta)
    turned = np.stack([np.stack([c, s]), np.stack([-s, c])])
    sign = np.stack([np.ones(8), (-1.0) ** (1 + np.arange(8))])
    forward_x = np.einsum("abqtk,gj,ji->takiqgbj", turned, sign, eye8)
    forward_x = forward_x.reshape(2, 256, 256)
    lower = np.einsum("abqtk,ji->akitqbj", turned[:, :, :4], eye8).reshape(256, 128)
    back = np.stack([np.stack([c, -s]), np.stack([s, c])])
    inverse_x = np.einsum("abqtk,ij->tqaibkj", back, eye8).reshape(256, 256)
    lower_back = np.einsum("abqtk,ij->tqaibkj", back[:, :, :4], eye8).reshape(128, 256)
    b = np.arange(16)
    phi = turn * ka[:, None] * b
    twiddle = np.stack([np.cos(phi), np.sin(phi)])[:, :, None, :, None]
    twiddle = np.broadcast_to(twiddle, (2, 16, 8, 16, 16)).reshape(2, 128, 256)
    angle = turn * 16 * b[:, None] * b
    kron = [np.kron(np.cos(angle), eye16), np.kron(np.sin(angle), eye16)]
    k = np.arange(256)
    angle = turn * (k[:, None] * k % 256)
    second = np.stack([np.cos(angle), np.sin(angle)])
    return dict(
        forward_z=pieces(forward_z),
        inverse_z=pieces(np.stack(inverse_z)),
        forward_x=pieces(forward_x),
        lower_x=pieces(lower),
        inverse_x=pieces(inverse_x),
        lower_back=pieces(lower_back),
        twiddle=twiddle.astype(np.float32),
        kron=pieces(np.stack(kron)),
        second=pieces(second),
        second_lower=pieces(second[:, :, :128]),
    )


def rotated(pair, value, direction):
    value = cut(value, 0)
    first = jnp.dot(pair[0], value, preferred_element_type=f32)
    second = jnp.dot(pair[1], value, preferred_element_type=f32)
    real = first[:, :128] - direction * second[:, 128:]
    imag = first[:, 128:] + direction * second[:, :128]
    return real, imag


def depth_waves(block, forward_z):
    return lax.dot_general(
        forward_z, cut(block, 1), (((1,), (1,)), ((), ())), preferred_element_type=f32
    )


def first_forward(mixed, twiddle, kron):
    real, imag = mixed[:128], mixed[128:]
    c, s = twiddle[0], twiddle[1]
    turned = jnp.concatenate([real * c + imag * s, imag * c - real * s], axis=0)
    return rotated(kron, turned.T, -1.0)


def first_inverse(value, twiddle, kron, inverse_x):
    real, imag = rotated(kron, value, 1.0)
    turned = jnp.concatenate([real, imag], axis=1).T
    real, imag = turned[:128], turned[128:]
    c, s = twiddle[0], twiddle[1]
    turned = jnp.concatenate([real * c - imag * s, imag * c + real * s], axis=0)
    return mul(inverse_x, turned)


def signed_wave(index):
    folded = jnp.where(index < 128, index, index - 256)
    return jnp.where(index == 128, 0, folded).astype(f32) * (full_turn / 256)


def factor_of(index, third):
    half = full_turn / 2
    return jnp.where(third == 128, jnp.where(index == 128, half, 0.0), signed_wave(index))


def spectral_factors(place, gy):
    row = lax.broadcasted_iota(jnp.int32, (256, 128), 0)
    lane = lax.broadcasted_iota(jnp.int32, (256, 128), 1)
    third = 1 + 8 * place + lane % 8
    first = lane // 8 + 16 * gy
    third_wave = third.astype(f32) * (full_turn / 256)
    fold = lambda i: jnp.where(i < 128, i, i - 256).astype(f32) * (full_turn / 256)
    first_wave, second_wave = fold(first), fold(row)
    square = first_wave * first_wave + second_wave * second_wave + third_wave * third_wave
    return -third_wave / square, factor_of(row, third)


def mixing_factors(place):
    row = lax.broadcasted_iota(jnp.int32, (256, 128), 0)
    lane = lax.broadcasted_iota(jnp.int32, (256, 128), 1)
    third = 1 + 8 * place + lane % 8
    return factor_of(lane // 8 + 16 * (row // 16), third), third.astype(f32) * (full_turn / 256)


def twice(value):
    return jnp.concatenate([value, value], axis=1)


class Place:
    def __init__(self):
        self.gx, self.gy, self.gz = (lax.axis_index(a) for a in ("gx", "gy", "gz"))
        self.wave = self.gx * 2 + self.gz

    def by_wave(self, wave):
        return (wave // 2, self.gy, wave % 2)

    def by_second(self, second):
        return (self.gx, second, self.gz)

    def greet(self):
        barrier = pltpu.get_barrier_semaphore()

        def signal(step, carry):
            for target in (
                self.by_wave((self.wave + step) % 16),
                self.by_second((self.gy + step) % 16),
            ):
                pl.semaphore_signal(barrier, inc=1, device_id=target, device_id_type=MESH)
            return carry

        lax.fori_loop(1, 16, signal, 0)
        pl.semaphore_wait(barrier, 30)


class Exchange:
    def __init__(self, me, device, src, dst, send_sem, recv_sem, wanted=None):
        self.me, self.device, self.src, self.dst = me, device, src, dst
        self.send_sem, self.recv_sem, self.wanted = send_sem, recv_sem, wanted

    def each(self, act):
        def body(step, carry):
            peer = (self.me + step) % 16
            copy = pltpu.make_async_remote_copy(
                src_ref=self.src(peer),
                dst_ref=self.dst,
                send_sem=self.send_sem(peer),
                recv_sem=self.recv_sem,
                device_id=self.device(peer),
                device_id_type=MESH,
            )
            if self.wanted is None:
                act(copy)
            else:
                pl.when(self.wanted(peer))(lambda: act(copy))
            return carry

        lax.fori_loop(1, 16, body, 0)

    def start(self):
        self.each(lambda copy: copy.start())
        own = pltpu.make_async_copy(self.src(self.me), self.dst, self.recv_sem)
        if self.wanted is None:
            own.start()
        else:
            pl.when(self.wanted(self.me))(lambda: own.start())

    def finish(self):
        self.each(lambda copy: copy.wait_send())


def arrived(count, block, sem, skip=None):
    def wait(step, carry):
        pltpu.make_async_copy(block(step), block(step), sem(step)).wait()
        return carry

    lax.fori_loop(0, count, wait, 0)


def region(at, bounds):
    row = lax.broadcasted_iota(jnp.int32, (512, 128), 0)
    third = lax.broadcasted_iota(jnp.int32, (512, 128), 1) + at.gz * 128
    first, second = row // 16 + at.gx * 32, row % 16 + at.gy * 16
    inside = (first >= bounds[0, 0]) & (first < bounds[1, 0])
    inside = inside & (second >= bounds[0, 1]) & (second < bounds[1, 1])
    inside = inside & (third >= bounds[0, 2]) & (third < bounds[1, 2])
    return jnp.where(inside, 1.0, 0.0)


class Halo:
    def __init__(self, at, block, second_out, second_in, third_out, third_in, sent, got):
        self.at, self.block = at, block
        self.second_out, self.second_in = second_out, second_in
        self.third_out, self.third_in = third_out, third_in
        gx, gy, gz = at.gx, at.gy, at.gz
        self.copies = []
        for number, (src, dst, there, here, target) in enumerate(
            (
                (block.at[:, 32], block.at[:, 0], gx < 7, gx > 0, ((gx + 1) % 8, gy, gz)),
                (block.at[:, 1], block.at[:, 33], gx > 0, gx < 7, ((gx + 7) % 8, gy, gz)),
                (second_out.at[1], second_in.at[0], gy < 15, gy > 0, (gx, (gy + 1) % 16, gz)),
                (second_out.at[0], second_in.at[1], gy > 0, gy < 15, (gx, (gy + 15) % 16, gz)),
                (third_out, third_in, None, None, (gx, gy, 1 - gz)),
            )
        ):
            copy = pltpu.make_async_remote_copy(
                src_ref=src,
                dst_ref=dst,
                send_sem=sent.at[number],
                recv_sem=got.at[number],
                device_id=target,
                device_id_type=MESH,
            )
            self.copies.append((copy, there, here, dst))

    def start(self):
        block = self.block
        for face, row in ((0, 0), (1, 15)):
            self.second_out[face] = block[:, 1:33, row, :]
        for f in range(block.shape[0]):
            cells = block[f, 1:33].reshape(512, 128).T
            row = jnp.where(self.at.gz == 0, cells[127:128], cells[0:1])
            self.third_out[f : f + 1] = row
        for copy, there, here, dst in self.copies:
            if there is None:
                copy.start()
            else:
                pl.when(there)(lambda copy=copy: copy.start())

    def arrive(self, wide):
        for copy, there, here, dst in self.copies:
            if here is None:
                copy.wait_recv()
            else:
                pl.when(here)(lambda copy=copy: copy.wait_recv())

                @pl.when(jnp.logical_not(here))
                def _(dst=dst):
                    dst[...] = jnp.zeros(dst.shape, f32)

        for f in range(self.block.shape[0]):
            row = jnp.broadcast_to(self.third_in[f : f + 1], (128, 512))
            wide[f] = row.T.reshape(32, 16, 128)

    def finish(self):
        for copy, there, here, dst in self.copies:
            if there is None:
                copy.wait_send()
            else:
                pl.when(there)(lambda copy=copy: copy.wait_send())


def neighbours(at, halo, wide, f, i):
    block = halo.block
    here = block[f, i + 1]
    row = lax.broadcasted_iota(jnp.int32, (16, 128), 0)
    lane = lax.broadcasted_iota(jnp.int32, (16, 128), 1)
    below = halo.second_in[0, f, pl.ds(i, 1)]
    above = halo.second_in[1, f, pl.ds(i, 1)]
    side = wide[f, i]
    second = (
        jnp.where(row == 0, below, pltpu.roll(here, 1, 0)),
        jnp.where(row == 15, above, pltpu.roll(here, 15, 0)),
    )
    third = (
        jnp.where(lane == 0, jnp.where(at.gz == 1, side, 0.0), pltpu.roll(here, 1, 1)),
        jnp.where(lane == 127, jnp.where(at.gz == 0, side, 0.0), pltpu.roll(here, 127, 1)),
    )
    return here, ((block[f, i], block[f, i + 2]), second, third)


def laplace(here, around):
    total = -6.0 * here
    for low, high in around:
        total = total + (low + high)
    return total


def slope(pair):
    return (pair[1] - pair[0]) * 0.5


def cell_rows(at, halo, wide, next_out, adjoint_out, source):
    def body(i, carry):
        cells = [neighbours(at, halo, wide, f, i) for f in range(7)]
        velocity, seed = cells[:3], cells[3:6]
        suscept = cells[6]
        total = 0.0
        for d in range(3):
            pair = [suscept[1][d][e] * seed[d][1][d][e] for e in range(2)]
            total = total + slope(pair)
        source[i] = -time_step * total
        for k in range(3):
            here, around = velocity[k]
            advect = sum(velocity[j][0] * slope(around[j]) for j in range(3))
            next_out[k, i] = here + time_step * (viscosity * laplace(here, around) - advect)
            here, around = seed[k]
            shear = sum(seed[j][0] * slope(velocity[j][1][k]) for j in range(3))
            carried = sum(
                slope([velocity[j][1][j][e] * around[j][e] for e in range(2)]) for j in range(3)
            )
            adjoint_out[k, i] = here + time_step * (
                viscosity * laplace(here, around) - shear + carried
            )
        return carry

    lax.fori_loop(0, 32, body, 0)


def energy_rows(at, halo, wide, suscept, next_out):
    def body(i, carry):
        _, around = neighbours(at, halo, wide, 0, i)
        scaled = time_step * suscept[i]
        for k in range(3):
            next_out[k, i] = next_out[k, i] + scaled * slope(around[k])
        return carry

    lax.fori_loop(0, 32, body, 0)


ORDER = (0, 2, 1)


def kernel(
    velocity, adjoint_seed, suscept, remanence, bounds, step,
    forward_z, inverse_z, forward_x, lower_x, inverse_x, lower_back, twiddle, kron, second,
    second_lower,
    next_out, adjoint_out, gradient_out,
    z_out, z_in, k_out, k_in, y_out, y_in, x_out, x_in,
    zb_out, zb_in, kb_out, kb_in, yb_out, yb_in, xb_out, xb_in,
    cells, cells_y_out, cells_y_in, cells_z_out, cells_z_in, cells_wide,
    energy, energy_y_out, energy_y_in, energy_z_out, energy_z_in, energy_wide, source,
    z_sent, z_got, k_sent, k_got, y_sent, y_got, x_sent, x_got,
    zb_sent, zb_got, kb_sent, kb_got, yb_sent, yb_got, xb_sent, xb_got,
    cells_sent, cells_got, energy_sent, energy_got,
):
    at = Place()
    at.greet()
    in_lower = (at.gx < 4) & (at.gy < 8) & (at.gz == 0)
    has_rows = at.gy < 8

    depths = Exchange(
        at.wave, at.by_wave, lambda p: z_out.at[p], z_in.at[at.gx % 4],
        lambda p: z_sent.at[p], z_got.at[at.gx % 4],
    )
    firsts = Exchange(
        at.gy, at.by_second, lambda p: k_out.at[p], k_in.at[at.gy % 8],
        lambda p: k_sent.at[p], k_got.at[at.gy % 8],
    )
    seconds = [
        Exchange(
            at.gy, at.by_second, lambda p, f=f: y_out.at[f, p], y_in.at[f, at.gy],
            lambda p, f=f: y_sent.at[f, p], y_got.at[f, at.gy],
        )
        for f in range(2)
    ]
    lasts = [
        Exchange(
            at.wave, at.by_wave, lambda p, f=f: x_out.at[f, p // 2], x_in.at[f, at.wave],
            lambda p, f=f: x_sent.at[f, p], x_got.at[f, at.wave],
        )
        for f in range(3)
    ]
    depths_back = [
        Exchange(
            at.wave, at.by_wave, lambda p, f=f: zb_out.at[f, p], zb_in.at[f, at.wave],
            lambda p, f=f: zb_sent.at[f, p], zb_got.at[f, at.wave],
        )
        for f in range(3)
    ]
    firsts_back = [
        Exchange(
            at.gy, at.by_second, lambda p, f=f: kb_out.at[f, p], kb_in.at[f, at.gy],
            lambda p, f=f: kb_sent.at[f, p], kb_got.at[f, at.gy],
        )
        for f in range(2)
    ]
    seconds_back = Exchange(
        at.gy, at.by_second, lambda p: yb_out.at[p % 8], yb_in.at[at.gy],
        lambda p: yb_sent.at[p], yb_got.at[at.gy], lambda p: p < 8,
    )
    lasts_back = Exchange(
        at.wave, at.by_wave, lambda p: xb_out.at[p // 2 % 4], xb_in.at[at.wave],
        lambda p: xb_sent.at[p], xb_got.at[at.wave], lambda p: (p < 8) & (p % 2 == 0),
    )
    cell_halo = Halo(
        at, cells, cells_y_out, cells_y_in, cells_z_out, cells_z_in, cells_sent, cells_got
    )
    energy_halo = Halo(
        at, energy, energy_y_out, energy_y_in, energy_z_out, energy_z_in, energy_sent, energy_got
    )

    @pl.when(in_lower)
    def _():
        magnet = remanence[...].reshape(512, 128) * region(at, bounds)
        z_out[...] = depth_waves(magnet, forward_z[...]).reshape(16, 16, 512)
        depths.start()

    cells[0:3, 1:33] = velocity[...]
    cells[3:6, 1:33] = adjoint_seed[...]
    cells[6, 1:33] = suscept[...]
    cell_halo.start()

    @pl.when(has_rows)
    def _():
        arrived(4, lambda i: z_in.at[i], lambda i: z_got.at[i])
        block = z_in[...].reshape(64, 512)
        block = jnp.concatenate([block[:, :256], block[:, 256:]], axis=0)
        real, imag = first_forward(mul(lower_x[...], block), twiddle[...], kron[...])
        k_out[...] = jnp.concatenate([real, imag], axis=1).reshape(16, 16, 256)
        firsts.start()

    cell_halo.arrive(cells_wide)
    cell_rows(at, cell_halo, cells_wide, next_out, adjoint_out, source)

    potential, second_factor = spectral_factors(at.wave, at.gy)
    arrived(8, lambda i: k_in.at[i], lambda i: k_got.at[i])
    real, imag = rotated(second_lower[...], k_in[...].reshape(128, 256), -1.0)
    value = jnp.concatenate([real * potential, imag * potential], axis=1)
    for f in range(2):
        if f == 1:
            value = value * twice(second_factor)
        real, imag = rotated(second[...], value, 1.0)
        y_out[f] = jnp.concatenate([real, imag], axis=1).reshape(16, 16, 256)
        seconds[f].start()

    first_factor, third_factor = mixing_factors(at.wave)

    def send_first(f, value):
        value = first_inverse(value, twiddle[...], kron[...], inverse_x[...])
        x_out[f, :, :, :256] = value[:128].reshape(8, 16, 256)
        x_out[f, :, :, 256:] = value[128:].reshape(8, 16, 256)
        lasts[f].start()

    arrived(16, lambda i: y_in.at[0, i], lambda i: y_got.at[0, i])
    value = y_in[0].reshape(256, 256)
    send_first(0, value * twice(first_factor))
    send_first(2, value * twice(third_factor))
    arrived(16, lambda i: y_in.at[1, i], lambda i: y_got.at[1, i])
    send_first(1, y_in[1].reshape(256, 256))

    turned = jnp.full((8, 128), step[0] % field_period, jnp.int32).astype(f32)
    turned = full_turn * turned / field_period
    applied = (jnp.cos(turned)[:1], jnp.sin(turned)[:1], None)
    square = jnp.zeros((512, 128), f32)
    weight = source[...].reshape(512, 128)
    for f in ORDER:
        arrived(16, lambda i, f=f: x_in.at[f, i], lambda i, f=f: x_got.at[f, i])
        field = mul(inverse_z[at.gz], x_in[f].reshape(256, 512)).T
        if applied[f] is not None:
            field = field + applied[f]
        square = square + field * field
        zb_out[f] = depth_waves(weight * field, forward_z[...]).reshape(16, 16, 512)
        depths_back[f].start()
    energy[0, 1:33] = (0.5 * square).reshape(32, 16, 128)
    energy_halo.start()

    def first_of(f):
        arrived(16, lambda i: zb_in.at[f, i], lambda i: zb_got.at[f, i])
        block = zb_in[f].reshape(256, 512)
        mixed = mul(forward_x[0], block[:, :256]) + mul(forward_x[1], block[:, 256:])
        real, imag = first_forward(mixed, twiddle[...], kron[...])
        return jnp.concatenate([real, imag], axis=1)

    value = first_of(0) * twice(first_factor)
    value = value + first_of(2) * twice(third_factor)
    kb_out[0] = value.reshape(16, 16, 256)
    firsts_back[0].start()
    kb_out[1] = first_of(1).reshape(16, 16, 256)
    firsts_back[1].start()

    energy_halo.arrive(energy_wide)
    energy_rows(at, energy_halo, energy_wide, suscept, next_out)

    def second_of(f):
        arrived(16, lambda i: kb_in.at[f, i], lambda i: kb_got.at[f, i])
        real, imag = rotated(second[...], kb_in[f].reshape(256, 256), -1.0)
        return jnp.concatenate([real, imag], axis=1)

    value = second_of(0)
    value = (value + second_of(1) * twice(second_factor)) * twice(potential)
    real, imag = rotated(second[:, :128], value, 1.0)
    yb_out[...] = jnp.concatenate([real, imag], axis=1).reshape(8, 16, 256)
    seconds_back.start()

    @pl.when(has_rows)
    def _():
        arrived(16, lambda i: yb_in.at[i], lambda i: yb_got.at[i])
        value = yb_in[...].reshape(256, 256)
        value = first_inverse(value, twiddle[...], kron[...], lower_back[...])
        xb_out[:, :, :256] = value[:64].reshape(4, 16, 256)
        xb_out[:, :, 256:] = value[64:].reshape(4, 16, 256)
        lasts_back.start()

    gradient_out[...] = jnp.zeros((32, 16, 128), f32)

    @pl.when(in_lower)
    def _():
        arrived(16, lambda i: xb_in.at[i], lambda i: xb_got.at[i])
        value = mul(inverse_z[0], xb_in[...].reshape(256, 512)).T
        gradient_out[...] = (value * region(at, bounds)).reshape(32, 16, 128)

    pl.when(in_lower)(lambda: depths.finish())
    pl.when(has_rows)(lambda: firsts.finish())
    for each in seconds + lasts + depths_back + firsts_back + [seconds_back]:
        each.finish()
    pl.when(has_rows)(lambda: lasts_back.finish())
    cell_halo.finish()
    energy_halo.finish()


TABLES = (
    "forward_z", "inverse_z", "forward_x", "lower_x", "inverse_x", "lower_back", "twiddle",
    "kron", "second", "second_lower",
)


def on_device(velocity, adjoint_seed, susceptibility, remanence, region_bounds, step_id):
    tables = make_tables()
    shapes = [(16, 16, 512), (4, 16, 512), (16, 16, 256), (8, 16, 256)]
    shapes += [(2, 16, 16, 256), (2, 16, 16, 256), (3, 8, 16, 512), (3, 16, 16, 512)]
    shapes += [(3, 16, 16, 512), (3, 16, 16, 512), (2, 16, 16, 256), (2, 16, 16, 256)]
    shapes += [(8, 16, 256), (16, 16, 256), (4, 16, 512), (16, 16, 512)]
    for n in (7, 1):
        shapes += [(n, 34, 16, 128), (2, n, 32, 128), (2, n, 32, 128), (8, 512), (8, 512)]
        shapes += [(n, 32, 16, 128)]
    shapes += [(32, 16, 128)]
    sems = [(16,), (4,), (16,), (8,), (2, 16), (2, 16), (3, 16), (3, 16)]
    sems += [(3, 16), (3, 16), (2, 16), (2, 16), (16,), (16,), (16,), (16,)]
    sems += [(5,)] * 4
    vmem = pl.BlockSpec(memory_space=pltpu.VMEM)
    smem = pl.BlockSpec(memory_space=pltpu.SMEM)
    return pl.pallas_call(
        kernel,
        out_shape=(
            jax.ShapeDtypeStruct((3, 32, 16, 128), f32),
            jax.ShapeDtypeStruct((3, 32, 16, 128), f32),
            jax.ShapeDtypeStruct((32, 16, 128), f32),
        ),
        in_specs=[vmem] * 4 + [smem] * 2 + [vmem] * len(TABLES),
        out_specs=(vmem, vmem, vmem),
        scratch_shapes=[pltpu.VMEM(s, f32) for s in shapes]
        + [pltpu.SemaphoreType.DMA(s) for s in sems],
        compiler_params=pltpu.CompilerParams(
            collective_id=0, has_side_effects=True, vmem_limit_bytes=60 << 20
        ),
    )(
        velocity, adjoint_seed, susceptibility, remanence, region_bounds, step_id,
        *[tables[n] for n in TABLES],
    )


def solution(mesh):
    return jax.shard_map(
        on_device,
        mesh=mesh,
        in_specs=(
            P(None, "gx", "gy", "gz"),
            P(None, "gx", "gy", "gz"),
            P("gx", "gy", "gz"),
            P("gx", "gy", "gz"),
            P(),
            P(),
        ),
        out_specs=(P(None, "gx", "gy", "gz"), P(None, "gx", "gy", "gz"), P("gx", "gy", "gz")),
        check_vma=False,
    )
```

time: 222 us -> 117 us (0.53); the launches traced: 219 us -> 117 us
  starting transfers between devices: 34.3 us -> 0 us
  other arithmetic: 33.3 us -> 0 us
  local copies, waits for them, and re-layouts: 18.2 us -> 3.93 us
  Pallas kernels: 123 us -> 111 us
  waiting for transfers between devices: 8.12 us -> 0 us
    ppermute x12 -> x0, starting transfers between devices: 34.3 us -> none  [the longest x3 13.6 us: padded_2(): lax.ppermute(last, axis, up)]
    concatenate x5 -> x0, other arithmetic: 17.5 us -> none  [the longest x2 15.8 us: padded_2(): jnp.concatenate([jnp.pad(low, around), array, jnp.pad(high, around)], axi...]
    pallas_call x2 -> x1, Pallas kernels: 123 us -> 111 us  [on_device(): pl.pallas_call(kernel, out_shape=(jax.ShapeDtypeStruct((3, 32, 16, 128),...]
    ppermute x12 -> x0, waiting for transfers between devices: 8.12 us -> none  [the longest x3 7.17 us: padded_3(): lax.ppermute(lax.slice_in_dim(block, 0, width, axis=dim), axis, backward)]
    add x2 -> x0, other arithmetic: 7.77 us -> none  [the longest x1 3.92 us: on_device(): velocity + time_step * (viscosity * laplace(padded_velocity) - advect + p...]
    slice x5 -> x0, local copies, waits for them, and re-layouts: 7.08 us -> none  [the longest x2 4.64 us: padded_2(): first = lax.slice_in_dim(array, 0, width, axis=dim)]
    pad x4 -> x0, local copies, waits for them, and re-layouts: 5.52 us -> none  [the longest x2 3.47 us: padded_2(): jnp.pad(high, around)]
    ppermute x2 -> x0, local copies, waits for them, and re-layouts: 4.02 us -> none  [the longest x1 2.01 us: padded_2(): lax.ppermute(last, axis, up)]
  transfers between devices with their start and end apart: 12 -> 0, of which waited for: 2 -> 0; matrix products, arithmetic and copies ran while one was open for 15% -> 0% of each run, Pallas kernels for 56% -> 0%
where the time goes in v2:
time: 117 us
  Pallas kernels  111 us (95%)
  local copies, waits for them, and re-layouts  3.93 us (3%)
  between operations  1.3 us (1%)
    pallas_call x1, Pallas kernels, on_device(): pl.pallas_call(kernel, out_shape=(jax.ShapeDtypeStruct((3, 32, 16, 128),...  111 us
    unnamed x7, local copies, waits for them, and re-layouts  3.93 us

profile of v2, /device:TPU:1, one launch (start us, length us, event | category | flops | bytes accessed | tf_op | source)
XLA Modules:
  0.0 116.7 jit_solution(3063792604443451724)
XLA Ops:
  1.3 111.5 %shard_map.175 = (f32[3,32,16,128]{3,2,1,0:T(8,128)}, f32[3,32,16,128]{3,2,1,0:T(8,128)}, f32[32,16,128]{2,1,0:T(8,128)}) custom-call(f32[3,32,16,128]{3,2,1,0:T(8,128)} %velocity.1, f32[3,32,16,128]{3,2,1,0:T(8,128)} %adjoint_seed.1, f32[32,16,128]{2,1,0:T(8,128)} %suscept.1, f32[32,16,128]{2,1,0:T(8,128)} %remanence.1, s32[2,3]{1,0:T(2,128)} %bounds.1, ...), custom_call_target="tpu_custom_call" | custom-call | tf_op jit(solution)/shard_map/pallas_call | solution.py:570
  112.8 0.0 copy-start
  112.8 2.1 %copy.23 = f32[3,32,16,128]{3,2,1,0:T(8,128)} copy(f32[3,32,16,128]{3,2,1,0:T(8,128)} %get-tuple-element.6) | data formatting | bytes 1572864
  114.9 0.0 copy-done
  114.9 0.0 copy-start.1
  114.9 0.9 copy.24
  115.8 0.2 copy-done.1
  116.0 0.7 copy.25
Async XLA Ops:
  112.8 2.1 %copy-start = (f32[3,32,16,128]{3,2,1,0:T(8,128)S(1)}, f32[3,32,16,128]{3,2,1,0:T(8,128)}, u32[]{:S(2)}) copy-start(f32[3,32,16,128]{3,2,1,0:T(8,128)} %get-tuple-element.7) | copy-start | bytes 2359300
  114.9 1.1 copy-start.1

commit v3 on v2

--- a/solution.py
+++ b/solution.py
@@ -20,17 +20,21 @@
     matrix = np.asarray(matrix, np.float32)
     high = matrix.astype(jnp.bfloat16)
     low = (matrix - high.astype(np.float32)).astype(jnp.bfloat16)
-    return np.concatenate([high, high, low], axis=-1)
-
-
-def cut(value, axis):
+    return np.stack([high, low])
+
+
+def cut(value):
     high = value.astype(bf16)
-    low = (value - high.astype(f32)).astype(bf16)
-    return jnp.concatenate([high, low, high], axis=axis)
+    return high, (value - high.astype(f32)).astype(bf16)
+
+
+def product(matrix, value, dims=(((1,), (0,)), ((), ()))):
+    dot = lambda a, b: lax.dot_general(a, b, dims, preferred_element_type=f32)
+    return dot(matrix[0], value[0]) + dot(matrix[0], value[1]) + dot(matrix[1], value[0])
 
 
 def mul(matrix, value):
-    return jnp.dot(matrix, cut(value, 0), preferred_element_type=f32)
+    return product(matrix, cut(value))
 
 
 def make_tables():
@@ -56,7 +60,6 @@
     lower = np.einsum("abqtk,ji->akitqbj", turned[:, :, :4], eye8).reshape(256, 128)
     back = np.stack([np.stack([c, -s]), np.stack([s, c])])
     inverse_x = np.einsum("abqtk,ij->tqaibkj", back, eye8).reshape(256, 256)
-    lower_back = np.einsum("abqtk,ij->tqaibkj", back[:, :, :4], eye8).reshape(128, 256)
     b = np.arange(16)
     phi = turn * ka[:, None] * b
     twiddle = np.stack([np.cos(phi), np.sin(phi)])[:, :, None, :, None]
@@ -68,42 +71,37 @@
     second = np.stack([np.cos(angle), np.sin(angle)])
     return dict(
         forward_z=pieces(forward_z),
-        inverse_z=pieces(np.stack(inverse_z)),
-        forward_x=pieces(forward_x),
+        inverse_z=np.stack([pieces(m) for m in inverse_z]),
+        forward_x=np.stack([pieces(m) for m in forward_x]),
         lower_x=pieces(lower),
         inverse_x=pieces(inverse_x),
-        lower_back=pieces(lower_back),
         twiddle=twiddle.astype(np.float32),
-        kron=pieces(np.stack(kron)),
-        second=pieces(second),
-        second_lower=pieces(second[:, :, :128]),
-    )
-
-
-def rotated(pair, value, direction):
-    value = cut(value, 0)
-    first = jnp.dot(pair[0], value, preferred_element_type=f32)
-    second = jnp.dot(pair[1], value, preferred_element_type=f32)
+        kron=np.stack([pieces(m) for m in kron]),
+        second=np.stack([pieces(m) for m in second]),
+    )
+
+
+def rotated(cosine, sine, value, direction):
+    value = cut(value)
+    first, second = product(cosine, value), product(sine, value)
     real = first[:, :128] - direction * second[:, 128:]
     imag = first[:, 128:] + direction * second[:, :128]
     return real, imag
 
 
 def depth_waves(block, forward_z):
-    return lax.dot_general(
-        forward_z, cut(block, 1), (((1,), (1,)), ((), ())), preferred_element_type=f32
-    )
+    return product(forward_z, cut(block), (((1,), (1,)), ((), ())))
 
 
 def first_forward(mixed, twiddle, kron):
     real, imag = mixed[:128], mixed[128:]
     c, s = twiddle[0], twiddle[1]
     turned = jnp.concatenate([real * c + imag * s, imag * c - real * s], axis=0)
-    return rotated(kron, turned.T, -1.0)
+    return rotated(*kron, turned.T, -1.0)
 
 
 def first_inverse(value, twiddle, kron, inverse_x):
-    real, imag = rotated(kron, value, 1.0)
+    real, imag = rotated(*kron, value, 1.0)
     turned = jnp.concatenate([real, imag], axis=1).T
     real, imag = turned[:128], turned[128:]
     c, s = twiddle[0], twiddle[1]
@@ -144,6 +142,9 @@
     return jnp.concatenate([value, value], axis=1)
 
 
+UNROLL = 5
+
+
 class Place:
     def __init__(self):
         self.gx, self.gy, self.gz = (lax.axis_index(a) for a in ("gx", "gy", "gz"))
@@ -155,7 +156,7 @@
     def by_second(self, second):
         return (self.gx, second, self.gz)
 
-    def greet(self):
+    def announce(self):
         barrier = pltpu.get_barrier_semaphore()
 
         def signal(step, carry):
@@ -166,8 +167,10 @@
                 pl.semaphore_signal(barrier, inc=1, device_id=target, device_id_type=MESH)
             return carry
 
-        lax.fori_loop(1, 16, signal, 0)
-        pl.semaphore_wait(barrier, 30)
+        lax.fori_loop(1, 16, signal, 0, unroll=UNROLL)
+
+    def meet(self):
+        pl.semaphore_wait(pltpu.get_barrier_semaphore(), 30)
 
 
 class Exchange:
@@ -178,40 +181,43 @@
     def each(self, act):
         def body(step, carry):
             peer = (self.me + step) % 16
-            copy = pltpu.make_async_remote_copy(
-                src_ref=self.src(peer),
-                dst_ref=self.dst,
-                send_sem=self.send_sem(peer),
-                recv_sem=self.recv_sem,
-                device_id=self.device(peer),
-                device_id_type=MESH,
-            )
             if self.wanted is None:
-                act(copy)
+                act(peer)
             else:
-                pl.when(self.wanted(peer))(lambda: act(copy))
+                pl.when(self.wanted(peer))(lambda: act(peer))
             return carry
 
-        lax.fori_loop(1, 16, body, 0)
-
-    def start(self):
-        self.each(lambda copy: copy.start())
+        lax.fori_loop(1, 16, body, 0, unroll=UNROLL)
+
+    def copy(self, peer):
+        return pltpu.make_async_remote_copy(
+            src_ref=self.src(peer),
+            dst_ref=self.dst,
+            send_sem=self.send_sem(peer),
+            recv_sem=self.recv_sem,
+            device_id=self.device(peer),
+            device_id_type=MESH,
+        )
+
+    def start(self, after=None):
+        def act(peer):
+            if after is not None:
+                after.copy(peer).wait_send()
+            self.copy(peer).start()
+
         own = pltpu.make_async_copy(self.src(self.me), self.dst, self.recv_sem)
         if self.wanted is None:
             own.start()
         else:
             pl.when(self.wanted(self.me))(lambda: own.start())
+        self.each(act)
 
     def finish(self):
-        self.each(lambda copy: copy.wait_send())
-
-
-def arrived(count, block, sem, skip=None):
-    def wait(step, carry):
-        pltpu.make_async_copy(block(step), block(step), sem(step)).wait()
-        return carry
-
-    lax.fori_loop(0, count, wait, 0)
+        self.each(lambda peer: self.copy(peer).wait_send())
+
+
+def arrived(buffer, sem):
+    pltpu.make_async_copy(buffer, buffer, sem).wait()
 
 
 def region(at, bounds):
@@ -222,6 +228,20 @@
     inside = inside & (second >= bounds[0, 1]) & (second < bounds[1, 1])
     inside = inside & (third >= bounds[0, 2]) & (third < bounds[1, 2])
     return jnp.where(inside, 1.0, 0.0)
+
+
+def parts(ref):
+    return ref.at[0], ref.at[1]
+
+
+def lower(ref, axis):
+    if axis == 0:
+        return ref[0, :, :128], ref[1, :, :128]
+    return ref[0, :, :, :128], ref[1, :, :, :128]
+
+
+def lower_rows(ref):
+    return jnp.concatenate([ref[:, 0:64], ref[:, 128:192]], axis=1)
 
 
 class Halo:
@@ -360,8 +380,7 @@
 
 def kernel(
     velocity, adjoint_seed, suscept, remanence, bounds, step,
-    forward_z, inverse_z, forward_x, lower_x, inverse_x, lower_back, twiddle, kron, second,
-    second_lower,
+    forward_z, inverse_z, forward_x, lower_x, inverse_x, twiddle, kron, second,
     next_out, adjoint_out, gradient_out,
     z_out, z_in, k_out, k_in, y_out, y_in, x_out, x_in,
     zb_out, zb_in, kb_out, kb_in, yb_out, yb_in, xb_out, xb_in,
@@ -372,53 +391,53 @@
     cells_sent, cells_got, energy_sent, energy_got,
 ):
     at = Place()
-    at.greet()
+    at.announce()
     in_lower = (at.gx < 4) & (at.gy < 8) & (at.gz == 0)
     has_rows = at.gy < 8
 
     depths = Exchange(
         at.wave, at.by_wave, lambda p: z_out.at[p], z_in.at[at.gx % 4],
-        lambda p: z_sent.at[p], z_got.at[at.gx % 4],
+        lambda p: z_sent.at[p], z_got,
     )
     firsts = Exchange(
         at.gy, at.by_second, lambda p: k_out.at[p], k_in.at[at.gy % 8],
-        lambda p: k_sent.at[p], k_got.at[at.gy % 8],
+        lambda p: k_sent.at[p], k_got,
     )
     seconds = [
         Exchange(
             at.gy, at.by_second, lambda p, f=f: y_out.at[f, p], y_in.at[f, at.gy],
-            lambda p, f=f: y_sent.at[f, p], y_got.at[f, at.gy],
+            lambda p, f=f: y_sent.at[f, p], y_got.at[f],
         )
         for f in range(2)
     ]
     lasts = [
         Exchange(
             at.wave, at.by_wave, lambda p, f=f: x_out.at[f, p // 2], x_in.at[f, at.wave],
-            lambda p, f=f: x_sent.at[f, p], x_got.at[f, at.wave],
+            lambda p, f=f: x_sent.at[f, p], x_got.at[f],
         )
         for f in range(3)
     ]
     depths_back = [
         Exchange(
             at.wave, at.by_wave, lambda p, f=f: zb_out.at[f, p], zb_in.at[f, at.wave],
-            lambda p, f=f: zb_sent.at[f, p], zb_got.at[f, at.wave],
+            lambda p, f=f: zb_sent.at[f, p], zb_got.at[f],
         )
         for f in range(3)
     ]
     firsts_back = [
         Exchange(
             at.gy, at.by_second, lambda p, f=f: kb_out.at[f, p], kb_in.at[f, at.gy],
-            lambda p, f=f: kb_sent.at[f, p], kb_got.at[f, at.gy],
+            lambda p, f=f: kb_sent.at[f, p], kb_got.at[f],
         )
         for f in range(2)
     ]
     seconds_back = Exchange(
         at.gy, at.by_second, lambda p: yb_out.at[p % 8], yb_in.at[at.gy],
-        lambda p: yb_sent.at[p], yb_got.at[at.gy], lambda p: p < 8,
+        lambda p: yb_sent.at[p], yb_got, lambda p: p < 8,
     )
     lasts_back = Exchange(
         at.wave, at.by_wave, lambda p: xb_out.at[p // 2 % 4], xb_in.at[at.wave],
-        lambda p: xb_sent.at[p], xb_got.at[at.wave], lambda p: (p < 8) & (p % 2 == 0),
+        lambda p: xb_sent.at[p], xb_got, lambda p: (p < 8) & (p % 2 == 0),
     )
     cell_halo = Halo(
         at, cells, cells_y_out, cells_y_in, cells_z_out, cells_z_in, cells_sent, cells_got
@@ -430,8 +449,10 @@
     @pl.when(in_lower)
     def _():
         magnet = remanence[...].reshape(512, 128) * region(at, bounds)
-        z_out[...] = depth_waves(magnet, forward_z[...]).reshape(16, 16, 512)
-        depths.start()
+        z_out[...] = depth_waves(magnet, forward_z).reshape(16, 16, 512)
+
+    at.meet()
+    pl.when(in_lower)(lambda: depths.start())
 
     cells[0:3, 1:33] = velocity[...]
     cells[3:6, 1:33] = adjoint_seed[...]
@@ -440,10 +461,10 @@
 
     @pl.when(has_rows)
     def _():
-        arrived(4, lambda i: z_in.at[i], lambda i: z_got.at[i])
+        arrived(z_in, z_got)
         block = z_in[...].reshape(64, 512)
         block = jnp.concatenate([block[:, :256], block[:, 256:]], axis=0)
-        real, imag = first_forward(mul(lower_x[...], block), twiddle[...], kron[...])
+        real, imag = first_forward(mul(lower_x, block), twiddle, parts(kron))
         k_out[...] = jnp.concatenate([real, imag], axis=1).reshape(16, 16, 256)
         firsts.start()
 
@@ -451,52 +472,54 @@
     cell_rows(at, cell_halo, cells_wide, next_out, adjoint_out, source)
 
     potential, second_factor = spectral_factors(at.wave, at.gy)
-    arrived(8, lambda i: k_in.at[i], lambda i: k_got.at[i])
-    real, imag = rotated(second_lower[...], k_in[...].reshape(128, 256), -1.0)
+    arrived(k_in, k_got)
+    real, imag = rotated(*lower(second, 1), k_in[...].reshape(128, 256), -1.0)
     value = jnp.concatenate([real * potential, imag * potential], axis=1)
     for f in range(2):
         if f == 1:
             value = value * twice(second_factor)
-        real, imag = rotated(second[...], value, 1.0)
+        real, imag = rotated(*parts(second), value, 1.0)
         y_out[f] = jnp.concatenate([real, imag], axis=1).reshape(16, 16, 256)
-        seconds[f].start()
+        seconds[f].start(seconds[0] if f == 1 else None)
 
     first_factor, third_factor = mixing_factors(at.wave)
 
-    def send_first(f, value):
-        value = first_inverse(value, twiddle[...], kron[...], inverse_x[...])
+    def send_first(f, value, after=None):
+        value = first_inverse(value, twiddle, parts(kron), inverse_x)
         x_out[f, :, :, :256] = value[:128].reshape(8, 16, 256)
         x_out[f, :, :, 256:] = value[128:].reshape(8, 16, 256)
-        lasts[f].start()
-
-    arrived(16, lambda i: y_in.at[0, i], lambda i: y_got.at[0, i])
+        lasts[f].start(after)
+
+    arrived(y_in.at[0], y_got.at[0])
     value = y_in[0].reshape(256, 256)
     send_first(0, value * twice(first_factor))
-    send_first(2, value * twice(third_factor))
-    arrived(16, lambda i: y_in.at[1, i], lambda i: y_got.at[1, i])
-    send_first(1, y_in[1].reshape(256, 256))
+    send_first(2, value * twice(third_factor), lasts[0])
+    arrived(y_in.at[1], y_got.at[1])
+    send_first(1, y_in[1].reshape(256, 256), lasts[2])
 
     turned = jnp.full((8, 128), step[0] % field_period, jnp.int32).astype(f32)
     turned = full_turn * turned / field_period
     applied = (jnp.cos(turned)[:1], jnp.sin(turned)[:1], None)
     square = jnp.zeros((512, 128), f32)
     weight = source[...].reshape(512, 128)
+    before = None
     for f in ORDER:
-        arrived(16, lambda i, f=f: x_in.at[f, i], lambda i, f=f: x_got.at[f, i])
-        field = mul(inverse_z[at.gz], x_in[f].reshape(256, 512)).T
+        arrived(x_in.at[f], x_got.at[f])
+        field = mul(inverse_z.at[at.gz], x_in[f].reshape(256, 512)).T
         if applied[f] is not None:
             field = field + applied[f]
         square = square + field * field
-        zb_out[f] = depth_waves(weight * field, forward_z[...]).reshape(16, 16, 512)
-        depths_back[f].start()
+        zb_out[f] = depth_waves(weight * field, forward_z).reshape(16, 16, 512)
+        depths_back[f].start(before)
+        before = depths_back[f]
     energy[0, 1:33] = (0.5 * square).reshape(32, 16, 128)
     energy_halo.start()
 
     def first_of(f):
-        arrived(16, lambda i: zb_in.at[f, i], lambda i: zb_got.at[f, i])
+        arrived(zb_in.at[f], zb_got.at[f])
         block = zb_in[f].reshape(256, 512)
-        mixed = mul(forward_x[0], block[:, :256]) + mul(forward_x[1], block[:, 256:])
-        real, imag = first_forward(mixed, twiddle[...], kron[...])
+        mixed = mul(forward_x.at[0], block[:, :256]) + mul(forward_x.at[1], block[:, 256:])
+        real, imag = first_forward(mixed, twiddle, parts(kron))
         return jnp.concatenate([real, imag], axis=1)
 
     value = first_of(0) * twice(first_factor)
@@ -504,51 +527,50 @@
     kb_out[0] = value.reshape(16, 16, 256)
     firsts_back[0].start()
     kb_out[1] = first_of(1).reshape(16, 16, 256)
-    firsts_back[1].start()
+    firsts_back[1].start(firsts_back[0])
 
     energy_halo.arrive(energy_wide)
     energy_rows(at, energy_halo, energy_wide, suscept, next_out)
+    pl.when(in_lower)(lambda: depths.finish())
+    pl.when(has_rows)(lambda: firsts.finish())
+    for each in (seconds[1], lasts[1], depths_back[1], cell_halo, energy_halo):
+        each.finish()
 
     def second_of(f):
-        arrived(16, lambda i: kb_in.at[f, i], lambda i: kb_got.at[f, i])
-        real, imag = rotated(second[...], kb_in[f].reshape(256, 256), -1.0)
+        arrived(kb_in.at[f], kb_got.at[f])
+        real, imag = rotated(*parts(second), kb_in[f].reshape(256, 256), -1.0)
         return jnp.concatenate([real, imag], axis=1)
 
     value = second_of(0)
     value = (value + second_of(1) * twice(second_factor)) * twice(potential)
-    real, imag = rotated(second[:, :128], value, 1.0)
+    real, imag = rotated(*lower(second, 0), value, 1.0)
     yb_out[...] = jnp.concatenate([real, imag], axis=1).reshape(8, 16, 256)
     seconds_back.start()
+    firsts_back[1].finish()
+    gradient_out[...] = jnp.zeros((32, 16, 128), f32)
 
     @pl.when(has_rows)
     def _():
-        arrived(16, lambda i: yb_in.at[i], lambda i: yb_got.at[i])
+        arrived(yb_in, yb_got)
         value = yb_in[...].reshape(256, 256)
-        value = first_inverse(value, twiddle[...], kron[...], lower_back[...])
+        value = first_inverse(value, twiddle, parts(kron), lower_rows(inverse_x))
         xb_out[:, :, :256] = value[:64].reshape(4, 16, 256)
         xb_out[:, :, 256:] = value[64:].reshape(4, 16, 256)
         lasts_back.start()
 
-    gradient_out[...] = jnp.zeros((32, 16, 128), f32)
-
     @pl.when(in_lower)
     def _():
-        arrived(16, lambda i: xb_in.at[i], lambda i: xb_got.at[i])
-        value = mul(inverse_z[0], xb_in[...].reshape(256, 512)).T
+        arrived(xb_in, xb_got)
+        value = mul(inverse_z.at[0], xb_in[...].reshape(256, 512)).T
         gradient_out[...] = (value * region(at, bounds)).reshape(32, 16, 128)
 
-    pl.when(in_lower)(lambda: depths.finish())
-    pl.when(has_rows)(lambda: firsts.finish())
-    for each in seconds + lasts + depths_back + firsts_back + [seconds_back]:
-        each.finish()
+    seconds_back.finish()
     pl.when(has_rows)(lambda: lasts_back.finish())
-    cell_halo.finish()
-    energy_halo.finish()
 
 
 TABLES = (
-    "forward_z", "inverse_z", "forward_x", "lower_x", "inverse_x", "lower_back", "twiddle",
-    "kron", "second", "second_lower",
+    "forward_z", "inverse_z", "forward_x", "lower_x", "inverse_x", "twiddle",
+    "kron", "second",
 )
 
 
@@ -562,8 +584,8 @@
         shapes += [(n, 34, 16, 128), (2, n, 32, 128), (2, n, 32, 128), (8, 512), (8, 512)]
         shapes += [(n, 32, 16, 128)]
     shapes += [(32, 16, 128)]
-    sems = [(16,), (4,), (16,), (8,), (2, 16), (2, 16), (3, 16), (3, 16)]
-    sems += [(3, 16), (3, 16), (2, 16), (2, 16), (16,), (16,), (16,), (16,)]
+    sems = [(16,), (), (16,), (), (2, 16), (2,), (3, 16), (3,)]
+    sems += [(3, 16), (3,), (2, 16), (2,), (16,), (), (16,), ()]
     sems += [(5,)] * 4
     vmem = pl.BlockSpec(memory_space=pltpu.VMEM)
     smem = pl.BlockSpec(memory_space=pltpu.SMEM)
@@ -579,7 +601,7 @@
         scratch_shapes=[pltpu.VMEM(s, f32) for s in shapes]
         + [pltpu.SemaphoreType.DMA(s) for s in sems],
         compiler_params=pltpu.CompilerParams(
-            collective_id=0, has_side_effects=True, vmem_limit_bytes=60 << 20
+            collective_id=0, has_side_effects=True, vmem_limit_bytes=24 << 20
         ),
     )(
         velocity, adjoint_seed, susceptibility, remanence, region_bounds, step_id,

time: 117 us -> 122 us (1.043); the launches traced: 117 us -> 120 us
  local copies, waits for them, and re-layouts: 3.93 us -> 14.4 us
  Pallas kernels: 111 us -> 104 us
    unnamed x7 -> x29, local copies, waits for them, and re-layouts: 3.93 us -> 14.4 us
    pallas_call x1, Pallas kernels: 111 us -> 104 us  [on_device(): pl.pallas_call(kernel, out_shape=(jax.ShapeDtypeStruct((3, 32, 16, 128),...]
where the time goes in v3:
time: 122 us; the launch traced here: 120 us
  Pallas kernels  104 us (85%)
  local copies, waits for them, and re-layouts  14.4 us (12%)
  between operations  1.33 us (1%)
    pallas_call x1, Pallas kernels, on_device(): pl.pallas_call(kernel, out_shape=(jax.ShapeDtypeStruct((3, 32, 16, 128),...  104 us
    unnamed x29, local copies, waits for them, and re-layouts  14.4 us

profile of v3, /device:TPU:1, one launch (start us, length us, event | category | flops | bytes accessed | tf_op | source)
XLA Modules:
  0.0 119.6 jit_solution(4631935100994046928)
XLA Ops:
  0.6 0.0 copy-start.12
  1.3 0.0 copy-done.12
  1.3 0.0 copy-start
  1.3 1.1 copy-done
  2.4 0.0 copy-start.1
  2.4 1.1 copy-done.1
  3.6 0.0 copy-start.2
  3.6 1.0 copy-done.2
  4.6 0.0 copy-start.3
  4.6 1.0 copy-done.3
  5.7 0.0 copy-start.4
  5.7 1.0 copy-done.4
  6.7 0.0 copy-start.5
  6.7 0.9 copy-done.5
  7.7 0.9 copy-done.6
  8.6 0.9 copy-done.7
  9.6 0.9 copy-done.8
  10.5 0.9 copy-done.9
  11.5 0.9 copy-done.10
  12.4 0.9 copy-done.11
  13.3 103.9 %shard_map.157 = (f32[3,32,16,128]{3,2,1,0:T(8,128)S(1)}, f32[3,32,16,128]{3,2,1,0:T(8,128)S(1)}, f32[32,16,128]{2,1,0:T(8,128)S(1)}) custom-call(f32[3,32,16,128]{3,2,1,0:T(8,128)S(1)} %copy-done, f32[3,32,16,128]{3,2,1,0:T(8,128)S(1)} %copy-done.1, f32[32,16,128]{2,1,0:T(8,128)S(1)} %copy-done.5, f32[32,16,128]{2,1,0:T(8,128)S(1)} %copy-done.6, ...), custom_call_target="tpu_custom_call" | custom-call | tf_op jit(solution)/shard_map/pallas_call | solution.py:592
  117.1 0.9 copy.21
  118.0 0.9 copy.22
  118.9 0.7 copy.23
  (6 shorter events, 0.0 us)
Async XLA Ops:
  0.6 0.7 copy-start.12
  1.3 1.1 copy-start
  2.4 1.1 copy-start.1
  3.6 1.0 copy-start.2
  4.6 1.0 copy-start.3
  5.7 1.0 copy-start.4
  6.7 0.9 copy-start.5
  7.7 0.9 copy-start.6
  8.6 0.9 copy-start.7
  9.6 0.9 copy-start.8
  10.5 0.9 copy-start.9
  11.5 0.9 copy-start.10
  12.4 0.9 copy-start.11

commit v4 on v3

--- a/solution.py
+++ b/solution.py
@@ -364,10 +364,10 @@
     lax.fori_loop(0, 32, body, 0)
 
 
-def energy_rows(at, halo, wide, suscept, next_out):
+def energy_rows(at, halo, wide, cells, next_out):
     def body(i, carry):
         _, around = neighbours(at, halo, wide, 0, i)
-        scaled = time_step * suscept[i]
+        scaled = time_step * cells[6, i + 1]
         for k in range(3):
             next_out[k, i] = next_out[k, i] + scaled * slope(around[k])
         return carry
@@ -379,8 +379,9 @@
 
 
 def kernel(
-    velocity, adjoint_seed, suscept, remanence, bounds, step,
-    forward_z, inverse_z, forward_x, lower_x, inverse_x, twiddle, kron, second,
+    velocity, adjoint_seed, suscept, remanence_in,
+    forward_z_in, inverse_z_in, forward_x_in, lower_x_in, inverse_x_in, twiddle_in, kron_in,
+    second_in, bounds, step,
     next_out, adjoint_out, gradient_out,
     z_out, z_in, k_out, k_in, y_out, y_in, x_out, x_in,
     zb_out, zb_in, kb_out, kb_in, yb_out, yb_in, xb_out, xb_in,
@@ -389,9 +390,29 @@
     z_sent, z_got, k_sent, k_got, y_sent, y_got, x_sent, x_got,
     zb_sent, zb_got, kb_sent, kb_got, yb_sent, yb_got, xb_sent, xb_got,
     cells_sent, cells_got, energy_sent, energy_got,
+    remanence, forward_z, inverse_z, forward_x, lower_x, inverse_x, twiddle, kron, second, loaded,
 ):
     at = Place()
     at.announce()
+    loads = {}
+    for number, (name, src, dst) in enumerate(
+        (
+            ("remanence", remanence_in, remanence),
+            ("forward_z", forward_z_in, forward_z),
+            ("velocity", velocity, cells.at[0:3, 1:33]),
+            ("seed", adjoint_seed, cells.at[3:6, 1:33]),
+            ("suscept", suscept, cells.at[6, 1:33]),
+            ("lower_x", lower_x_in, lower_x),
+            ("twiddle", twiddle_in, twiddle),
+            ("kron", kron_in, kron),
+            ("second", second_in, second),
+            ("inverse_x", inverse_x_in, inverse_x),
+            ("inverse_z", inverse_z_in, inverse_z),
+            ("forward_x", forward_x_in, forward_x),
+        )
+    ):
+        loads[name] = pltpu.make_async_copy(src, dst, loaded.at[number])
+        loads[name].start()
     in_lower = (at.gx < 4) & (at.gy < 8) & (at.gz == 0)
     has_rows = at.gy < 8
 
@@ -446,6 +467,8 @@
         at, energy, energy_y_out, energy_y_in, energy_z_out, energy_z_in, energy_sent, energy_got
     )
 
+    loads["remanence"].wait()
+    loads["forward_z"].wait()
     @pl.when(in_lower)
     def _():
         magnet = remanence[...].reshape(512, 128) * region(at, bounds)
@@ -454,11 +477,13 @@
     at.meet()
     pl.when(in_lower)(lambda: depths.start())
 
-    cells[0:3, 1:33] = velocity[...]
-    cells[3:6, 1:33] = adjoint_seed[...]
-    cells[6, 1:33] = suscept[...]
+    for name in ("velocity", "seed", "suscept"):
+        loads[name].wait()
     cell_halo.start()
 
+    loads["lower_x"].wait()
+    loads["twiddle"].wait()
+    loads["kron"].wait()
     @pl.when(has_rows)
     def _():
         arrived(z_in, z_got)
@@ -471,6 +496,7 @@
     cell_halo.arrive(cells_wide)
     cell_rows(at, cell_halo, cells_wide, next_out, adjoint_out, source)
 
+    loads["second"].wait()
     potential, second_factor = spectral_factors(at.wave, at.gy)
     arrived(k_in, k_got)
     real, imag = rotated(*lower(second, 1), k_in[...].reshape(128, 256), -1.0)
@@ -482,6 +508,7 @@
         y_out[f] = jnp.concatenate([real, imag], axis=1).reshape(16, 16, 256)
         seconds[f].start(seconds[0] if f == 1 else None)
 
+    loads["inverse_x"].wait()
     first_factor, third_factor = mixing_factors(at.wave)
 
     def send_first(f, value, after=None):
@@ -497,6 +524,7 @@
     arrived(y_in.at[1], y_got.at[1])
     send_first(1, y_in[1].reshape(256, 256), lasts[2])
 
+    loads["inverse_z"].wait()
     turned = jnp.full((8, 128), step[0] % field_period, jnp.int32).astype(f32)
     turned = full_turn * turned / field_period
     applied = (jnp.cos(turned)[:1], jnp.sin(turned)[:1], None)
@@ -515,6 +543,7 @@
     energy[0, 1:33] = (0.5 * square).reshape(32, 16, 128)
     energy_halo.start()
 
+    loads["forward_x"].wait()
     def first_of(f):
         arrived(zb_in.at[f], zb_got.at[f])
         block = zb_in[f].reshape(256, 512)
@@ -530,7 +559,7 @@
     firsts_back[1].start(firsts_back[0])
 
     energy_halo.arrive(energy_wide)
-    energy_rows(at, energy_halo, energy_wide, suscept, next_out)
+    energy_rows(at, energy_halo, energy_wide, cells, next_out)
     pl.when(in_lower)(lambda: depths.finish())
     pl.when(has_rows)(lambda: firsts.finish())
     for each in (seconds[1], lasts[1], depths_back[1], cell_halo, energy_halo):
@@ -568,6 +597,7 @@
     pl.when(has_rows)(lambda: lasts_back.finish())
 
 
+VMEM_GRANT = 24 << 20
 TABLES = (
     "forward_z", "inverse_z", "forward_x", "lower_x", "inverse_x", "twiddle",
     "kron", "second",
@@ -589,6 +619,12 @@
     sems += [(5,)] * 4
     vmem = pl.BlockSpec(memory_space=pltpu.VMEM)
     smem = pl.BlockSpec(memory_space=pltpu.SMEM)
+    hbm = pl.BlockSpec(memory_space=pltpu.HBM)
+    held = [pltpu.VMEM((32, 16, 128), f32)]
+    held += [pltpu.VMEM(tables[n].shape, tables[n].dtype) for n in TABLES]
+    operands = [velocity, adjoint_seed, susceptibility, remanence]
+    operands += [jnp.asarray(tables[n]) for n in TABLES]
+    operands = [pltpu.with_memory_space_constraint(x, pltpu.HBM) for x in operands]
     return pl.pallas_call(
         kernel,
         out_shape=(
@@ -596,17 +632,16 @@
             jax.ShapeDtypeStruct((3, 32, 16, 128), f32),
             jax.ShapeDtypeStruct((32, 16, 128), f32),
         ),
-        in_specs=[vmem] * 4 + [smem] * 2 + [vmem] * len(TABLES),
+        in_specs=[hbm] * (4 + len(TABLES)) + [smem] * 2,
         out_specs=(vmem, vmem, vmem),
         scratch_shapes=[pltpu.VMEM(s, f32) for s in shapes]
-        + [pltpu.SemaphoreType.DMA(s) for s in sems],
+        + [pltpu.SemaphoreType.DMA(s) for s in sems]
+        + held
+        + [pltpu.SemaphoreType.DMA((12,))],
         compiler_params=pltpu.CompilerParams(
-            collective_id=0, has_side_effects=True, vmem_limit_bytes=24 << 20
+            collective_id=0, has_side_effects=True, vmem_limit_bytes=VMEM_GRANT
         ),
-    )(
-        velocity, adjoint_seed, susceptibility, remanence, region_bounds, step_id,
-        *[tables[n] for n in TABLES],
-    )
+    )(*operands, region_bounds, step_id)
 
 
 def solution(mesh):

time: 122 us -> 109 us (0.89)
  local copies, waits for them, and re-layouts: 14.4 us -> 2.48 us
    unnamed x29 -> x5, local copies, waits for them, and re-layouts: 14.4 us -> 2.48 us
where the time goes in v4:
time: 109 us; the launch traced here: 107 us
  Pallas kernels  104 us (95%)
  local copies, waits for them, and re-layouts  2.48 us (2%)
  between operations  1.31 us (1%)
    pallas_call x1, Pallas kernels, on_device(): pl.pallas_call(kernel, out_shape=(jax.ShapeDtypeStruct((3, 32, 16, 128),...  104 us
    unnamed x5, local copies, waits for them, and re-layouts  2.48 us

profile of v4, /device:TPU:1, one launch (start us, length us, event | category | flops | bytes accessed | tf_op | source)
XLA Modules:
  0.0 107.5 jit_solution(2460910903242831473)
XLA Ops:
  0.6 0.0 copy-start
  1.3 0.0 copy-done
  1.3 103.7 %shard_map.157 = (f32[3,32,16,128]{3,2,1,0:T(8,128)S(1)}, f32[3,32,16,128]{3,2,1,0:T(8,128)S(1)}, f32[32,16,128]{2,1,0:T(8,128)S(1)}) custom-call(f32[3,32,16,128]{3,2,1,0:T(8,128)} %velocity.1, f32[3,32,16,128]{3,2,1,0:T(8,128)} %adjoint_seed.1, f32[32,16,128]{2,1,0:T(8,128)} %suscept.1, f32[32,16,128]{2,1,0:T(8,128)} %remanence_in.1, ...), custom_call_target="tpu_custom_call" | custom-call | tf_op jit(solution)/shard_map/pallas_call | solution.py:628
  105.0 0.9 copy.21
  105.9 0.9 copy.22
  106.8 0.7 copy.23
Async XLA Ops:
  0.6 0.7 copy-start

commit v5 on v4

--- a/solution.py
+++ b/solution.py
@@ -39,76 +39,94 @@
 
 def make_tables():
     turn = 2.0 * np.pi / 256
-    eye8, eye16 = np.eye(8), np.eye(16)
-    k3 = 1 + 8 * np.arange(16)[:, None] + np.arange(8)[None, :]
+    eye4, eye16 = np.eye(4), np.eye(16)
+    c, s, j = np.arange(2)[:, None, None], np.arange(16)[:, None], np.arange(4)
+    k3 = 1 + 8 * s + 4 * c + j
     z = np.arange(128)
-    phase = turn * k3[:, :, None] * z
-    forward_z = np.stack([np.cos(phase), -np.sin(phase)], 1).reshape(256, 128)
-    weight = np.where(k3 == 128, 1.0, 2.0)[:, :, None] / 256.0**3
+    phase = turn * k3[..., None] * z
+    forward_z = np.stack([np.cos(phase), -np.sin(phase)], 2).reshape(256, 128)
+    weight = np.where(k3 == 128, 1.0, 2.0)[..., None] / 256.0**3
     inverse_z = []
     for part in range(2):
-        phase = turn * k3[:, :, None] * (z + 128 * part)
-        both = np.stack([np.cos(phase) * weight, -np.sin(phase) * weight], 1)
+        phase = turn * k3[..., None] * (z + 128 * part)
+        both = np.stack([np.cos(phase) * weight, -np.sin(phase) * weight], 2)
         inverse_z.append(both.reshape(256, 128).T)
     q, t, ka = np.arange(8), np.arange(2), np.arange(16)
     theta = turn * 16 * (2 * q[:, None, None] + t[None, :, None]) * ka
     c, s = np.cos(theta), np.sin(theta)
     turned = np.stack([np.stack([c, s]), np.stack([-s, c])])
-    sign = np.stack([np.ones(8), (-1.0) ** (1 + np.arange(8))])
-    forward_x = np.einsum("abqtk,gj,ji->takiqgbj", turned, sign, eye8)
-    forward_x = forward_x.reshape(2, 256, 256)
-    lower = np.einsum("abqtk,ji->akitqbj", turned[:, :, :4], eye8).reshape(256, 128)
+    sign = np.stack([np.ones(4), (-1.0) ** (1 + j)])
+    forward_x = np.einsum("abqtk,gj,ji->akitqgbj", turned, sign, eye4).reshape(128, 256)
+    lower_x = np.einsum("abqtk,ji->akitqbj", turned[:, :, :4], eye4).reshape(128, 64)
     back = np.stack([np.stack([c, -s]), np.stack([s, c])])
-    inverse_x = np.einsum("abqtk,ij->tqaibkj", back, eye8).reshape(256, 256)
+    inverse_x = np.einsum("abqtk,ij->tqaibkj", back, eye4).reshape(128, 128)
     b = np.arange(16)
     phi = turn * ka[:, None] * b
     twiddle = np.stack([np.cos(phi), np.sin(phi)])[:, :, None, :, None]
-    twiddle = np.broadcast_to(twiddle, (2, 16, 8, 16, 16)).reshape(2, 128, 256)
+    twiddle = np.broadcast_to(twiddle, (2, 16, 4, 16, 16)).reshape(2, 64, 256)
     angle = turn * 16 * b[:, None] * b
-    kron = [np.kron(np.cos(angle), eye16), np.kron(np.sin(angle), eye16)]
+    kron = np.concatenate([np.kron(np.cos(angle), eye16), np.kron(np.sin(angle), eye16)], 1)
     k = np.arange(256)
     angle = turn * (k[:, None] * k % 256)
-    second = np.stack([np.cos(angle), np.sin(angle)])
     return dict(
         forward_z=pieces(forward_z),
         inverse_z=np.stack([pieces(m) for m in inverse_z]),
-        forward_x=np.stack([pieces(m) for m in forward_x]),
-        lower_x=pieces(lower),
+        forward_x=pieces(forward_x),
+        lower_x=pieces(lower_x),
         inverse_x=pieces(inverse_x),
         twiddle=twiddle.astype(np.float32),
-        kron=np.stack([pieces(m) for m in kron]),
-        second=np.stack([pieces(m) for m in second]),
-    )
+        kron=pieces(kron),
+        second=np.stack([pieces(np.cos(angle)), pieces(np.sin(angle))]),
+    )
+
+
+def half_turned(value):
+    return pltpu.roll(value, 64, 1)
 
 
 def rotated(cosine, sine, value, direction):
     value = cut(value)
     first, second = product(cosine, value), product(sine, value)
-    real = first[:, :128] - direction * second[:, 128:]
-    imag = first[:, 128:] + direction * second[:, :128]
-    return real, imag
+    lane = lax.broadcasted_iota(jnp.int32, (first.shape[0], 128), 1)
+    sign = jnp.where(lane < 64, -direction, direction)
+    blocks = [
+        first[:, at : at + 128] + sign * half_turned(second[:, at : at + 128])
+        for at in range(0, first.shape[1], 128)
+    ]
+    return blocks[0] if len(blocks) == 1 else jnp.concatenate(blocks, axis=1)
 
 
 def depth_waves(block, forward_z):
     return product(forward_z, cut(block), (((1,), (1,)), ((), ())))
 
 
+def sixteenths(value, kron, direction):
+    both = product(cut(value), kron)
+    first, second = both[:, :256], both[:, 256:]
+    return jnp.concatenate(
+        [first[:64] - direction * second[64:], first[64:] + direction * second[:64]], axis=0
+    )
+
+
 def first_forward(mixed, twiddle, kron):
-    real, imag = mixed[:128], mixed[128:]
+    real, imag = mixed[:64], mixed[64:]
     c, s = twiddle[0], twiddle[1]
     turned = jnp.concatenate([real * c + imag * s, imag * c - real * s], axis=0)
-    return rotated(*kron, turned.T, -1.0)
+    return sixteenths(turned, kron, -1.0).T
 
 
 def first_inverse(value, twiddle, kron, inverse_x):
-    real, imag = rotated(*kron, value, 1.0)
-    turned = jnp.concatenate([real, imag], axis=1).T
-    real, imag = turned[:128], turned[128:]
+    turned = sixteenths(value.T, kron, 1.0)
+    real, imag = turned[:64], turned[64:]
     c, s = twiddle[0], twiddle[1]
     turned = jnp.concatenate([real * c - imag * s, imag * c + real * s], axis=0)
     return mul(inverse_x, turned)
 
 
+def halves_on_rows(block):
+    return jnp.concatenate([block[:, :256], block[:, 256:]], axis=0)
+
+
 def signed_wave(index):
     folded = jnp.where(index < 128, index, index - 256)
     return jnp.where(index == 128, 0, folded).astype(f32) * (full_turn / 256)
@@ -119,11 +137,15 @@
     return jnp.where(third == 128, jnp.where(index == 128, half, 0.0), signed_wave(index))
 
 
-def spectral_factors(place, gy):
+def wave_numbers(place, chunk):
     row = lax.broadcasted_iota(jnp.int32, (256, 128), 0)
     lane = lax.broadcasted_iota(jnp.int32, (256, 128), 1)
-    third = 1 + 8 * place + lane % 8
-    first = lane // 8 + 16 * gy
+    return row, lane % 64 // 4, 1 + 8 * place + 4 * chunk + lane % 4
+
+
+def spectral_factors(place, gy, chunk):
+    row, low, third = wave_numbers(place, chunk)
+    first = low + 16 * gy
     third_wave = third.astype(f32) * (full_turn / 256)
     fold = lambda i: jnp.where(i < 128, i, i - 256).astype(f32) * (full_turn / 256)
     first_wave, second_wave = fold(first), fold(row)
@@ -131,18 +153,13 @@
     return -third_wave / square, factor_of(row, third)
 
 
-def mixing_factors(place):
-    row = lax.broadcasted_iota(jnp.int32, (256, 128), 0)
-    lane = lax.broadcasted_iota(jnp.int32, (256, 128), 1)
-    third = 1 + 8 * place + lane % 8
-    return factor_of(lane // 8 + 16 * (row // 16), third), third.astype(f32) * (full_turn / 256)
-
-
-def twice(value):
-    return jnp.concatenate([value, value], axis=1)
+def mixing_factors(place, chunk):
+    row, low, third = wave_numbers(place, chunk)
+    return factor_of(low + 16 * (row // 16), third), third.astype(f32) * (full_turn / 256)
 
 
 UNROLL = 5
+DEPTH = 2
 
 
 class Place:
@@ -151,7 +168,7 @@
         self.wave = self.gx * 2 + self.gz
 
     def by_wave(self, wave):
-        return (wave // 2, self.gy, wave % 2)
+        return (lax.div(wave, 2), self.gy, lax.rem(wave, 2))
 
     def by_second(self, second):
         return (self.gx, second, self.gz)
@@ -161,8 +178,8 @@
 
         def signal(step, carry):
             for target in (
-                self.by_wave((self.wave + step) % 16),
-                self.by_second((self.gy + step) % 16),
+                self.by_wave(lax.rem(self.wave + step, 16)),
+                self.by_second(lax.rem(self.gy + step, 16)),
             ):
                 pl.semaphore_signal(barrier, inc=1, device_id=target, device_id_type=MESH)
             return carry
@@ -180,7 +197,7 @@
 
     def each(self, act):
         def body(step, carry):
-            peer = (self.me + step) % 16
+            peer = lax.rem(self.me + step, 16)
             if self.wanted is None:
                 act(peer)
             else:
@@ -216,6 +233,21 @@
         self.each(lambda peer: self.copy(peer).wait_send())
 
 
+class Chain:
+    def __init__(self, exchanges):
+        self.exchanges, self.count = exchanges, 0
+
+    def start(self, number):
+        before = self.exchanges[number - DEPTH] if number >= DEPTH else None
+        assert number == self.count
+        self.exchanges[number].start(before)
+        self.count += 1
+
+    def finish(self):
+        for exchange in self.exchanges[-DEPTH:]:
+            exchange.finish()
+
+
 def arrived(buffer, sem):
     pltpu.make_async_copy(buffer, buffer, sem).wait()
 
@@ -230,18 +262,8 @@
     return jnp.where(inside, 1.0, 0.0)
 
 
-def parts(ref):
-    return ref.at[0], ref.at[1]
-
-
-def lower(ref, axis):
-    if axis == 0:
-        return ref[0, :, :128], ref[1, :, :128]
-    return ref[0, :, :, :128], ref[1, :, :, :128]
-
-
 def lower_rows(ref):
-    return jnp.concatenate([ref[:, 0:64], ref[:, 128:192]], axis=1)
+    return jnp.concatenate([ref[:, 0:32], ref[:, 64:96]], axis=1)
 
 
 class Halo:
@@ -376,6 +398,10 @@
 
 
 ORDER = (0, 2, 1)
+CHUNKS = ((0,), (1,))
+SECONDS = ((0, 0), (0, 1), (1, 0), (1, 1))
+LASTS = ((0, 0), (2, 0), (0, 1), (2, 1), (1, 0), (1, 1))
+BACK = ((0, 0), (0, 1), (2, 0), (2, 1), (1, 0), (1, 1))
 
 
 def kernel(
@@ -416,49 +442,42 @@
     in_lower = (at.gx < 4) & (at.gy < 8) & (at.gz == 0)
     has_rows = at.gy < 8
 
-    depths = Exchange(
-        at.wave, at.by_wave, lambda p: z_out.at[p], z_in.at[at.gx % 4],
-        lambda p: z_sent.at[p], z_got,
-    )
-    firsts = Exchange(
-        at.gy, at.by_second, lambda p: k_out.at[p], k_in.at[at.gy % 8],
-        lambda p: k_sent.at[p], k_got,
-    )
-    seconds = [
-        Exchange(
-            at.gy, at.by_second, lambda p, f=f: y_out.at[f, p], y_in.at[f, at.gy],
-            lambda p, f=f: y_sent.at[f, p], y_got.at[f],
+    def over_waves(order, out, into, sent, got, block=lambda p: p, slot=None, wanted=None):
+        slot = at.wave if slot is None else slot
+        return Chain(
+            [
+                Exchange(
+                    at.wave, at.by_wave, lambda p, k=k: out.at[*k, block(p)], into.at[*k, slot],
+                    lambda p, n=n: sent.at[n, p], got.at[n], wanted,
+                )
+                for n, k in enumerate(order)
+            ]
         )
-        for f in range(2)
-    ]
-    lasts = [
-        Exchange(
-            at.wave, at.by_wave, lambda p, f=f: x_out.at[f, p // 2], x_in.at[f, at.wave],
-            lambda p, f=f: x_sent.at[f, p], x_got.at[f],
+
+    def over_seconds(order, out, into, sent, got, block=lambda p: p, slot=None, wanted=None):
+        slot = at.gy if slot is None else slot
+        return Chain(
+            [
+                Exchange(
+                    at.gy, at.by_second, lambda p, k=k: out.at[*k, block(p)], into.at[*k, slot],
+                    lambda p, n=n: sent.at[n, p], got.at[n], wanted,
+                )
+                for n, k in enumerate(order)
+            ]
         )
-        for f in range(3)
-    ]
-    depths_back = [
-        Exchange(
-            at.wave, at.by_wave, lambda p, f=f: zb_out.at[f, p], zb_in.at[f, at.wave],
-            lambda p, f=f: zb_sent.at[f, p], zb_got.at[f],
-        )
-        for f in range(3)
-    ]
-    firsts_back = [
-        Exchange(
-            at.gy, at.by_second, lambda p, f=f: kb_out.at[f, p], kb_in.at[f, at.gy],
-            lambda p, f=f: kb_sent.at[f, p], kb_got.at[f],
-        )
-        for f in range(2)
-    ]
-    seconds_back = Exchange(
-        at.gy, at.by_second, lambda p: yb_out.at[p % 8], yb_in.at[at.gy],
-        lambda p: yb_sent.at[p], yb_got, lambda p: p < 8,
-    )
-    lasts_back = Exchange(
-        at.wave, at.by_wave, lambda p: xb_out.at[p // 2 % 4], xb_in.at[at.wave],
-        lambda p: xb_sent.at[p], xb_got, lambda p: (p < 8) & (p % 2 == 0),
+
+    depths = over_waves(CHUNKS, z_out, z_in, z_sent, z_got, slot=lax.rem(at.gx, 4))
+    firsts = over_seconds(CHUNKS, k_out, k_in, k_sent, k_got, slot=lax.rem(at.gy, 8))
+    seconds = over_seconds(SECONDS, y_out, y_in, y_sent, y_got)
+    lasts = over_waves(LASTS, x_out, x_in, x_sent, x_got, lambda p: lax.div(p, 2))
+    depths_back = over_waves(BACK, zb_out, zb_in, zb_sent, zb_got)
+    firsts_back = over_seconds(SECONDS, kb_out, kb_in, kb_sent, kb_got)
+    seconds_back = over_seconds(
+        CHUNKS, yb_out, yb_in, yb_sent, yb_got, lambda p: lax.rem(p, 8), None, lambda p: p < 8
+    )
+    lasts_back = over_waves(
+        CHUNKS, xb_out, xb_in, xb_sent, xb_got, lambda p: lax.rem(lax.div(p, 2), 4), None,
+        lambda p: (p < 8) & (lax.rem(p, 2) == 0),
     )
     cell_halo = Halo(
         at, cells, cells_y_out, cells_y_in, cells_z_out, cells_z_in, cells_sent, cells_got
@@ -469,60 +488,69 @@
 
     loads["remanence"].wait()
     loads["forward_z"].wait()
+
     @pl.when(in_lower)
     def _():
         magnet = remanence[...].reshape(512, 128) * region(at, bounds)
-        z_out[...] = depth_waves(magnet, forward_z).reshape(16, 16, 512)
+        z_out[...] = depth_waves(magnet, forward_z).reshape(2, 16, 8, 512)
 
     at.meet()
-    pl.when(in_lower)(lambda: depths.start())
+
+    @pl.when(in_lower)
+    def _():
+        depths.start(0)
+        depths.start(1)
 
     for name in ("velocity", "seed", "suscept"):
         loads[name].wait()
     cell_halo.start()
-
-    loads["lower_x"].wait()
-    loads["twiddle"].wait()
-    loads["kron"].wait()
+    for name in ("lower_x", "twiddle", "kron"):
+        loads[name].wait()
+
     @pl.when(has_rows)
     def _():
-        arrived(z_in, z_got)
-        block = z_in[...].reshape(64, 512)
-        block = jnp.concatenate([block[:, :256], block[:, 256:]], axis=0)
-        real, imag = first_forward(mul(lower_x, block), twiddle, parts(kron))
-        k_out[...] = jnp.concatenate([real, imag], axis=1).reshape(16, 16, 256)
-        firsts.start()
+        for c in range(2):
+            arrived(z_in.at[c], z_got.at[c])
+            block = mul(lower_x, halves_on_rows(z_in[c].reshape(32, 512)))
+            k_out[c] = first_forward(block, twiddle, kron).reshape(16, 16, 128)
+            firsts.start(c)
 
     cell_halo.arrive(cells_wide)
     cell_rows(at, cell_halo, cells_wide, next_out, adjoint_out, source)
 
     loads["second"].wait()
-    potential, second_factor = spectral_factors(at.wave, at.gy)
-    arrived(k_in, k_got)
-    real, imag = rotated(*lower(second, 1), k_in[...].reshape(128, 256), -1.0)
-    value = jnp.concatenate([real * potential, imag * potential], axis=1)
-    for f in range(2):
-        if f == 1:
-            value = value * twice(second_factor)
-        real, imag = rotated(*parts(second), value, 1.0)
-        y_out[f] = jnp.concatenate([real, imag], axis=1).reshape(16, 16, 256)
-        seconds[f].start(seconds[0] if f == 1 else None)
+    factors = [spectral_factors(at.wave, at.gy, c) for c in range(2)]
+    cosine, sine = second.at[0], second.at[1]
+    for c in range(2):
+        potential, second_factor = factors[c]
+        arrived(k_in.at[c], k_got.at[c])
+        value = k_in[c].reshape(128, 128)
+        value = rotated(cosine[:, :, :128], sine[:, :, :128], value, -1.0) * potential
+        value = jnp.concatenate([value, value * second_factor], axis=1)
+        value = rotated(cosine, sine, value, 1.0)
+        y_out[0, c] = value[:, :128].reshape(16, 16, 128)
+        y_out[1, c] = value[:, 128:].reshape(16, 16, 128)
+        seconds.start(c)
+    seconds.start(2)
+    seconds.start(3)
 
     loads["inverse_x"].wait()
-    first_factor, third_factor = mixing_factors(at.wave)
-
-    def send_first(f, value, after=None):
-        value = first_inverse(value, twiddle, parts(kron), inverse_x)
-        x_out[f, :, :, :256] = value[:128].reshape(8, 16, 256)
-        x_out[f, :, :, 256:] = value[128:].reshape(8, 16, 256)
-        lasts[f].start(after)
-
-    arrived(y_in.at[0], y_got.at[0])
-    value = y_in[0].reshape(256, 256)
-    send_first(0, value * twice(first_factor))
-    send_first(2, value * twice(third_factor), lasts[0])
-    arrived(y_in.at[1], y_got.at[1])
-    send_first(1, y_in[1].reshape(256, 256), lasts[2])
+    mixing = [mixing_factors(at.wave, c) for c in range(2)]
+
+    def send_first(f, c, value):
+        value = first_inverse(value, twiddle, kron, inverse_x)
+        x_out[f, c, :, :, :256] = value[:64].reshape(8, 8, 256)
+        x_out[f, c, :, :, 256:] = value[64:].reshape(8, 8, 256)
+        lasts.start(LASTS.index((f, c)))
+
+    for c in range(2):
+        arrived(y_in.at[0, c], y_got.at[c])
+        value = y_in[0, c].reshape(256, 128)
+        send_first(0, c, value * mixing[c][0])
+        send_first(2, c, value * mixing[c][1])
+    for c in range(2):
+        arrived(y_in.at[1, c], y_got.at[2 + c])
+        send_first(1, c, y_in[1, c].reshape(256, 128))
 
     loads["inverse_z"].wait()
     turned = jnp.full((8, 128), step[0] % field_period, jnp.int32).astype(f32)
@@ -530,66 +558,68 @@
     applied = (jnp.cos(turned)[:1], jnp.sin(turned)[:1], None)
     square = jnp.zeros((512, 128), f32)
     weight = source[...].reshape(512, 128)
-    before = None
     for f in ORDER:
-        arrived(x_in.at[f], x_got.at[f])
+        for c in range(2):
+            arrived(x_in.at[f, c], x_got.at[LASTS.index((f, c))])
         field = mul(inverse_z.at[at.gz], x_in[f].reshape(256, 512)).T
         if applied[f] is not None:
             field = field + applied[f]
         square = square + field * field
-        zb_out[f] = depth_waves(weight * field, forward_z).reshape(16, 16, 512)
-        depths_back[f].start(before)
-        before = depths_back[f]
+        zb_out[f] = depth_waves(weight * field, forward_z).reshape(2, 16, 8, 512)
+        for c in range(2):
+            depths_back.start(BACK.index((f, c)))
     energy[0, 1:33] = (0.5 * square).reshape(32, 16, 128)
     energy_halo.start()
 
     loads["forward_x"].wait()
-    def first_of(f):
-        arrived(zb_in.at[f], zb_got.at[f])
-        block = zb_in[f].reshape(256, 512)
-        mixed = mul(forward_x.at[0], block[:, :256]) + mul(forward_x.at[1], block[:, 256:])
-        real, imag = first_forward(mixed, twiddle, parts(kron))
-        return jnp.concatenate([real, imag], axis=1)
-
-    value = first_of(0) * twice(first_factor)
-    value = value + first_of(2) * twice(third_factor)
-    kb_out[0] = value.reshape(16, 16, 256)
-    firsts_back[0].start()
-    kb_out[1] = first_of(1).reshape(16, 16, 256)
-    firsts_back[1].start(firsts_back[0])
+
+    def first_of(f, c):
+        arrived(zb_in.at[f, c], zb_got.at[BACK.index((f, c))])
+        block = mul(forward_x, halves_on_rows(zb_in[f, c].reshape(128, 512)))
+        return first_forward(block, twiddle, kron)
+
+    for c in range(2):
+        value = first_of(0, c) * mixing[c][0] + first_of(2, c) * mixing[c][1]
+        kb_out[0, c] = value.reshape(16, 16, 128)
+        firsts_back.start(c)
+    for c in range(2):
+        kb_out[1, c] = first_of(1, c).reshape(16, 16, 128)
+        firsts_back.start(2 + c)
 
     energy_halo.arrive(energy_wide)
     energy_rows(at, energy_halo, energy_wide, cells, next_out)
     pl.when(in_lower)(lambda: depths.finish())
     pl.when(has_rows)(lambda: firsts.finish())
-    for each in (seconds[1], lasts[1], depths_back[1], cell_halo, energy_halo):
+    for each in (seconds, lasts, depths_back, cell_halo, energy_halo):
         each.finish()
 
-    def second_of(f):
-        arrived(kb_in.at[f], kb_got.at[f])
-        real, imag = rotated(*parts(second), kb_in[f].reshape(256, 256), -1.0)
-        return jnp.concatenate([real, imag], axis=1)
-
-    value = second_of(0)
-    value = (value + second_of(1) * twice(second_factor)) * twice(potential)
-    real, imag = rotated(*lower(second, 0), value, 1.0)
-    yb_out[...] = jnp.concatenate([real, imag], axis=1).reshape(8, 16, 256)
-    seconds_back.start()
-    firsts_back[1].finish()
+    for c in range(2):
+        potential, second_factor = factors[c]
+        for f in range(2):
+            arrived(kb_in.at[f, c], kb_got.at[2 * f + c])
+        value = [kb_in[f, c].reshape(256, 128) for f in range(2)]
+        value = rotated(cosine, sine, jnp.concatenate(value, axis=1), -1.0)
+        value = (value[:, :128] + value[:, 128:] * second_factor) * potential
+        value = rotated(cosine[:, :128], sine[:, :128], value, 1.0)
+        yb_out[c] = value.reshape(8, 16, 128)
+        seconds_back.start(c)
+    firsts_back.finish()
     gradient_out[...] = jnp.zeros((32, 16, 128), f32)
 
     @pl.when(has_rows)
     def _():
-        arrived(yb_in, yb_got)
-        value = yb_in[...].reshape(256, 256)
-        value = first_inverse(value, twiddle, parts(kron), lower_rows(inverse_x))
-        xb_out[:, :, :256] = value[:64].reshape(4, 16, 256)
-        xb_out[:, :, 256:] = value[64:].reshape(4, 16, 256)
-        lasts_back.start()
+        for c in range(2):
+            arrived(yb_in.at[c], yb_got.at[c])
+            value = yb_in[c].reshape(256, 128)
+            value = first_inverse(value, twiddle, kron, lower_rows(inverse_x))
+            xb_out[c, :, :, :256] = value[:32].reshape(4, 8, 256)
+            xb_out[c, :, :, 256:] = value[32:].reshape(4, 8, 256)
+            lasts_back.start(c)
 
     @pl.when(in_lower)
     def _():
-        arrived(xb_in, xb_got)
+        for c in range(2):
+            arrived(xb_in.at[c], xb_got.at[c])
         value = mul(inverse_z.at[0], xb_in[...].reshape(256, 512)).T
         gradient_out[...] = (value * region(at, bounds)).reshape(32, 16, 128)
 
@@ -606,16 +636,17 @@
 
 def on_device(velocity, adjoint_seed, susceptibility, remanence, region_bounds, step_id):
     tables = make_tables()
-    shapes = [(16, 16, 512), (4, 16, 512), (16, 16, 256), (8, 16, 256)]
-    shapes += [(2, 16, 16, 256), (2, 16, 16, 256), (3, 8, 16, 512), (3, 16, 16, 512)]
-    shapes += [(3, 16, 16, 512), (3, 16, 16, 512), (2, 16, 16, 256), (2, 16, 16, 256)]
-    shapes += [(8, 16, 256), (16, 16, 256), (4, 16, 512), (16, 16, 512)]
+    shapes = [(2, 16, 8, 512), (2, 4, 8, 512), (2, 16, 16, 128), (2, 8, 16, 128)]
+    shapes += [(2, 2, 16, 16, 128)] * 2 + [(3, 2, 8, 8, 512), (3, 2, 16, 8, 512)]
+    shapes += [(3, 2, 16, 8, 512)] * 2 + [(2, 2, 16, 16, 128)] * 2
+    shapes += [(2, 8, 16, 128), (2, 16, 16, 128), (2, 4, 8, 512), (2, 16, 8, 512)]
     for n in (7, 1):
         shapes += [(n, 34, 16, 128), (2, n, 32, 128), (2, n, 32, 128), (8, 512), (8, 512)]
         shapes += [(n, 32, 16, 128)]
     shapes += [(32, 16, 128)]
-    sems = [(16,), (), (16,), (), (2, 16), (2,), (3, 16), (3,)]
-    sems += [(3, 16), (3,), (2, 16), (2,), (16,), (), (16,), ()]
+    sems = []
+    for n in (2, 2, 4, 6, 6, 4, 2, 2):
+        sems += [(n, 16), (n,)]
     sems += [(5,)] * 4
     vmem = pl.BlockSpec(memory_space=pltpu.VMEM)
     smem = pl.BlockSpec(memory_space=pltpu.SMEM)

time: 109 us -> 98.8 us (0.906); the launches traced: 107 us -> 98.7 us
  Pallas kernels: 104 us -> 94.9 us
    pallas_call x1, Pallas kernels: 104 us -> 94.9 us  [on_device(): pl.pallas_call(kernel, out_shape=(jax.ShapeDtypeStruct((3, 32, 16, 128),...]
where the time goes in v5:
time: 98.8 us; the launch traced here: 98.7 us
  Pallas kernels  94.9 us (96%)
  local copies, waits for them, and re-layouts  2.48 us (3%)
  between operations  1.31 us (1%)
    pallas_call x1, Pallas kernels, on_device(): pl.pallas_call(kernel, out_shape=(jax.ShapeDtypeStruct((3, 32, 16, 128),...  94.9 us
    unnamed x5, local copies, waits for them, and re-layouts  2.48 us

profile of v5, /device:TPU:1, one launch (start us, length us, event | category | flops | bytes accessed | tf_op | source)
XLA Modules:
  0.0 98.7 jit_solution(2787821673881623525)
XLA Ops:
  0.6 0.0 copy-start
  1.3 0.0 copy-done
  1.3 94.9 %shard_map.157 = (f32[3,32,16,128]{3,2,1,0:T(8,128)S(1)}, f32[3,32,16,128]{3,2,1,0:T(8,128)S(1)}, f32[32,16,128]{2,1,0:T(8,128)S(1)}) custom-call(f32[3,32,16,128]{3,2,1,0:T(8,128)} %velocity.1, f32[3,32,16,128]{3,2,1,0:T(8,128)} %adjoint_seed.1, f32[32,16,128]{2,1,0:T(8,128)} %suscept.1, f32[32,16,128]{2,1,0:T(8,128)} %remanence_in.1, ...), custom_call_target="tpu_custom_call" | custom-call | tf_op jit(solution)/shard_map/pallas_call | solution.py:659
  96.2 0.9 copy.21
  97.1 0.9 copy.22
  98.0 0.7 copy.23
Async XLA Ops:
  0.6 0.7 copy-start

commit v6 on v5

--- a/solution.py
+++ b/solution.py
@@ -42,24 +42,20 @@
     eye4, eye16 = np.eye(4), np.eye(16)
     c, s, j = np.arange(2)[:, None, None], np.arange(16)[:, None], np.arange(4)
     k3 = 1 + 8 * s + 4 * c + j
-    z = np.arange(128)
+    z = np.arange(256)
     phase = turn * k3[..., None] * z
-    forward_z = np.stack([np.cos(phase), -np.sin(phase)], 2).reshape(256, 128)
+    forward_z = np.stack([np.cos(phase), -np.sin(phase)], 2).reshape(256, 256)
     weight = np.where(k3 == 128, 1.0, 2.0)[..., None] / 256.0**3
-    inverse_z = []
-    for part in range(2):
-        phase = turn * k3[..., None] * (z + 128 * part)
-        both = np.stack([np.cos(phase) * weight, -np.sin(phase) * weight], 2)
-        inverse_z.append(both.reshape(256, 128).T)
+    both = np.stack([np.cos(phase) * weight, -np.sin(phase) * weight], 2)
+    inverse_z = both.reshape(256, 256).T
     q, t, ka = np.arange(8), np.arange(2), np.arange(16)
     theta = turn * 16 * (2 * q[:, None, None] + t[None, :, None]) * ka
     c, s = np.cos(theta), np.sin(theta)
     turned = np.stack([np.stack([c, s]), np.stack([-s, c])])
-    sign = np.stack([np.ones(4), (-1.0) ** (1 + j)])
-    forward_x = np.einsum("abqtk,gj,ji->akitqgbj", turned, sign, eye4).reshape(128, 256)
+    forward_x = np.einsum("abqtk,ji->akiqtbj", turned, eye4).reshape(128, 128)
     lower_x = np.einsum("abqtk,ji->akitqbj", turned[:, :, :4], eye4).reshape(128, 64)
     back = np.stack([np.stack([c, -s]), np.stack([s, c])])
-    inverse_x = np.einsum("abqtk,ij->tqaibkj", back, eye4).reshape(128, 128)
+    inverse_x = np.einsum("abqtk,ij->qtaibkj", back, eye4).reshape(128, 128)
     b = np.arange(16)
     phi = turn * ka[:, None] * b
     twiddle = np.stack([np.cos(phi), np.sin(phi)])[:, :, None, :, None]
@@ -70,7 +66,7 @@
     angle = turn * (k[:, None] * k % 256)
     return dict(
         forward_z=pieces(forward_z),
-        inverse_z=np.stack([pieces(m) for m in inverse_z]),
+        inverse_z=pieces(inverse_z),
         forward_x=pieces(forward_x),
         lower_x=pieces(lower_x),
         inverse_x=pieces(inverse_x),
@@ -260,10 +256,6 @@
     inside = inside & (second >= bounds[0, 1]) & (second < bounds[1, 1])
     inside = inside & (third >= bounds[0, 2]) & (third < bounds[1, 2])
     return jnp.where(inside, 1.0, 0.0)
-
-
-def lower_rows(ref):
-    return jnp.concatenate([ref[:, 0:32], ref[:, 64:96]], axis=1)
 
 
 class Halo:
@@ -413,9 +405,10 @@
     zb_out, zb_in, kb_out, kb_in, yb_out, yb_in, xb_out, xb_in,
     cells, cells_y_out, cells_y_in, cells_z_out, cells_z_in, cells_wide,
     energy, energy_y_out, energy_y_in, energy_z_out, energy_z_in, energy_wide, source,
+    source_in, energy_out,
     z_sent, z_got, k_sent, k_got, y_sent, y_got, x_sent, x_got,
     zb_sent, zb_got, kb_sent, kb_got, yb_sent, yb_got, xb_sent, xb_got,
-    cells_sent, cells_got, energy_sent, energy_got,
+    cells_sent, cells_got, energy_sent, energy_got, swap_sent, swap_got,
     remanence, forward_z, inverse_z, forward_x, lower_x, inverse_x, twiddle, kron, second, loaded,
 ):
     at = Place()
@@ -469,7 +462,7 @@
     depths = over_waves(CHUNKS, z_out, z_in, z_sent, z_got, slot=lax.rem(at.gx, 4))
     firsts = over_seconds(CHUNKS, k_out, k_in, k_sent, k_got, slot=lax.rem(at.gy, 8))
     seconds = over_seconds(SECONDS, y_out, y_in, y_sent, y_got)
-    lasts = over_waves(LASTS, x_out, x_in, x_sent, x_got, lambda p: lax.div(p, 2))
+    lasts = over_waves(LASTS, x_out, x_in, x_sent, x_got)
     depths_back = over_waves(BACK, zb_out, zb_in, zb_sent, zb_got)
     firsts_back = over_seconds(SECONDS, kb_out, kb_in, kb_sent, kb_got)
     seconds_back = over_seconds(
@@ -492,7 +485,7 @@
     @pl.when(in_lower)
     def _():
         magnet = remanence[...].reshape(512, 128) * region(at, bounds)
-        z_out[...] = depth_waves(magnet, forward_z).reshape(2, 16, 8, 512)
+        z_out[...] = depth_waves(magnet, forward_z[:, :, :128]).reshape(2, 16, 8, 512)
 
     at.meet()
 
@@ -517,6 +510,24 @@
 
     cell_halo.arrive(cells_wide)
     cell_rows(at, cell_halo, cells_wide, next_out, adjoint_out, source)
+    here, there = at.gz * 16, (1 - at.gz) * 16
+    source_swap = pltpu.make_async_remote_copy(
+        src_ref=source.at[pl.ds(there, 16)],
+        dst_ref=source_in,
+        send_sem=swap_sent.at[0],
+        recv_sem=swap_got.at[0],
+        device_id=(at.gx, at.gy, 1 - at.gz),
+        device_id_type=MESH,
+    )
+    energy_swap = pltpu.make_async_remote_copy(
+        src_ref=energy_out,
+        dst_ref=energy.at[0, pl.ds(1 + here, 16)],
+        send_sem=swap_sent.at[1],
+        recv_sem=swap_got.at[1],
+        device_id=(at.gx, at.gy, 1 - at.gz),
+        device_id_type=MESH,
+    )
+    source_swap.start()
 
     loads["second"].wait()
     factors = [spectral_factors(at.wave, at.gy, c) for c in range(2)]
@@ -539,8 +550,7 @@
 
     def send_first(f, c, value):
         value = first_inverse(value, twiddle, kron, inverse_x)
-        x_out[f, c, :, :, :256] = value[:64].reshape(8, 8, 256)
-        x_out[f, c, :, :, 256:] = value[64:].reshape(8, 8, 256)
+        x_out[f, c] = value.reshape(16, 8, 256)
         lasts.start(LASTS.index((f, c)))
 
     for c in range(2):
@@ -553,29 +563,37 @@
         send_first(1, c, y_in[1, c].reshape(256, 128))
 
     loads["inverse_z"].wait()
-    turned = jnp.full((8, 128), step[0] % field_period, jnp.int32).astype(f32)
+    turned = jnp.full((8, 256), step[0] % field_period, jnp.int32).astype(f32)
     turned = full_turn * turned / field_period
     applied = (jnp.cos(turned)[:1], jnp.sin(turned)[:1], None)
-    square = jnp.zeros((512, 128), f32)
-    weight = source[...].reshape(512, 128)
+    square = jnp.zeros((256, 256), f32)
+    source_swap.wait_recv()
+    mine = source[pl.ds(here, 16)].reshape(256, 128).T
+    theirs = source_in[...].reshape(256, 128).T
+    weight = jnp.concatenate(
+        [jnp.where(at.gz == 0, mine, theirs), jnp.where(at.gz == 0, theirs, mine)], axis=0
+    )
     for f in ORDER:
         for c in range(2):
             arrived(x_in.at[f, c], x_got.at[LASTS.index((f, c))])
-        field = mul(inverse_z.at[at.gz], x_in[f].reshape(256, 512)).T
+        field = mul(inverse_z, x_in[f].reshape(256, 256))
         if applied[f] is not None:
             field = field + applied[f]
         square = square + field * field
-        zb_out[f] = depth_waves(weight * field, forward_z).reshape(2, 16, 8, 512)
+        zb_out[f] = mul(forward_z, weight * field).reshape(2, 16, 8, 256)
         for c in range(2):
             depths_back.start(BACK.index((f, c)))
-    energy[0, 1:33] = (0.5 * square).reshape(32, 16, 128)
-    energy_halo.start()
+    low, high = 0.5 * square[:128].T, 0.5 * square[128:].T
+    mine, theirs = jnp.where(at.gz == 0, low, high), jnp.where(at.gz == 0, high, low)
+    energy[0, pl.ds(1 + here, 16)] = mine.reshape(16, 16, 128)
+    energy_out[...] = theirs.reshape(16, 16, 128)
+    energy_swap.start()
 
     loads["forward_x"].wait()
 
     def first_of(f, c):
         arrived(zb_in.at[f, c], zb_got.at[BACK.index((f, c))])
-        block = mul(forward_x, halves_on_rows(zb_in[f, c].reshape(128, 512)))
+        block = mul(forward_x, zb_in[f, c].reshape(128, 256))
         return first_forward(block, twiddle, kron)
 
     for c in range(2):
@@ -586,12 +604,14 @@
         kb_out[1, c] = first_of(1, c).reshape(16, 16, 128)
         firsts_back.start(2 + c)
 
-    energy_halo.arrive(energy_wide)
-    energy_rows(at, energy_halo, energy_wide, cells, next_out)
+    energy_swap.wait_recv()
+    energy_halo.start()
     pl.when(in_lower)(lambda: depths.finish())
     pl.when(has_rows)(lambda: firsts.finish())
-    for each in (seconds, lasts, depths_back, cell_halo, energy_halo):
+    for each in (seconds, lasts, depths_back, cell_halo):
         each.finish()
+    source_swap.wait_send()
+    energy_swap.wait_send()
 
     for c in range(2):
         potential, second_factor = factors[c]
@@ -604,6 +624,9 @@
         yb_out[c] = value.reshape(8, 16, 128)
         seconds_back.start(c)
     firsts_back.finish()
+    energy_halo.arrive(energy_wide)
+    energy_rows(at, energy_halo, energy_wide, cells, next_out)
+    energy_halo.finish()
     gradient_out[...] = jnp.zeros((32, 16, 128), f32)
 
     @pl.when(has_rows)
@@ -611,16 +634,16 @@
         for c in range(2):
             arrived(yb_in.at[c], yb_got.at[c])
             value = yb_in[c].reshape(256, 128)
-            value = first_inverse(value, twiddle, kron, lower_rows(inverse_x))
-            xb_out[c, :, :, :256] = value[:32].reshape(4, 8, 256)
-            xb_out[c, :, :, 256:] = value[32:].reshape(4, 8, 256)
+            value = first_inverse(value, twiddle, kron, inverse_x[:, :64]).reshape(4, 2, 8, 256)
+            xb_out[c, :, :, :256] = value[:, 0]
+            xb_out[c, :, :, 256:] = value[:, 1]
             lasts_back.start(c)
 
     @pl.when(in_lower)
     def _():
         for c in range(2):
             arrived(xb_in.at[c], xb_got.at[c])
-        value = mul(inverse_z.at[0], xb_in[...].reshape(256, 512)).T
+        value = mul(inverse_z[:, :128], xb_in[...].reshape(256, 512)).T
         gradient_out[...] = (value * region(at, bounds)).reshape(32, 16, 128)
 
     seconds_back.finish()
@@ -637,17 +660,17 @@
 def on_device(velocity, adjoint_seed, susceptibility, remanence, region_bounds, step_id):
     tables = make_tables()
     shapes = [(2, 16, 8, 512), (2, 4, 8, 512), (2, 16, 16, 128), (2, 8, 16, 128)]
-    shapes += [(2, 2, 16, 16, 128)] * 2 + [(3, 2, 8, 8, 512), (3, 2, 16, 8, 512)]
-    shapes += [(3, 2, 16, 8, 512)] * 2 + [(2, 2, 16, 16, 128)] * 2
+    shapes += [(2, 2, 16, 16, 128)] * 2 + [(3, 2, 16, 8, 256)] * 2
+    shapes += [(3, 2, 16, 8, 256)] * 2 + [(2, 2, 16, 16, 128)] * 2
     shapes += [(2, 8, 16, 128), (2, 16, 16, 128), (2, 4, 8, 512), (2, 16, 8, 512)]
     for n in (7, 1):
         shapes += [(n, 34, 16, 128), (2, n, 32, 128), (2, n, 32, 128), (8, 512), (8, 512)]
         shapes += [(n, 32, 16, 128)]
-    shapes += [(32, 16, 128)]
+    shapes += [(32, 16, 128)] + [(16, 16, 128)] * 2
     sems = []
     for n in (2, 2, 4, 6, 6, 4, 2, 2):
         sems += [(n, 16), (n,)]
-    sems += [(5,)] * 4
+    sems += [(5,)] * 4 + [(2,)] * 2
     vmem = pl.BlockSpec(memory_space=pltpu.VMEM)
     smem = pl.BlockSpec(memory_space=pltpu.SMEM)
     hbm = pl.BlockSpec(memory_space=pltpu.HBM)

time: 98.8 us -> 86.4 us (0.87)
  Pallas kernels: 94.9 us -> 82.5 us
    pallas_call x1, Pallas kernels: 94.9 us -> 82.5 us  [on_device(): pl.pallas_call(kernel, out_shape=(jax.ShapeDtypeStruct((3, 32, 16, 128),...]
where the time goes in v6:
time: 86.4 us; the launch traced here: 86.3 us
  Pallas kernels  82.5 us (95%)
  local copies, waits for them, and re-layouts  2.48 us (3%)
  between operations  1.31 us (2%)
    pallas_call x1, Pallas kernels, on_device(): pl.pallas_call(kernel, out_shape=(jax.ShapeDtypeStruct((3, 32, 16, 128),...  82.5 us
    unnamed x5, local copies, waits for them, and re-layouts  2.48 us

profile of v6, /device:TPU:1, one launch (start us, length us, event | category | flops | bytes accessed | tf_op | source)
XLA Modules:
  0.0 86.3 jit_solution(16576223517810732250)
XLA Ops:
  0.6 0.0 copy-start
  1.3 0.0 copy-done
  1.3 82.5 %shard_map.157 = (f32[3,32,16,128]{3,2,1,0:T(8,128)S(1)}, f32[3,32,16,128]{3,2,1,0:T(8,128)S(1)}, f32[32,16,128]{2,1,0:T(8,128)S(1)}) custom-call(f32[3,32,16,128]{3,2,1,0:T(8,128)} %velocity.1, f32[3,32,16,128]{3,2,1,0:T(8,128)} %adjoint_seed.1, f32[32,16,128]{2,1,0:T(8,128)} %suscept.1, f32[32,16,128]{2,1,0:T(8,128)} %remanence_in.1, ...), custom_call_target="tpu_custom_call" | custom-call | tf_op jit(solution)/shard_map/pallas_call | solution.py:682
  83.8 0.9 %copy.21 = f32[3,32,16,128]{3,2,1,0:T(8,128)} copy(f32[3,32,16,128]{3,2,1,0:T(8,128)S(1)} %get-tuple-element.6) | data formatting | bytes 1572864
  84.7 0.9 %copy.22 = f32[3,32,16,128]{3,2,1,0:T(8,128)} copy(f32[3,32,16,128]{3,2,1,0:T(8,128)S(1)} %get-tuple-element.7) | data formatting | bytes 1572864
  85.6 0.7 copy.23
Async XLA Ops:
  0.6 0.7 copy-start

commit v7 on v6

--- a/solution.py
+++ b/solution.py
@@ -28,13 +28,15 @@
     return high, (value - high.astype(f32)).astype(bf16)
 
 
-def product(matrix, value, dims=(((1,), (0,)), ((), ()))):
-    dot = lambda a, b: lax.dot_general(a, b, dims, preferred_element_type=f32)
-    return dot(matrix[0], value[0]) + dot(matrix[0], value[1]) + dot(matrix[1], value[0])
+def dot(left, right, dims=(((1,), (0,)), ((), ()))):
+    return lax.dot_general(left, right, dims, preferred_element_type=f32)
 
 
 def mul(matrix, value):
-    return product(matrix, cut(value))
+    high, low = cut(value)
+    rows = matrix.shape[1]
+    both = dot(matrix[...].reshape(2 * rows, matrix.shape[2]), high)
+    return both[:rows] + both[rows:] + dot(matrix[0], low)
 
 
 def make_tables():
@@ -80,10 +82,14 @@
     return pltpu.roll(value, 64, 1)
 
 
-def rotated(cosine, sine, value, direction):
-    value = cut(value)
-    first, second = product(cosine, value), product(sine, value)
-    lane = lax.broadcasted_iota(jnp.int32, (first.shape[0], 128), 1)
+def rotated(tables, value, direction):
+    high, low = cut(value)
+    rows, depth = tables.shape[2], tables.shape[3]
+    both = dot(tables.reshape(4 * rows, depth), high)
+    rest = dot(tables[:, 0].reshape(2 * rows, depth), low)
+    first = both[:rows] + both[rows : 2 * rows] + rest[:rows]
+    second = both[2 * rows : 3 * rows] + both[3 * rows :] + rest[rows:]
+    lane = lax.broadcasted_iota(jnp.int32, (rows, 128), 1)
     sign = jnp.where(lane < 64, -direction, direction)
     blocks = [
         first[:, at : at + 128] + sign * half_turned(second[:, at : at + 128])
@@ -93,11 +99,16 @@
 
 
 def depth_waves(block, forward_z):
-    return product(forward_z, cut(block), (((1,), (1,)), ((), ())))
+    high, low = cut(block)
+    dims = (((1,), (1,)), ((), ()))
+    both = dot(forward_z.reshape(512, 128), high, dims)
+    return both[:256] + both[256:] + dot(forward_z[0], low, dims)
 
 
 def sixteenths(value, kron, direction):
-    both = product(cut(value), kron)
+    high, low = cut(value)
+    both = dot(jnp.concatenate([high, low], axis=0), kron[0])
+    both = both[:128] + both[128:] + dot(high, kron[1])
     first, second = both[:, :256], both[:, 256:]
     return jnp.concatenate(
         [first[:64] - direction * second[64:], first[64:] + direction * second[:64]], axis=0
@@ -531,14 +542,13 @@
 
     loads["second"].wait()
     factors = [spectral_factors(at.wave, at.gy, c) for c in range(2)]
-    cosine, sine = second.at[0], second.at[1]
     for c in range(2):
         potential, second_factor = factors[c]
         arrived(k_in.at[c], k_got.at[c])
         value = k_in[c].reshape(128, 128)
-        value = rotated(cosine[:, :, :128], sine[:, :, :128], value, -1.0) * potential
+        value = rotated(second[:, :, :, :128], value, -1.0) * potential
         value = jnp.concatenate([value, value * second_factor], axis=1)
-        value = rotated(cosine, sine, value, 1.0)
+        value = rotated(second[...], value, 1.0)
         y_out[0, c] = value[:, :128].reshape(16, 16, 128)
         y_out[1, c] = value[:, 128:].reshape(16, 16, 128)
         seconds.start(c)
@@ -618,9 +628,9 @@
         for f in range(2):
             arrived(kb_in.at[f, c], kb_got.at[2 * f + c])
         value = [kb_in[f, c].reshape(256, 128) for f in range(2)]
-        value = rotated(cosine, sine, jnp.concatenate(value, axis=1), -1.0)
+        value = rotated(second[...], jnp.concatenate(value, axis=1), -1.0)
         value = (value[:, :128] + value[:, 128:] * second_factor) * potential
-        value = rotated(cosine[:, :128], sine[:, :128], value, 1.0)
+        value = rotated(second[:, :, :128], value, 1.0)
         yb_out[c] = value.reshape(8, 16, 128)
         seconds_back.start(c)
     firsts_back.finish()
@@ -639,6 +649,9 @@
             xb_out[c, :, :, 256:] = value[:, 1]
             lasts_back.start(c)
 
+    seconds_back.finish()
+    pl.when(has_rows)(lambda: lasts_back.finish())
+
     @pl.when(in_lower)
     def _():
         for c in range(2):
@@ -646,15 +659,21 @@
         value = mul(inverse_z[:, :128], xb_in[...].reshape(256, 512)).T
         gradient_out[...] = (value * region(at, bounds)).reshape(32, 16, 128)
 
-    seconds_back.finish()
-    pl.when(has_rows)(lambda: lasts_back.finish())
-
 
 VMEM_GRANT = 24 << 20
 TABLES = (
     "forward_z", "inverse_z", "forward_x", "lower_x", "inverse_x", "twiddle",
     "kron", "second",
 )
+
+
+def put_out(a_in, b_in, c_in, a_out, b_out, c_out, sems):
+    pairs = ((a_in, a_out), (b_in, b_out), (c_in, c_out))
+    copies = [pltpu.make_async_copy(*pair, sems.at[n]) for n, pair in enumerate(pairs)]
+    for copy in copies:
+        copy.start()
+    for copy in copies:
+        copy.wait()
 
 
 def on_device(velocity, adjoint_seed, susceptibility, remanence, region_bounds, step_id):
@@ -679,7 +698,7 @@
     operands = [velocity, adjoint_seed, susceptibility, remanence]
     operands += [jnp.asarray(tables[n]) for n in TABLES]
     operands = [pltpu.with_memory_space_constraint(x, pltpu.HBM) for x in operands]
-    return pl.pallas_call(
+    results = pl.pallas_call(
         kernel,
         out_shape=(
             jax.ShapeDtypeStruct((3, 32, 16, 128), f32),
@@ -696,6 +715,15 @@
             collective_id=0, has_side_effects=True, vmem_limit_bytes=VMEM_GRANT
         ),
     )(*operands, region_bounds, step_id)
+    anywhere = pl.BlockSpec(memory_space=pl.ANY)
+    return pl.pallas_call(
+        put_out,
+        out_shape=[jax.ShapeDtypeStruct(r.shape, f32) for r in results],
+        in_specs=[anywhere] * 3,
+        out_specs=[hbm] * 3,
+        scratch_shapes=[pltpu.SemaphoreType.DMA((3,))],
+        compiler_params=pltpu.CompilerParams(vmem_limit_bytes=1 << 20),
+    )(*results)
 
 
 def solution(mesh):

time: 86.4 us -> 85.8 us (level)
  local copies, waits for them, and re-layouts: 2.48 us -> 0.01 us
  Pallas kernels: 82.5 us -> 84.4 us
    unnamed x5 -> x2, local copies, waits for them, and re-layouts: 2.48 us -> 0.01 us
    pallas_call x0 -> x1, Pallas kernels: none -> 1.25 us  [on_device(): pl.pallas_call(put_out, out_shape=[jax.ShapeDtypeStruct(r.shape, f32) for...]
where the time goes in v7:
time: 85.8 us; the launch traced here: 85.7 us
  Pallas kernels  84.4 us (98%)
  between operations  1.31 us (2%)
    pallas_call x1, Pallas kernels, on_device(): pl.pallas_call(kernel, out_shape=(jax.ShapeDtypeStruct((3, 32, 16, 128),...  83.2 us

profile of v7, /device:TPU:1, one launch (start us, length us, event | category | flops | bytes accessed | tf_op | source)
XLA Modules:
  0.0 85.7 jit_solution(9336370656545488407)
XLA Ops:
  0.6 0.0 copy-start
  1.3 0.0 copy-done
  1.3 83.2 %shard_map.157 = (f32[3,32,16,128]{3,2,1,0:T(8,128)S(1)}, f32[3,32,16,128]{3,2,1,0:T(8,128)S(1)}, f32[32,16,128]{2,1,0:T(8,128)S(1)}) custom-call(f32[3,32,16,128]{3,2,1,0:T(8,128)} %velocity.1, f32[3,32,16,128]{3,2,1,0:T(8,128)} %adjoint_seed.1, f32[32,16,128]{2,1,0:T(8,128)} %suscept.1, f32[32,16,128]{2,1,0:T(8,128)} %remanence_in.1, ...), custom_call_target="tpu_custom_call" | custom-call | tf_op jit(solution)/shard_map/pallas_call | solution.py:701
  84.5 1.2 %shard_map.158 = (f32[3,32,16,128]{3,2,1,0:T(8,128)}, f32[3,32,16,128]{3,2,1,0:T(8,128)}, f32[32,16,128]{2,1,0:T(8,128)}) custom-call(f32[3,32,16,128]{3,2,1,0:T(8,128)S(1)} %get-tuple-element.6.a_in, f32[3,32,16,128]{3,2,1,0:T(8,128)S(1)} %get-tuple-element.7.b_in, f32[32,16,128]{2,1,0:T(8,128)S(1)} %get-tuple-element.8.c_in), custom_call_target="tpu_custom_call" | custom-call | tf_op jit(solution)/shard_map/pallas_call | solution.py:719
Async XLA Ops:
  0.6 0.7 copy-start

commit v8 on v7

--- a/solution.py
+++ b/solution.py
@@ -101,8 +101,8 @@
 def depth_waves(block, forward_z):
     high, low = cut(block)
     dims = (((1,), (1,)), ((), ()))
-    both = dot(forward_z.reshape(512, 128), high, dims)
-    return both[:256] + both[256:] + dot(forward_z[0], low, dims)
+    both = dot(forward_z.reshape(256, 128), high, dims)
+    return both[:128] + both[128:] + dot(forward_z[0], low, dims)
 
 
 def sixteenths(value, kron, direction):
@@ -166,7 +166,7 @@
 
 
 UNROLL = 5
-DEPTH = 2
+DEPTH = 3
 
 
 class Place:
@@ -496,13 +496,16 @@
     @pl.when(in_lower)
     def _():
         magnet = remanence[...].reshape(512, 128) * region(at, bounds)
-        z_out[...] = depth_waves(magnet, forward_z[:, :, :128]).reshape(2, 16, 8, 512)
+        remanence[...] = magnet.reshape(32, 16, 128)
+        z_out[0] = depth_waves(magnet, forward_z[:, :128, :128]).reshape(16, 8, 512)
 
     at.meet()
 
     @pl.when(in_lower)
     def _():
         depths.start(0)
+        magnet = remanence[...].reshape(512, 128)
+        z_out[1] = depth_waves(magnet, forward_z[:, 128:, :128]).reshape(16, 8, 512)
         depths.start(1)
 
     for name in ("velocity", "seed", "suscept"):
@@ -654,10 +657,13 @@
 
     @pl.when(in_lower)
     def _():
+        inside = region(at, bounds)
+        value = 0.0
         for c in range(2):
             arrived(xb_in.at[c], xb_got.at[c])
-        value = mul(inverse_z[:, :128], xb_in[...].reshape(256, 512)).T
-        gradient_out[...] = (value * region(at, bounds)).reshape(32, 16, 128)
+            table = inverse_z[:, :128, 128 * c : 128 * (c + 1)]
+            value = value + mul(table, xb_in[c].reshape(128, 512))
+        gradient_out[...] = (value.T * inside).reshape(32, 16, 128)
 
 
 VMEM_GRANT = 24 << 20

time: 85.8 us -> 85.6 us (level)
  no operation moved by 1% of the time
where the time goes in v8:
time: 85.6 us; the launch traced here: 85.5 us
  Pallas kernels  84.2 us (98%)
  between operations  1.31 us (2%)
    pallas_call x1, Pallas kernels, on_device(): pl.pallas_call(kernel, out_shape=(jax.ShapeDtypeStruct((3, 32, 16, 128),...  82.9 us

profile of v8, /device:TPU:1, one launch (start us, length us, event | category | flops | bytes accessed | tf_op | source)
XLA Modules:
  0.0 85.5 jit_solution(10953906191295449355)
XLA Ops:
  0.6 0.0 copy-start
  1.3 0.0 copy-done
  1.3 82.9 %shard_map.157 = (f32[3,32,16,128]{3,2,1,0:T(8,128)S(1)}, f32[3,32,16,128]{3,2,1,0:T(8,128)S(1)}, f32[32,16,128]{2,1,0:T(8,128)S(1)}) custom-call(f32[3,32,16,128]{3,2,1,0:T(8,128)} %velocity.1, f32[3,32,16,128]{3,2,1,0:T(8,128)} %adjoint_seed.1, f32[32,16,128]{2,1,0:T(8,128)} %suscept.1, f32[32,16,128]{2,1,0:T(8,128)} %remanence_in.1, ...), custom_call_target="tpu_custom_call" | custom-call | tf_op jit(solution)/shard_map/pallas_call | solution.py:707
  84.3 1.2 %shard_map.158 = (f32[3,32,16,128]{3,2,1,0:T(8,128)}, f32[3,32,16,128]{3,2,1,0:T(8,128)}, f32[32,16,128]{2,1,0:T(8,128)}) custom-call(f32[3,32,16,128]{3,2,1,0:T(8,128)S(1)} %get-tuple-element.6.a_in, f32[3,32,16,128]{3,2,1,0:T(8,128)S(1)} %get-tuple-element.7.b_in, f32[32,16,128]{2,1,0:T(8,128)S(1)} %get-tuple-element.8.c_in), custom_call_target="tpu_custom_call" | custom-call | tf_op jit(solution)/shard_map/pallas_call | solution.py:725
Async XLA Ops:
  0.6 0.7 copy-start

commit v9 on v8

--- a/solution.py
+++ b/solution.py
@@ -637,9 +637,6 @@
         yb_out[c] = value.reshape(8, 16, 128)
         seconds_back.start(c)
     firsts_back.finish()
-    energy_halo.arrive(energy_wide)
-    energy_rows(at, energy_halo, energy_wide, cells, next_out)
-    energy_halo.finish()
     gradient_out[...] = jnp.zeros((32, 16, 128), f32)
 
     @pl.when(has_rows)
@@ -652,6 +649,9 @@
             xb_out[c, :, :, 256:] = value[:, 1]
             lasts_back.start(c)
 
+    energy_halo.arrive(energy_wide)
+    energy_rows(at, energy_halo, energy_wide, cells, next_out)
+    energy_halo.finish()
     seconds_back.finish()
     pl.when(has_rows)(lambda: lasts_back.finish())
 

time: 85.6 us -> 85.6 us (level)
  no operation moved by 1% of the time
where the time goes in v9:
time: 85.6 us; the launch traced here: 85.5 us
  Pallas kernels  84.2 us (98%)
  between operations  1.31 us (2%)
    pallas_call x1, Pallas kernels, on_device(): pl.pallas_call(kernel, out_shape=(jax.ShapeDtypeStruct((3, 32, 16, 128),...  82.9 us

profile of v9, /device:TPU:1, one launch (start us, length us, event | category | flops | bytes accessed | tf_op | source)
XLA Modules:
  0.0 85.5 jit_solution(17579264588232707586)
XLA Ops:
  0.6 0.0 copy-start
  1.3 0.0 copy-done
  1.3 82.9 %shard_map.157 = (f32[3,32,16,128]{3,2,1,0:T(8,128)S(1)}, f32[3,32,16,128]{3,2,1,0:T(8,128)S(1)}, f32[32,16,128]{2,1,0:T(8,128)S(1)}) custom-call(f32[3,32,16,128]{3,2,1,0:T(8,128)} %velocity.1, f32[3,32,16,128]{3,2,1,0:T(8,128)} %adjoint_seed.1, f32[32,16,128]{2,1,0:T(8,128)} %suscept.1, f32[32,16,128]{2,1,0:T(8,128)} %remanence_in.1, ...), custom_call_target="tpu_custom_call" | custom-call | tf_op jit(solution)/shard_map/pallas_call | solution.py:707
  84.3 1.2 %shard_map.158 = (f32[3,32,16,128]{3,2,1,0:T(8,128)}, f32[3,32,16,128]{3,2,1,0:T(8,128)}, f32[32,16,128]{2,1,0:T(8,128)}) custom-call(f32[3,32,16,128]{3,2,1,0:T(8,128)S(1)} %get-tuple-element.6.a_in, f32[3,32,16,128]{3,2,1,0:T(8,128)S(1)} %get-tuple-element.7.b_in, f32[32,16,128]{2,1,0:T(8,128)S(1)} %get-tuple-element.8.c_in), custom_call_target="tpu_custom_call" | custom-call | tf_op jit(solution)/shard_map/pallas_call | solution.py:725
Async XLA Ops:
  0.6 0.7 copy-start
